TPU v7x, 256 devices: a whole 4x4x8 slice. The times are simulated.
256 devices in a mesh: graph: 64 (over x, z, core), mp: 4 (over y).
Axes of the slice: x: 4, y: 4, z: 8, core: 2. Of those that a mesh axis runs over, the one named last changes fastest.
Arguments:
- edge_state: bfloat16 [32768, 1536], P('graph', 'mp'), may hold values from -6 to 6
- down_weight: bfloat16 [1536, 384], P('mp'), may hold values from -0.15625 to 0.15625
- basis: float32 [42, 1048576], P(None, ('graph', 'mp')), may hold values from -6 to 6
- basis_weight: float32 [42, 384], replicated, may hold values from -1 to 1
- up_weight: bfloat16 [384, 1536], P(None, 'mp'), may hold values from -0.3125 to 0.3125
- dense_weight: bfloat16 [3, 2, 1536, 1536], P(None, None, None, 'mp'), may hold values from -0.15625 to 0.15625
- send_rows: int32 [64, 256, 64], P('graph', 'mp'), may hold values from 0 to 512, as said below
- trip_in: int32 [1048576], P(('graph', 'mp')), may hold values from 0 to 4095, as said below
- trip_out: int32 [1048576], P(('graph', 'mp')), may hold values from 0 to 4095, as said below
- trip_live: int32 [1048576], P(('graph', 'mp')), may hold values from 0 to 1, as said below
- edge_atom: int32 [32768], P('graph'), may hold values from 0 to 2047
Outputs:
- edge_out: bfloat16 [32768, 1536], P('graph', 'mp')
- atom_out: bfloat16 [2048, 1536], P('graph', 'mp')
Inputs may be any that keep to these rules, and one draw needn't show every extreme that they name: `send_rows`: entry [s, m * 64 + g, c] is a row among the 512 edges of graph index s listed in slot c for the device at graph index g and mp index m, or 512 for an empty slot; used slots come first in each list, and some device has every list full. `trip_in`: A slot s * 64 + c of the triplet's own device whose list entry from graph index s is used. `trip_out`: A slot s * 64 + c of the triplet's own device whose list entry from graph index s is used. `trip_live`: on each device the real triplets come first; some device has no padding.
All inputs are finite; a program needn't handle non-finite values.
Results may differ from a plain program's by a relative error of at most 0.014.
Values may be sent and summed in bfloat16 or wider, within the bound.
No kernel may reach another device: no remote copies, remote signals or barrier semaphores. Data moves between devices by JAX's collectives and lax.ppermute only.
A program may use at most 128 MiB of HBM per device.

v0:
```python
import jax
import jax.numpy as jnp
from jax import lax
from jax.sharding import Mesh
from jax.sharding import PartitionSpec as P

ATOM_DEV = 32
GRAPH = ("graph_0", "graph_1", "graph_2")
GRAPH_MP = ("graph_0", "graph_1", "graph_2", "mp")


inv_root_two = 0.7071067811865476
atom_scale = 0.2


def joined_along(blocks, dim):
    blocks = jnp.moveaxis(blocks, 0, dim)
    lengths = blocks.shape
    return blocks.reshape(*lengths[:dim], lengths[dim] * lengths[dim + 1], *lengths[dim + 2 :])


def sent_to_all(array, axis):
    count = lax.axis_size(axis)
    return lax.all_to_all(
        jnp.broadcast_to(array[None], (count, *array.shape)), axis, 0, 0, tiled=True
    )


def collect(array, axis, dim):
    return joined_along(sent_to_all(array, axis), dim)


def of_everyone(array, axis):
    everything = sent_to_all(array, axis)
    return jnp.sum(everything.astype(jnp.float32), axis=0)


def split_up(array, dim, count):
    lengths = array.shape
    blocks = array.reshape(*lengths[:dim], count, lengths[dim] // count, *lengths[dim + 1 :])
    return jnp.moveaxis(blocks, dim, 0)


def turned_blocks(blocks, axes, order):
    inside = blocks.shape[1:]
    filled = blocks.reshape(*(lax.axis_size(a) for a in axes), *inside)
    for k in order:
        filled = lax.all_to_all(filled, axes[k], k, k, tiled=True)
    return filled.reshape(-1, *inside)


def exchange_by_chip(array, groups, order, split_dim, concat_dim):
    count = lax.axis_size(groups[0]) * lax.axis_size(groups[1])
    blocks = split_up(array, split_dim, count)
    return joined_along(turned_blocks(blocks, groups, order), concat_dim)


def dense_map(inputs, weight):
    return jnp.dot(collect(inputs, "mp", 1), weight, preferred_element_type=jnp.float32)


def local(
    edge_state,
    down_weight,
    basis,
    basis_weight,
    up_weight,
    dense_weight,
    send_rows,
    trip_in,
    trip_out,
    trip_live,
    edge_atom,
):
    edge_rows = edge_state.shape[0]
    width = down_weight.shape[1]
    graph_size = lax.axis_size(GRAPH)
    partial_value = jnp.dot(edge_state, down_weight, preferred_element_type=jnp.float32)
    projected = (
        of_everyone(partial_value.astype(jnp.bfloat16), "mp")
        .astype(jnp.float32)
        .astype(jnp.bfloat16)
    )
    padded = jnp.concatenate([projected, jnp.zeros((1, width), jnp.bfloat16)], axis=0)
    row_lists = send_rows[0]
    outgoing = jnp.take(padded, row_lists, axis=0)
    received = lax.all_to_all(outgoing, GRAPH, split_axis=0, concat_axis=0, tiled=True)
    slot_total = received.shape[0] * received.shape[1]
    slot_rows = received.reshape(slot_total, width)
    angle_coef = lax.dot_general(
        basis,
        basis_weight,
        (((0,), (0,)), ((), ())),
        precision=lax.Precision.HIGHEST,
        preferred_element_type=jnp.float32,
    )
    trip_values = (
        jnp.take(slot_rows, trip_in, axis=0).astype(jnp.float32)
        * angle_coef
        * trip_live[:, None].astype(jnp.float32)
    )
    slot_sums = jax.ops.segment_sum(trip_values, trip_out, num_segments=slot_total).astype(
        jnp.bfloat16
    )
    returned = exchange_by_chip(
        slot_sums.reshape(received.shape), (("graph_0", "graph_1"), "graph_2"), (1, 0), 0, 0
    )
    edge_sums = jax.ops.segment_sum(
        returned.reshape(slot_total, width).astype(jnp.float32),
        row_lists.reshape(-1),
        num_segments=edge_rows + 1,
    )[:edge_rows]
    update_rows = (
        of_everyone(edge_sums.astype(jnp.bfloat16), "mp").astype(jnp.float32).astype(jnp.bfloat16)
    )
    hidden = edge_state.astype(jnp.float32) + jnp.dot(
        update_rows, up_weight, preferred_element_type=jnp.float32
    )
    for layer_index in range(dense_weight.shape[0]):
        inner = jax.nn.silu(
            dense_map(hidden.astype(jnp.bfloat16), dense_weight[layer_index, 0])
        ).astype(jnp.bfloat16)
        outer = jax.nn.silu(dense_map(inner, dense_weight[layer_index, 1]))
        hidden = (hidden + outer) * inv_root_two
    atom_total = ATOM_DEV * graph_size
    partial_atoms = jax.ops.segment_sum(hidden, edge_atom, num_segments=atom_total)
    summed_atoms = lax.psum(partial_atoms, GRAPH)
    atom_table = jax.nn.silu(atom_scale * summed_atoms).astype(jnp.bfloat16)
    atom_out = lax.dynamic_slice_in_dim(atom_table, lax.axis_index(GRAPH) * ATOM_DEV, ATOM_DEV, 0)
    edge_out = (hidden + jnp.take(atom_table, edge_atom, axis=0).astype(jnp.float32)).astype(
        jnp.bfloat16
    )
    return (edge_out, atom_out)


def solution(mesh):
    split = Mesh(
        mesh.devices.reshape(4, 8, 2, mesh.shape["mp"]), ("graph_0", "graph_1", "graph_2", "mp")
    )
    return jax.shard_map(
        local,
        mesh=split,
        in_specs=(
            P(GRAPH, "mp"),
            P("mp", None),
            P(None, GRAPH_MP),
            P(),
            P(None, "mp"),
            P(None, None, None, "mp"),
            P(GRAPH, "mp", None),
            P(GRAPH_MP),
            P(GRAPH_MP),
            P(GRAPH_MP),
            P(GRAPH),
        ),
        out_specs=(P(GRAPH, "mp"), P(GRAPH, "mp")),
        check_vma=False,
    )
```

profile of v0, /device:TPU:1, one launch (start us, length us, event | category | flops | bytes accessed | tf_op | source)
XLA Modules:
  0.0 687.4 jit_solution(2016446874768917343)
XLA Ops:
  7.2 0.0 copy-start
  7.2 0.0 copy-start.4
  7.2 1.5 convolution_convert_fusion
  8.7 1.3 broadcast_in_dim.104
  10.0 5.0 all-to-all-start
  15.1 0.1 reshape.91
  15.2 18.9 %all-to-all-done = bf16[4,512,384]{2,1,0:T(8,128)(2,1)S(1)} async-done(((bf16[4,512,384]{2,1,0:T(8,128)(2,1)}), bf16[4,512,384]{2,1,0:T(8,128)(2,1)S(1)}, u32[]{:S(2)}, u32[]{:S(2)}) %all-to-all-start) | async-done | bytes 1572896 | tf_op jit(solution)/shard_map/all_to_all | solution.py:24
  34.0 0.4 reduce_sum.24
  34.5 17.1 %gather_fusion = bf16[4096,384]{1,0:T(8,128)(2,1)} fusion(bf16[513,384]{1,0:T(8,128)(2,1)S(1)} %concatenate.3, s32[4096]{0:T(1024)S(1)} %broadcast_clamp_fusion), kind=kCustom, calls=%fused_computation | custom fusion | bytes 6307840 | tf_op jit(solution)/shard_map/jit(_take)/gather | solution.py:86
  51.6 3.5 broadcast_select_fusion
  55.1 14.5 %all-to-all-start.1 = ((bf16[64,64,384]{2,1,0:T(8,128)(2,1)}), bf16[64,64,384]{2,1,0:T(8,128)(2,1)}, u32[]{:S(2)}, u32[]{:S(2)}) async-start(bf16[64,64,384]{2,1,0:T(8,128)(2,1)} %broadcast_select_fusion), calls=%async_computation.1 | async-start | bytes 6291456 | tf_op jit(solution)/shard_map/all_to_all | solution.py:87
  69.6 0.0 copy-done.7
  69.7 7.1 %fusion.49 = f32[4096,384]{1,0:T(8,128)} fusion(f32[42,4096]{1,0:T(8,128)S(1)} %copy-done, f32[42,384]{1,0:T(8,128)S(1)} %copy-done.5), kind=kOutput, calls=%fused_computation.65 | convolution fusion | flops 792723456 | bytes 7044096 | tf_op jit(solution)/shard_map/dot_general | solution.py:90
  76.8 66.2 %all-to-all-done.1 = bf16[64,64,384]{2,1,0:T(8,128)(2,1)} async-done(((bf16[64,64,384]{2,1,0:T(8,128)(2,1)}), bf16[64,64,384]{2,1,0:T(8,128)(2,1)}, u32[]{:S(2)}, u32[]{:S(2)}) %all-to-all-start.1) | async-done | bytes 3145760 | tf_op jit(solution)/shard_map/all_to_all | solution.py:87
  143.0 59.0 %scatter_custom_fusion = f32[4096,384]{1,0:T(8,128)} fusion(s32[4096]{0:T(1024)} %param.19, f32[4096,384]{1,0:T(8,128)} %fusion.49, f32[4096]{0:T(1024)S(1)} %convert_element_type.57, f32[]{:T(128)} %constant.47.clone.1, pred[4096]{0:T(1024)(128)(4,1)S(1)} %compare_and_fusion.1, bf16[]{:T(256)} %constant.76.clone.1, bf16[4096,384]{1,0:T(8,128)(2,1)} %bitcast.3, ...), kind=kCustom, calls=%fused_computation.8 | custom fusion | flops 7864320 | bytes 15766528 | tf_op jit(solution)/shard_map/scatter-add | solution.py:102
  202.0 3.1 convert_element_type.58
  205.2 0.3 copy.34
  205.5 6.1 all_to_all.55
  211.6 2.1 copy.35
  213.7 5.5 all-to-all-start.3
  219.3 0.3 all-reduce.3.cloned.1.call-start
  219.5 0.1 reshape.123
  219.6 71.5 %all-to-all-done.3 = bf16[32,2,1,64,384]{4,3,1,2,0:T(8,128)(2,1)} async-done(((bf16[32,2,1,64,384]{4,3,1,2,0:T(8,128)(2,1)}), bf16[32,2,1,64,384]{4,3,1,2,0:T(8,128)(2,1)}, u32[]{:S(2)}, u32[]{:S(2)}) %all-to-all-start.3) | async-done | bytes 3145760 | tf_op jit(solution)/shard_map/all_to_all | solution.py:48
  291.1 26.8 %scatter_custom_fusion.1 = f32[513,384]{1,0:T(8,128)S(1)} fusion(s32[4096]{0:T(1024)S(1)} %reshape.123, bf16[4096,384]{1,0:T(8,128)(2,1)} %bitcast.24, f32[]{:T(128)} %constant.47.clone.1), kind=kCustom, calls=%fused_computation.6 | custom fusion | flops 3145728 | bytes 3933700 | tf_op jit(solution)/shard_map/scatter-add | solution.py:108
  318.0 0.0 copy-start.2
  318.0 0.0 copy-start.3
  318.0 0.1 broadcast_in_dim.108
  318.2 19.5 %all_to_all.56 = bf16[4,512,384]{2,1,0:T(8,128)(2,1)S(1)} all-to-all(bf16[4,512,384]{2,1,0:T(8,128)(2,1)S(1)} %broadcast_in_dim.108), channel_id=1, replica_groups=mesh['graph_0'=4,'graph_1'=8,'graph_2'=2,'mp'=4] {'mp'}, dimensions={0} | all-to-all | bytes 3145728 | tf_op jit(solution)/shard_map/all_to_all | solution.py:24
  337.7 0.4 reduce_sum.25
  338.1 0.0 copy-done.2
  338.1 0.0 copy-done.3
  338.2 0.4 fusion.46
  338.6 0.2 copy.36
  338.8 0.1 broadcast_in_dim.109
  338.9 18.5 %all_to_all.57 = bf16[4,512,384]{1,2,0:T(8,128)(2,1)S(1)} all-to-all(bf16[4,512,384]{1,2,0:T(8,128)(2,1)S(1)} %broadcast_in_dim.109), channel_id=1, replica_groups=mesh['graph_0'=4,'graph_1'=8,'graph_2'=2,'mp'=4] {'mp'}, dimensions={0} | all-to-all | bytes 3145728 | tf_op jit(solution)/shard_map/all_to_all | solution.py:24
  357.3 2.4 multiply_convert_fusion.3
  359.7 0.2 copy.37
  359.9 0.1 broadcast_in_dim.110
  360.0 17.3 %all_to_all.58 = bf16[4,512,384]{1,2,0:T(8,128)(2,1)S(1)} all-to-all(bf16[4,512,384]{1,2,0:T(8,128)(2,1)S(1)} %broadcast_in_dim.110), channel_id=1, replica_groups=mesh['graph_0'=4,'graph_1'=8,'graph_2'=2,'mp'=4] {'mp'}, dimensions={0} | all-to-all | bytes 3145728 | tf_op jit(solution)/shard_map/all_to_all | solution.py:24
  377.3 2.4 fusion.47
  379.7 0.2 copy.38
  379.9 0.1 broadcast_in_dim.111
  380.0 16.0 %all_to_all.59 = bf16[4,512,384]{1,2,0:T(8,128)(2,1)S(1)} all-to-all(bf16[4,512,384]{1,2,0:T(8,128)(2,1)S(1)} %broadcast_in_dim.111), channel_id=1, replica_groups=mesh['graph_0'=4,'graph_1'=8,'graph_2'=2,'mp'=4] {'mp'}, dimensions={0} | all-to-all | bytes 3145728 | tf_op jit(solution)/shard_map/all_to_all | solution.py:24
  396.0 2.4 multiply_convert_fusion.2
  398.4 0.2 copy.39
  398.6 0.1 broadcast_in_dim.112
  398.7 15.0 %all_to_all.60 = bf16[4,512,384]{1,2,0:T(8,128)(2,1)S(1)} all-to-all(bf16[4,512,384]{1,2,0:T(8,128)(2,1)S(1)} %broadcast_in_dim.112), channel_id=1, replica_groups=mesh['graph_0'=4,'graph_1'=8,'graph_2'=2,'mp'=4] {'mp'}, dimensions={0} | all-to-all | bytes 3145728 | tf_op jit(solution)/shard_map/all_to_all | solution.py:24
  413.7 2.4 fusion.48
  416.1 0.2 copy.40
  416.3 0.1 broadcast_in_dim.113
  416.4 15.0 %all_to_all.61 = bf16[4,512,384]{1,2,0:T(8,128)(2,1)S(1)} all-to-all(bf16[4,512,384]{1,2,0:T(8,128)(2,1)S(1)} %broadcast_in_dim.113), channel_id=1, replica_groups=mesh['graph_0'=4,'graph_1'=8,'graph_2'=2,'mp'=4] {'mp'}, dimensions={0} | all-to-all | bytes 3145728 | tf_op jit(solution)/shard_map/all_to_all | solution.py:24
  431.4 2.4 multiply_convert_fusion.1
  433.8 0.2 copy.41
  434.0 0.1 broadcast_in_dim.114
  434.1 15.4 %all_to_all.62 = bf16[4,512,384]{1,2,0:T(8,128)(2,1)S(1)} all-to-all(bf16[4,512,384]{1,2,0:T(8,128)(2,1)S(1)} %broadcast_in_dim.114), channel_id=1, replica_groups=mesh['graph_0'=4,'graph_1'=8,'graph_2'=2,'mp'=4] {'mp'}, dimensions={0} | all-to-all | bytes 3145728 | tf_op jit(solution)/shard_map/all_to_all | solution.py:24
  449.5 2.4 add_multiply_fusion
  451.9 5.4 scatter_custom_fusion.2
  457.3 0.0 all-reduce.3.cloned.1.call-update
  457.4 216.7 %all-reduce.3.cloned.1.call-done = f32[2048,384]{1,0:T(8,128)} async-done(((f32[2048,384]{1,0:T(8,128)}), f32[2048,384]{1,0:T(8,128)}) %all-reduce.3.cloned.1.call-update) | async-done | bytes 3145744 | tf_op jit(solution)/shard_map/psum | solution.py:127
  674.1 3.0 multiply_convert_fusion
  677.1 0.6 constant_dynamic-slice_fusion
  677.7 1.9 gather_fusion.1
  679.6 0.9 add_convert_fusion
  680.5 0.0 copy-done.1
  (21 shorter events, 0.2 us)
Async XLA Ops:
  7.2 62.5 %copy-start = (f32[42,4096]{1,0:T(8,128)S(1)}, f32[42,4096]{1,0:T(8,128)}, u32[]{:S(2)}) copy-start(f32[42,4096]{1,0:T(8,128)} %param.13) | copy-start | bytes 2064388
  7.2 7.9 %copy-start.4 = (s32[1,64,64]{2,1,0:T(8,128)S(1)}, s32[1,64,64]{2,1,0:T(8,128)}, u32[]{:S(2)}) copy-start(s32[1,64,64]{2,1,0:T(8,128)} %param.17) | copy-start | bytes 49156
  10.0 24.0 %all-to-all-start = ((bf16[4,512,384]{2,1,0:T(8,128)(2,1)}), bf16[4,512,384]{2,1,0:T(8,128)(2,1)S(1)}, u32[]{:S(2)}, u32[]{:S(2)}) async-start(bf16[4,512,384]{2,1,0:T(8,128)(2,1)} %broadcast_in_dim.104), calls=%async_computation | async-start | bytes 3145728 | tf_op jit(solution)/shard_map/all_to_all | solution.py:24
  55.1 14.5 %copy-start.7 = (s32[4096]{0:T(1024)S(1)}, s32[4096]{0:T(1024)}, u32[]{:S(2)}) copy-start(s32[4096]{0:T(1024)} %param.20) | copy-start | bytes 49156
  55.1 14.5 %copy-start.6 = (s32[4096]{0:T(1024)S(1)}, s32[4096]{0:T(1024)}, u32[]{:S(2)}) copy-start(s32[4096]{0:T(1024)} %param.18) | copy-start | bytes 49156
  55.1 14.6 %copy-start.5 = (f32[42,384]{1,0:T(8,128)S(1)}, f32[42,384]{1,0:T(8,128)}, u32[]{:S(2)}) copy-start(f32[42,384]{1,0:T(8,128)} %param.14) | copy-start | bytes 193540
  55.1 87.9 %all-to-all-start.1 = ((bf16[64,64,384]{2,1,0:T(8,128)(2,1)}), bf16[64,64,384]{2,1,0:T(8,128)(2,1)}, u32[]{:S(2)}, u32[]{:S(2)}) async-start(bf16[64,64,384]{2,1,0:T(8,128)(2,1)} %broadcast_select_fusion), calls=%async_computation.1 | async-start | bytes 6291456 | tf_op jit(solution)/shard_map/all_to_all | solution.py:87
  213.7 77.4 %all-to-all-start.3 = ((bf16[32,2,1,64,384]{4,3,1,2,0:T(8,128)(2,1)}), bf16[32,2,1,64,384]{4,3,1,2,0:T(8,128)(2,1)}, u32[]{:S(2)}, u32[]{:S(2)}) async-start(bf16[32,2,1,64,384]{4,3,1,2,0:T(8,128)(2,1)} %copy.35), calls=%async_computation.3 | async-start | bytes 6291456 | tf_op jit(solution)/shard_map/all_to_all | solution.py:48
  219.3 454.8 %all-reduce.3.cloned.1.call-start = ((), (), s32[]{:S(2)}) async-start(), calls=%async_computation.11 | async-start | bytes 6291456 | tf_op jit(solution)/shard_map/psum | solution.py:127
  318.0 20.1 %copy-start.2 = (bf16[512,384]{1,0:T(8,128)(2,1)S(1)}, bf16[512,384]{1,0:T(8,128)(2,1)}, u32[]{:S(2)}) copy-start(bf16[512,384]{1,0:T(8,128)(2,1)} %param.11) | copy-start | bytes 1179652
  318.0 20.1 %copy-start.3 = (bf16[384,384]{1,0:T(8,128)(2,1)S(1)}, bf16[384,384]{1,0:T(8,128)(2,1)}, u32[]{:S(2)}) copy-start(bf16[384,384]{1,0:T(8,128)(2,1)} %param.15) | copy-start | bytes 884740
  449.5 2.4 copy-start.8
  674.1 6.4 copy-start.1
Sparse Core Ops, SparseCore 0:
  457.5 216.5 all-reduce.2
where the time goes:
time: 689 us; the launch traced here: 687 us
  waiting for transfers between devices  373 us (54%)
  blocking collectives  123 us (18%)
  other arithmetic  103 us (15%)
  local copies, waits for them, and re-layouts  25.7 us (4%)
  starting transfers between devices  25.3 us (4%)
  matrix products  23.2 us (3%)
  between operations  14.4 us (2%)
    psum x1, waiting for transfers between devices, local(): summed_atoms = lax.psum(partial_atoms, GRAPH)  217 us
    all_to_all x7, blocking collectives, sent_to_all(): lax.all_to_all(jnp.broadcast_to(array[None], (count, *array.shape)), axis...  117 us
    all_to_all x1, waiting for transfers between devices, turned_blocks(): filled = lax.all_to_all(filled, axes[k], k, k, tiled=True)  71.5 us
    all_to_all x1, waiting for transfers between devices, local(): lax.all_to_all(outgoing, GRAPH, split_axis=0, concat_axis=0, tiled=True)  66.2 us
    scatter-add x1, other arithmetic, local(): jax.ops.segment_sum(trip_values, trip_out, num_segments=slot_total)  59 us
    scatter-add x1, other arithmetic, local(): jax.ops.segment_sum(returned.reshape(slot_total, width).astype(jnp.float3...  26.8 us
    all_to_all x1, waiting for transfers between devices, sent_to_all(): lax.all_to_all(jnp.broadcast_to(array[None], (count, *array.shape)), axis...  18.9 us
    gather x1, local copies, waits for them, and re-layouts, local(): outgoing = jnp.take(padded, row_lists, axis=0)  17.1 us
  transfers between devices with their start and end apart: 4, of which 4 were waited for; matrix products, arithmetic and copies ran while one was open for 1% of the time, Pallas kernels for 0%

commit v1 on v0

v1 whole, which is shorter than its diff:
```python
import functools

import jax
import jax.numpy as jnp
from jax import lax
from jax.experimental import pallas as pl
from jax.experimental.pallas import tpu as pltpu
from jax.sharding import Mesh
from jax.sharding import PartitionSpec as P

ATOM_DEV = 32
GRAPH = ("graph_0", "graph_1", "graph_2")
GRAPH_MP = ("graph_0", "graph_1", "graph_2", "mp")
N_X, N_Z, N_CORE, N_MP = 4, 8, 2, 4
N_GRAPH = N_X * N_Z * N_CORE
CAP = 64
EDGE_DEV = 512
ROWS = EDGE_DEV // N_MP
SLOTS = N_GRAPH * CAP
TRIPS = 4096
NSBF = 42
BASIS_PAD = 48
D = 1536
COLS = D // N_MP
TRIP = 384
MAPS = 6
HALF_MAPS = MAPS // N_CORE
UP_HALF = TRIP // N_CORE
ATOMS = ATOM_DEV * N_GRAPH
HALF_ATOMS = ATOMS // N_CORE
BLOCK = 512

F32 = jnp.float32
BF16 = jnp.bfloat16
I32 = jnp.int32

inv_root_two = 0.7071067811865476
atom_scale = 0.2


def silu(v):
    return v / (1.0 + jnp.exp(-v))


def product(a, b):
    return jnp.dot(a, b, preferred_element_type=F32)


def ones_where(mask):
    return jnp.where(mask, jnp.ones((), F32), jnp.zeros((), F32)).astype(BF16)


def picks(row, count, first):
    n = row.shape[1]
    column = jnp.broadcast_to(row, (128, n)).T
    lane = lax.broadcasted_iota(I32, (n, 128), 1)
    return jnp.concatenate(
        [ones_where(column == lane + (first + k)) for k in range(0, count, 128)], axis=1
    )


def members(row, count, first):
    place = lax.broadcasted_iota(I32, (count, 128), 0) + first
    return jnp.concatenate(
        [ones_where(place == row[:, k : k + 128]) for k in range(0, row.shape[1], 128)], axis=1
    )


def params(mib):
    return pltpu.CompilerParams(
        dimension_semantics=("arbitrary",), vmem_limit_bytes=mib * 1024 * 1024
    )


def whole(shape):
    return pl.BlockSpec(shape, lambda *_: (0,) * len(shape))


def shape_of(*shape, kind=BF16):
    return jax.ShapeDtypeStruct(shape, kind)


SCALAR = pl.BlockSpec(memory_space=pltpu.SMEM)


def project_kernel(mp_ref, state_ref, weight_ref, partial_ref, *turned_refs):
    partial_ref[...] = product(state_ref[...], weight_ref[...]).astype(BF16)
    for k, turned_ref in enumerate(turned_refs):
        place = lax.rem(mp_ref[0] + k, N_MP) * ROWS
        turned_ref[...] = state_ref[pl.ds(pl.multiple_of(place, ROWS), ROWS), :]


def project(mp, edge_state, down_weight):
    return pl.pallas_call(
        project_kernel,
        grid=(1,),
        in_specs=[SCALAR, whole((EDGE_DEV, COLS)), whole((COLS, TRIP))],
        out_specs=[whole((EDGE_DEV, TRIP))] + [whole((ROWS, COLS))] * N_MP,
        out_shape=[shape_of(EDGE_DEV, TRIP)] + [shape_of(ROWS, COLS)] * N_MP,
        compiler_params=params(24),
        name="project",
        cost_estimate=pl.CostEstimate(
            flops=2 * EDGE_DEV * COLS * TRIP, bytes_accessed=1500000, transcendentals=0
        ),
    )(mp, edge_state, down_weight)


def send_kernel(list_ref, a_ref, b_ref, c_ref, d_ref, out_ref, table):
    @pl.when(pl.program_id(0) == 0)
    def _():
        total = a_ref[...].astype(F32) + b_ref[...].astype(F32)
        total = total + (c_ref[...].astype(F32) + d_ref[...].astype(F32))
        table[...] = total.astype(BF16)

    out_ref[...] = product(picks(list_ref[...], EDGE_DEV, 0), table[...]).astype(BF16)


def send(lists, partials):
    return pl.pallas_call(
        send_kernel,
        grid=(SLOTS // BLOCK,),
        in_specs=[pl.BlockSpec((1, BLOCK), lambda i: (0, i))] + [whole((EDGE_DEV, TRIP))] * N_MP,
        out_specs=pl.BlockSpec((BLOCK, TRIP), lambda i: (i, 0)),
        out_shape=shape_of(SLOTS, TRIP),
        scratch_shapes=[pltpu.VMEM((EDGE_DEV, TRIP), BF16)],
        compiler_params=params(24),
        name="send",
        cost_estimate=pl.CostEstimate(
            flops=2 * SLOTS * EDGE_DEV * TRIP, bytes_accessed=4700000, transcendentals=0
        ),
    )(lists, *partials)


TRIP_STEPS = TRIPS // BLOCK
CHUNK = 1024


def triplet_kernel(
    in_ref, live_ref, to_ref, basis_ref, weight_ref, table_ref, out_ref, values, padded
):
    step = pl.program_id(0)

    @pl.when(step == 0)
    def _():
        padded[...] = jnp.zeros_like(padded)

    @pl.when(step < TRIP_STEPS)
    def _():
        padded[0:NSBF, :] = basis_ref[...] * live_ref[...].astype(F32)
        basis = padded[...]
        high = basis.astype(BF16)
        low = (basis - high.astype(F32)).astype(BF16)
        stacked = jnp.concatenate([high, low, high], axis=0)
        coef = lax.dot_general(
            stacked, weight_ref[...], (((0,), (0,)), ((), ())), preferred_element_type=F32
        )
        row = in_ref[...]
        gathered = product(picks(row, CHUNK, 0), table_ref[0:CHUNK, :])
        for k in range(CHUNK, SLOTS, CHUNK):
            gathered = gathered + product(picks(row, CHUNK, k), table_ref[k : k + CHUNK, :])
        place = pl.multiple_of(step * BLOCK, BLOCK)
        values[pl.ds(place, BLOCK), :] = (gathered * coef).astype(BF16)

    @pl.when(step >= TRIP_STEPS)
    def _():
        first = (step - TRIP_STEPS) * BLOCK
        total = product(members(to_ref[:, 0:CHUNK], BLOCK, first), values[0:CHUNK, :])
        for k in range(CHUNK, TRIPS, CHUNK):
            total = total + product(
                members(to_ref[:, k : k + CHUNK], BLOCK, first), values[k : k + CHUNK, :]
            )
        out_ref[...] = total.astype(BF16)


def triplets(trip_in, trip_live, trip_out, basis, weight, table):
    gather_step = lambda i: (0, jnp.minimum(i, TRIP_STEPS - 1))
    return pl.pallas_call(
        triplet_kernel,
        grid=(TRIP_STEPS + SLOTS // BLOCK,),
        in_specs=[
            pl.BlockSpec((1, BLOCK), gather_step),
            pl.BlockSpec((1, BLOCK), gather_step),
            whole((1, TRIPS)),
            pl.BlockSpec((NSBF, BLOCK), gather_step),
            whole((3 * BASIS_PAD, TRIP)),
            whole((SLOTS, TRIP)),
        ],
        out_specs=pl.BlockSpec((BLOCK, TRIP), lambda i: (jnp.maximum(i - TRIP_STEPS, 0), 0)),
        out_shape=shape_of(SLOTS, TRIP),
        scratch_shapes=[pltpu.VMEM((TRIPS, TRIP), BF16), pltpu.VMEM((BASIS_PAD, BLOCK), F32)],
        compiler_params=params(48),
        name="triplets",
        cost_estimate=pl.CostEstimate(
            flops=4 * TRIPS * SLOTS * TRIP, bytes_accessed=7000000, transcendentals=0
        ),
    )(trip_in, trip_live, trip_out, basis, weight, table)


EDGE_CHUNK = 1024


def edges_kernel(mp_ref, list_ref, table_ref, *refs):
    outs, total = refs[:N_MP], refs[N_MP]
    step = pl.program_id(0)
    part = product(members(list_ref[...], EDGE_DEV, 0), table_ref[...])

    @pl.when(step == 0)
    def _():
        total[...] = part

    @pl.when(step > 0)
    def _():
        total[...] += part

    @pl.when(step == SLOTS // EDGE_CHUNK - 1)
    def _():
        for k, out_ref in enumerate(outs):
            place = lax.rem(mp_ref[0] + k, N_MP) * ROWS
            out_ref[...] = total[pl.ds(pl.multiple_of(place, ROWS), ROWS), :].astype(BF16)


def edges(mp, lists, returned):
    return pl.pallas_call(
        edges_kernel,
        grid=(SLOTS // EDGE_CHUNK,),
        in_specs=[
            SCALAR,
            pl.BlockSpec((1, EDGE_CHUNK), lambda i: (0, i)),
            pl.BlockSpec((EDGE_CHUNK, TRIP), lambda i: (i, 0)),
        ],
        out_specs=[whole((ROWS, TRIP))] * N_MP,
        out_shape=[shape_of(ROWS, TRIP)] * N_MP,
        scratch_shapes=[pltpu.VMEM((EDGE_DEV, TRIP), F32)],
        compiler_params=params(24),
        name="edges",
        cost_estimate=pl.CostEstimate(
            flops=2 * SLOTS * EDGE_DEV * TRIP, bytes_accessed=3500000, transcendentals=0
        ),
    )(mp, lists, returned)


SIDE = 2
MAP_STEPS = N_MP // SIDE


def layers_kernel(mp_ref, u0, u1, u2, u3, s0, s1, s2, s3, up_ref, weight_ref, *refs):
    outs = refs[:N_MP]
    hidden, given, inner = refs[N_MP:]
    step = pl.program_id(0)
    me = mp_ref[0]
    which = lax.div(step, MAP_STEPS)
    side = lax.rem(step, MAP_STEPS) * SIDE

    def columns(block):
        return pl.ds(pl.multiple_of(block * COLS, 128), COLS)

    @pl.when(step == 0)
    def _():
        total = u0[...].astype(F32) + u1[...].astype(F32)
        total = total + (u2[...].astype(F32) + u3[...].astype(F32))
        update = total.astype(BF16)
        for k, state_ref in enumerate((s0, s1, s2, s3)):
            hidden[:, columns(lax.rem(me + N_MP - k, N_MP))] = state_ref[...].astype(F32)
        for block in range(N_MP):
            added = product(update[:, :UP_HALF], up_ref[block])
            added = added + product(update[:, UP_HALF:], up_ref[N_MP + block])
            at = slice(block * COLS, (block + 1) * COLS)
            fresh = hidden[:, at] + added
            hidden[:, at] = fresh
            given[:, at] = fresh.astype(BF16)

    @pl.when(lax.rem(which, 2) == 0)
    def _():
        x = given[...]
        for j in range(SIDE):
            inner[:, columns(side + j)] = silu(product(x, weight_ref[j])).astype(BF16)

    @pl.when(lax.rem(which, 2) == 1)
    def _():
        x = inner[...]
        for j in range(SIDE):
            at = columns(side + j)
            fresh = (hidden[:, at] + silu(product(x, weight_ref[j]))) * inv_root_two
            hidden[:, at] = fresh
            given[:, at] = fresh.astype(BF16)

    @pl.when(step == MAPS * MAP_STEPS - 1)
    def _():
        for k, out_ref in enumerate(outs):
            out_ref[...] = given[:, columns(lax.rem(me + k, N_MP))]


def layers(mp, updates, states, gathered):
    def weight_block(i):
        which = i // MAP_STEPS
        side = i % MAP_STEPS
        return ((which // HALF_MAPS) * MAP_STEPS + side, which % HALF_MAPS, 0)

    return pl.pallas_call(
        layers_kernel,
        grid=(MAPS * MAP_STEPS,),
        in_specs=[SCALAR]
        + [whole((ROWS, TRIP))] * N_MP
        + [whole((ROWS, COLS))] * N_MP
        + [
            pl.BlockSpec(
                (N_CORE * N_MP, UP_HALF, COLS), lambda i: (0, HALF_MAPS * D // UP_HALF, 0)
            ),
            pl.BlockSpec((SIDE, D, COLS), weight_block),
        ],
        out_specs=[whole((ROWS, COLS))] * N_MP,
        out_shape=[shape_of(ROWS, COLS)] * N_MP,
        scratch_shapes=[
            pltpu.VMEM((ROWS, D), F32),
            pltpu.VMEM((ROWS, D), BF16),
            pltpu.VMEM((ROWS, D), BF16),
        ],
        compiler_params=params(32),
        name="layers",
        cost_estimate=pl.CostEstimate(
            flops=2 * ROWS * D * D * MAPS,
            bytes_accessed=2 * D * D * MAPS,
            transcendentals=ROWS * D * MAPS,
        ),
    )(mp, *updates, *states, gathered, gathered)


def at_block(ref, me, k):
    place = lax.rem(me + N_MP - k, N_MP) * ROWS
    return ref[:, pl.ds(pl.multiple_of(place, ROWS), ROWS)]


def atoms_kernel(mp_ref, core_ref, atom_ref, h0, h1, h2, h3, keep_ref, give_ref):
    me, core = mp_ref[0], core_ref[0]
    row = jnp.concatenate([at_block(atom_ref, me, k) for k in range(N_MP)], axis=1)
    hidden = jnp.concatenate([h0[...], h1[...], h2[...], h3[...]], axis=0)
    group = row // ATOM_DEV
    spot = (group // N_CORE) * ATOM_DEV + row % ATOM_DEV
    for out_ref, owner in ((keep_ref, core), (give_ref, 1 - core)):
        mine = jnp.where(group % N_CORE == owner, spot, -1)
        for first in range(0, HALF_ATOMS, BLOCK):
            part = product(members(mine, BLOCK, first), hidden)
            out_ref[first : first + BLOCK, :] = part.astype(BF16)


def atoms(mp, core, edge_atom, hiddens):
    return pl.pallas_call(
        atoms_kernel,
        grid=(1,),
        in_specs=[SCALAR, SCALAR, whole((1, EDGE_DEV))] + [whole((ROWS, COLS))] * N_MP,
        out_specs=[whole((HALF_ATOMS, COLS))] * 2,
        out_shape=[shape_of(HALF_ATOMS, COLS)] * 2,
        compiler_params=params(24),
        name="atoms",
        cost_estimate=pl.CostEstimate(
            flops=2 * ATOMS * EDGE_DEV * COLS, bytes_accessed=2000000, transcendentals=0
        ),
    )(mp, core, edge_atom, *hiddens)


def final_kernel(mp_ref, core_ref, atom_ref, h0, h1, h2, h3, mine_ref, other_ref, out_ref):
    me, core = mp_ref[0], core_ref[0]
    for k, hidden_ref in enumerate((h0, h1, h2, h3)):
        row = at_block(atom_ref, me, k)
        group = row // ATOM_DEV
        spot = (group // N_CORE) * ATOM_DEV + row % ATOM_DEV
        near = jnp.where(group % N_CORE == core, spot, -1)
        far = jnp.where(group % N_CORE == core, -1, spot)
        taken = product(picks(near, HALF_ATOMS, 0), mine_ref[...])
        taken = taken + product(picks(far, HALF_ATOMS, 0), other_ref[...])
        place = lax.rem(me + N_MP - k, N_MP) * ROWS
        out_ref[pl.ds(pl.multiple_of(place, ROWS), ROWS), :] = (
            hidden_ref[...].astype(F32) + taken
        ).astype(BF16)


def final(mp, core, edge_atom, hiddens, mine, other):
    return pl.pallas_call(
        final_kernel,
        grid=(1,),
        in_specs=[SCALAR, SCALAR, whole((1, EDGE_DEV))]
        + [whole((ROWS, COLS))] * N_MP
        + [whole((HALF_ATOMS, COLS))] * 2,
        out_specs=whole((EDGE_DEV, COLS)),
        out_shape=shape_of(EDGE_DEV, COLS),
        compiler_params=params(24),
        name="final",
        cost_estimate=pl.CostEstimate(
            flops=2 * ATOMS * EDGE_DEV * COLS, bytes_accessed=2400000, transcendentals=0
        ),
    )(mp, core, edge_atom, *hiddens, mine, other)


def turn(array, axis, count, shift):
    return lax.ppermute(array, axis, [(i, (i + shift) % count) for i in range(count)])


def turned(blocks, axis):
    count = len(blocks)
    return [blocks[0]] + [turn(blocks[k], axis, count, k) for k in range(1, count)]


def summed(blocks):
    return jnp.sum(blocks.astype(F32), axis=0)


def local(
    edge_state,
    down_weight,
    basis,
    basis_weight,
    up_weight,
    dense_weight,
    send_rows,
    trip_in,
    trip_out,
    trip_live,
    edge_atom,
):
    mp = jnp.full((1,), lax.axis_index("mp"), I32)
    core_index = lax.axis_index("graph_2")
    core = jnp.full((1,), core_index, I32)
    lists = send_rows.reshape(1, SLOTS)
    atom_row = edge_atom.reshape(1, EDGE_DEV)
    high = basis_weight.astype(BF16)
    low = (basis_weight - high.astype(F32)).astype(BF16)
    pad = ((0, BASIS_PAD - NSBF), (0, 0))
    high, low = jnp.pad(high, pad), jnp.pad(low, pad)
    coef_weight = jnp.concatenate([high, high, low], axis=0)
    half = jnp.concatenate(
        [
            lax.dynamic_slice_in_dim(
                dense_weight.reshape(MAPS * D, COLS), core_index * (HALF_MAPS * D), HALF_MAPS * D, 0
            ),
            lax.dynamic_slice_in_dim(up_weight, core_index * UP_HALF, UP_HALF, 0),
        ],
        axis=0,
    )

    partial, *state_blocks = project(mp, edge_state, down_weight)
    partials = turned([partial] * N_MP, "mp")
    outgoing = send(lists, partials)
    outgoing, half, *state_blocks = lax.optimization_barrier((outgoing, half, *state_blocks))
    gathered = lax.all_gather(half, ("graph_2", "mp"), axis=0, tiled=False)
    received = lax.all_to_all(
        outgoing.reshape(N_GRAPH, CAP, TRIP), GRAPH, split_axis=0, concat_axis=0, tiled=True
    )
    states = turned(state_blocks, "mp")
    slot_sums = triplets(
        trip_in.reshape(1, TRIPS),
        trip_live.reshape(1, TRIPS),
        trip_out.reshape(1, TRIPS),
        basis,
        coef_weight,
        received.reshape(SLOTS, TRIP),
    )
    returned = lax.all_to_all(
        slot_sums.reshape(N_GRAPH, CAP, TRIP), GRAPH, split_axis=0, concat_axis=0, tiled=True
    )
    updates = turned(edges(mp, lists, returned.reshape(SLOTS, TRIP)), "mp")
    hiddens = turned(layers(mp, updates, states, gathered), "mp")
    keep, give = atoms(mp, core, atom_row, hiddens)
    part = keep.astype(F32) + turn(give, "graph_2", N_CORE, 1).astype(F32)
    part = part.astype(BF16).reshape(N_X, HALF_ATOMS // N_X, COLS)
    part = summed(lax.all_to_all(part, "graph_0", 0, 0, tiled=True))
    part = part.astype(BF16).reshape(N_Z, ATOM_DEV, COLS)
    atom_sum = summed(lax.all_to_all(part, "graph_1", 0, 0, tiled=True))
    atom_out = jax.nn.silu(atom_scale * atom_sum).astype(BF16)
    table = lax.all_to_all(
        jnp.broadcast_to(atom_out[None], (N_Z, ATOM_DEV, COLS)), "graph_1", 0, 0, tiled=True
    ).reshape(N_Z * ATOM_DEV, COLS)
    table = lax.all_to_all(
        jnp.broadcast_to(table[None], (N_X, N_Z * ATOM_DEV, COLS)), "graph_0", 0, 0, tiled=True
    ).reshape(HALF_ATOMS, COLS)
    other = turn(table, "graph_2", N_CORE, 1)
    edge_out = final(mp, core, atom_row, hiddens, table, other)
    return (edge_out, atom_out)


def solution(mesh):
    split = Mesh(
        mesh.devices.reshape(N_X, N_Z, N_CORE, mesh.shape["mp"]),
        ("graph_0", "graph_1", "graph_2", "mp"),
    )
    return jax.shard_map(
        local,
        mesh=split,
        in_specs=(
            P(GRAPH, "mp"),
            P("mp", None),
            P(None, GRAPH_MP),
            P(),
            P(None, "mp"),
            P(None, None, None, "mp"),
            P(GRAPH, "mp", None),
            P(GRAPH_MP),
            P(GRAPH_MP),
            P(GRAPH_MP),
            P(GRAPH),
        ),
        out_specs=(P(GRAPH, "mp"), P(GRAPH, "mp")),
        check_vma=False,
    )
```

time: 689 us -> 354 us (0.51)
  waiting for transfers between devices: 373 us -> 164 us
  other arithmetic: 103 us -> 2.57 us
  blocking collectives: 123 us -> 48.3 us
  Pallas kernels: 0 us -> 71.3 us
  matrix products: 23.2 us -> 0 us
  starting transfers between devices: 25.3 us -> 45.8 us
  local copies, waits for them, and re-layouts: 25.7 us -> 6.99 us
    psum x1 -> x0, waiting for transfers between devices: 217 us -> none  [local(): summed_atoms = lax.psum(partial_atoms, GRAPH)]
    scatter-add x3 -> x0, other arithmetic: 91.3 us -> none  [the longest x1 59 us: local(): jax.ops.segment_sum(trip_values, trip_out, num_segments=slot_total)]
    all_to_all x8 -> x4, blocking collectives: 123 us -> 48.3 us  [the longest x1 14.4 us: local(): part = summed(lax.all_to_all(part, 'graph_0', 0, 0, tiled=True))]
    pallas_call x0 -> x7, Pallas kernels: none -> 71.3 us  [the longest x1 41.3 us: triplets(): pl.pallas_call(triplet_kernel, grid=(TRIP_STEPS + SLOTS // BLOCK,), in_sp...]
    ppermute x0 -> x14, starting transfers between devices: none -> 26.3 us  [turn(): lax.ppermute(array, axis, [(i, (i + shift) % count) for i in range(count)])]
    dot_general x9 -> x0, matrix products: 23.2 us -> none  [the longest x6 14.2 us: dense_map(): jnp.dot(collect(inputs, 'mp', 1), weight, preferred_element_type=jnp.floa...]
    ppermute x0 -> x14, waiting for transfers between devices: none -> 21.7 us  [turn(): lax.ppermute(array, axis, [(i, (i + shift) % count) for i in range(count)])]
    gather x2 -> x0, local copies, waits for them, and re-layouts: 19 us -> none  [the longest x1 17.1 us: local(): outgoing = jnp.take(padded, row_lists, axis=0)]
  transfers between devices with their start and end apart: 4 -> 17, of which waited for: 4 -> 11; matrix products, arithmetic and copies ran while one was open for 1% -> 2% of each run, Pallas kernels for 0% -> 13%
where the time goes in v1:
time: 354 us
  waiting for transfers between devices  164 us (46%)
  Pallas kernels  71.3 us (20%)
  blocking collectives  48.3 us (14%)
  starting transfers between devices  45.8 us (13%)
  between operations  14.3 us (4%)
  local copies, waits for them, and re-layouts  6.99 us (2%)
    all_to_all x1, waiting for transfers between devices, local(): lax.all_to_all(outgoing.reshape(N_GRAPH, CAP, TRIP), GRAPH, split_axis=0,...  73.4 us
    all_to_all x1, waiting for transfers between devices, local(): lax.all_to_all(slot_sums.reshape(N_GRAPH, CAP, TRIP), GRAPH, split_axis=0...  69.2 us
    pallas_call x1, Pallas kernels, triplets(): pl.pallas_call(triplet_kernel, grid=(TRIP_STEPS + SLOTS // BLOCK,), in_sp...  41.3 us
    ppermute x14, starting transfers between devices, turn(): lax.ppermute(array, axis, [(i, (i + shift) % count) for i in range(count)])  26.3 us
    ppermute x14, waiting for transfers between devices, turn(): lax.ppermute(array, axis, [(i, (i + shift) % count) for i in range(count)])  21.7 us
    pallas_call x1, Pallas kernels, layers(): pl.pallas_call(layers_kernel, grid=(MAPS * MAP_STEPS,), in_specs=[SCALAR]...  16.6 us
    all_to_all x1, blocking collectives, local(): part = summed(lax.all_to_all(part, 'graph_0', 0, 0, tiled=True))  14.4 us
    all_to_all x1, starting transfers between devices, local(): lax.all_to_all(outgoing.reshape(N_GRAPH, CAP, TRIP), GRAPH, split_axis=0,...  13.3 us
  transfers between devices with their start and end apart: 17, of which 11 were waited for; matrix products, arithmetic and copies ran while one was open for 2% of the time, Pallas kernels for 13%

profile of v1, /device:TPU:1, one launch (start us, length us, event | category | flops | bytes accessed | tf_op | source)
XLA Modules:
  0.0 353.6 jit_solution(7479551403231844302)
XLA Ops:
  7.2 0.0 copy-start
  7.2 0.0 all-gather.3.cloned.1.call-start
  7.2 1.0 copy-done.3
  8.3 1.0 copy-done.4
  9.2 1.0 project.1
  10.3 2.1 collective-permute-start
  12.4 2.6 collective-permute-start.1
  15.0 1.1 collective-permute-start.2
  16.1 0.8 reshape.54.list_ref
  17.0 2.4 constant_dynamic-slice_fusion.1
  19.3 2.1 pad_maximum_fusion
  21.5 0.0 collective-permute-done.b_ref
  21.5 10.5 %collective-permute-done.1.c_ref = bf16[512,384]{1,0:T(8,128)(2,1)S(1)} collective-permute-done((bf16[512,384]{1,0:T(8,128)(2,1)S(1)}, bf16[512,384]{1,0:T(8,128)(2,1)S(1)}, u32[]{:S(2)}, u32[]{:S(2)}) %collective-permute-start.1) | collective-permute-done | bytes 393248 | tf_op jit(solution)/shard_map/ppermute | solution.py:395
  31.9 0.0 collective-permute-done.2.d_ref
  31.9 5.7 %send.1 = bf16[4096,384]{1,0:T(8,128)(2,1)} custom-call(s32[1,4096]{1,0:T(1,128)S(1)} %reshape.54.list_ref, bf16[512,384]{1,0:T(8,128)(2,1)S(1)} %get-tuple-element.23.a_ref, bf16[512,384]{1,0:T(8,128)(2,1)S(1)} %collective-permute-done.b_ref, bf16[512,384]{1,0:T(8,128)(2,1)S(1)} %collective-permute-done.1.c_ref, ...), custom_call_target="tpu_custom_call" | custom-call | flops 1610612736 | bytes 4700000 | tf_op jit(solution)/shard_map/send/pallas_call | solution.py:119
  37.7 0.0 all-gather.3.cloned.1.call-update
  37.7 0.0 copy-start.11
  37.7 0.0 copy-start.5
  37.7 0.0 copy-start.6
  37.7 0.0 copy-start.7
  37.7 0.0 copy-start.8
  37.7 13.3 %all-to-all-start = ((bf16[64,64,384]{2,1,0:T(8,128)(2,1)}), bf16[64,64,384]{2,1,0:T(8,128)(2,1)}, u32[]{:S(2)}, u32[]{:S(2)}) async-start(bf16[64,64,384]{2,1,0:T(8,128)(2,1)} %bitcast.7), calls=%async_computation | async-start | bytes 6291456 | tf_op jit(solution)/shard_map/all_to_all | solution.py:445
  51.2 73.4 %all-to-all-done = bf16[64,64,384]{2,1,0:T(8,128)(2,1)} async-done(((bf16[64,64,384]{2,1,0:T(8,128)(2,1)}), bf16[64,64,384]{2,1,0:T(8,128)(2,1)}, u32[]{:S(2)}, u32[]{:S(2)}) %all-to-all-start) | async-done | bytes 3145760 | tf_op jit(solution)/shard_map/all_to_all | solution.py:445
  124.5 0.0 copy-done.8
  124.5 41.3 %triplets.1 = bf16[4096,384]{1,0:T(8,128)(2,1)S(1)} custom-call(s32[1,4096]{1,0:T(1,128)S(1)} %bitcast.20, s32[1,4096]{1,0:T(1,128)S(1)} %bitcast.21, s32[1,4096]{1,0:T(1,128)S(1)} %bitcast.22, f32[42,4096]{1,0:T(8,128)S(1)} %copy-done.5, bf16[144,384]{1,0:T(8,128)(2,1)S(1)} %fusion.1.weight_ref, bf16[4096,384]{1,0:T(8,128)(2,1)} %bitcast.8.table_ref), custom_call_target="tpu_custom_call" | custom-call | flops 25769803776 | bytes 7000000 | tf_op jit(solution)/shard_map/triplets/pallas_call | solution.py:177
  165.8 1.6 copy-done.2
  167.4 6.2 %all-to-all-start.1 = ((bf16[64,64,384]{2,1,0:T(8,128)(2,1)}), bf16[64,64,384]{2,1,0:T(8,128)(2,1)S(1)}, u32[]{:S(2)}, u32[]{:S(2)}) async-start(bf16[64,64,384]{2,1,0:T(8,128)(2,1)} %bitcast.17), calls=%async_computation.1 | async-start | bytes 6291456 | tf_op jit(solution)/shard_map/all_to_all | solution.py:457
  173.6 0.8 collective-permute-start.6
  174.5 2.1 collective-permute-start.7
  176.6 1.4 collective-permute-start.8
  178.0 69.2 %all-to-all-done.1 = bf16[64,64,384]{2,1,0:T(8,128)(2,1)S(1)} async-done(((bf16[64,64,384]{2,1,0:T(8,128)(2,1)}), bf16[64,64,384]{2,1,0:T(8,128)(2,1)S(1)}, u32[]{:S(2)}, u32[]{:S(2)}) %all-to-all-start.1) | async-done | bytes 3145760 | tf_op jit(solution)/shard_map/all_to_all | solution.py:457
  247.1 3.2 edges.1
  250.3 1.0 collective-permute-start.3
  251.3 2.1 collective-permute-start.4
  253.5 0.0 collective-permute-done.6.s1
  253.5 1.4 collective-permute-start.5
  254.9 0.0 collective-permute-done.7.s2
  254.9 0.0 collective-permute-done.8.s3
  254.9 1.1 collective-permute-done.3.u1
  255.9 2.3 collective-permute-done.4.u2
  258.2 0.1 collective-permute-done.5.u3
  258.3 16.6 %layers.1 = (bf16[128,384]{1,0:T(8,128)(2,1)S(1)}, bf16[128,384]{1,0:T(8,128)(2,1)S(1)}, bf16[128,384]{1,0:T(8,128)(2,1)S(1)}, bf16[128,384]{1,0:T(8,128)(2,1)S(1)}) custom-call(s32[1]{0:T(128)} %bitcast.mp_ref, bf16[128,384]{1,0:T(8,128)(2,1)S(1)} %get-tuple-element.29.u0, bf16[128,384]{1,0:T(8,128)(2,1)S(1)} %collective-permute-done.3.u1, ...), custom_call_target="tpu_custom_call" | custom-call | flops 3623878656 | bytes 28311552 | tf_op jit(solution)/shard_map/layers/pallas_call | solution.py:299
  274.9 2.3 collective-permute-start.9
  277.2 1.7 collective-permute-start.10
  278.9 0.8 collective-permute-start.11
  279.7 0.1 collective-permute-done.9.h1
  279.8 3.2 collective-permute-done.10.h2
  282.9 0.8 collective-permute-done.11.h3
  283.7 0.0 copy-done.9
  283.7 1.3 atoms.1
  284.9 1.6 collective-permute-start.12
  286.6 1.9 collective-permute-done.12
  288.5 0.2 add_convert_fusion
  288.7 0.0 copy-start.1
  288.7 14.4 %all_to_all.30 = bf16[4,256,384]{2,1,0:T(8,128)(2,1)S(1)} all-to-all(bf16[4,256,384]{2,1,0:T(8,128)(2,1)S(1)} %bitcast.27), channel_id=1, replica_groups=mesh['graph_0'=4,'graph_1'=8,'graph_2'=2,'mp'=4] {'graph_0'}, dimensions={0} | all-to-all | bytes 1572864 | tf_op jit(solution)/shard_map/all_to_all | solution.py:465
  303.1 0.2 reduce_sum.21
  303.2 12.1 %all_to_all.31 = bf16[8,32,384]{2,1,0:T(8,128)(2,1)S(1)} all-to-all(bf16[8,32,384]{2,1,0:T(8,128)(2,1)S(1)} %bitcast.29), channel_id=1, replica_groups=mesh['graph_0'=4,'graph_1'=8,'graph_2'=2,'mp'=4] {'graph_1'}, dimensions={0} | all-to-all | bytes 393216 | tf_op jit(solution)/shard_map/all_to_all | solution.py:467
  315.5 0.0 copy-start.10
  315.5 11.0 %all_to_all.32 = bf16[8,32,384]{2,1,0:T(8,128)(2,1)S(1)} all-to-all(bf16[8,32,384]{2,1,0:T(8,128)(2,1)S(1)} %broadcast_in_dim.21), channel_id=1, replica_groups=mesh['graph_0'=4,'graph_1'=8,'graph_2'=2,'mp'=4] {'graph_1'}, dimensions={0} | all-to-all | bytes 393216 | tf_op jit(solution)/shard_map/all_to_all | solution.py:469
  326.5 0.1 broadcast_in_dim.23
  326.6 10.7 %all_to_all.33 = bf16[4,256,384]{2,1,0:T(8,128)(2,1)S(1)} all-to-all(bf16[4,256,384]{2,1,0:T(8,128)(2,1)S(1)} %broadcast_in_dim.23), channel_id=1, replica_groups=mesh['graph_0'=4,'graph_1'=8,'graph_2'=2,'mp'=4] {'graph_0'}, dimensions={0} | all-to-all | bytes 1572864 | tf_op jit(solution)/shard_map/all_to_all | solution.py:472
  337.3 5.2 %collective-permute-start.13 = (bf16[1024,384]{1,0:T(8,128)(2,1)S(1)}, bf16[1024,384]{1,0:T(8,128)(2,1)S(1)}, u32[]{:S(2)}, u32[]{:S(2)}) collective-permute-start(bf16[1024,384]{1,0:T(8,128)(2,1)S(1)} %bitcast.18), channel_id=1, source_target_pairs={{0,4},{4,0},{1,5},{5,1},{2,6},{6,2},{3,7},{7,3},{8,12},{12,8},{9,1... | collective-permute-start | bytes 2359304 | tf_op jit(solution)/shard_map/ppermute | solution.py:395
  342.5 1.9 collective-permute-done.13.other_ref
  344.4 2.3 final.1
  (19 shorter events, 0.2 us)
Async XLA Ops:
  7.2 9.8 %copy-start = (bf16[384,384]{1,0:T(8,128)(2,1)S(1)}, bf16[384,384]{1,0:T(8,128)(2,1)}, u32[]{:S(2)}) copy-start(bf16[384,384]{1,0:T(8,128)(2,1)} %param.15) | copy-start | bytes 884740
  7.2 251.1 %all-gather.3.cloned.1.call-start = ((), (), s32[]{:S(2)}) async-start(), calls=%async_computation.6 | async-start | bytes 33177600 | tf_op jit(solution)/shard_map/all_gather | solution.py:444
  7.2 1.0 copy-start.3
  8.3 1.0 copy-start.4
  10.3 11.2 %collective-permute-start = (bf16[512,384]{1,0:T(8,128)(2,1)S(1)}, bf16[512,384]{1,0:T(8,128)(2,1)S(1)}, u32[]{:S(2)}, u32[]{:S(2)}) collective-permute-start(bf16[512,384]{1,0:T(8,128)(2,1)S(1)} %get-tuple-element.23.a_ref), channel_id=1, source_target_pairs={{0,1},{1,2},{2,3},{3,0},{4,5},{5,6},{6,7},{7,4},{8,9},{9,10},{10,1... | collective-permute-start | bytes 1179656 | tf_op jit(solution)/shard_map/ppermute | solution.py:395
  12.4 19.6 %collective-permute-start.1 = (bf16[512,384]{1,0:T(8,128)(2,1)S(1)}, bf16[512,384]{1,0:T(8,128)(2,1)S(1)}, u32[]{:S(2)}, u32[]{:S(2)}) collective-permute-start(bf16[512,384]{1,0:T(8,128)(2,1)S(1)} %get-tuple-element.23.a_ref), channel_id=1, source_target_pairs={{0,2},{1,3},{2,0},{3,1},{4,6},{5,7},{6,4},{7,5},{8,10},{9,11},{10,... | collective-permute-start | bytes 1179656 | tf_op jit(solution)/shard_map/ppermute | solution.py:395
  15.0 16.9 %collective-permute-start.2 = (bf16[512,384]{1,0:T(8,128)(2,1)S(1)}, bf16[512,384]{1,0:T(8,128)(2,1)S(1)}, u32[]{:S(2)}, u32[]{:S(2)}) collective-permute-start(bf16[512,384]{1,0:T(8,128)(2,1)S(1)} %get-tuple-element.23.a_ref), channel_id=1, source_target_pairs={{0,3},{1,0},{2,1},{3,2},{4,7},{5,4},{6,5},{7,6},{8,11},{9,8},{10,9... | collective-permute-start | bytes 1179656 | tf_op jit(solution)/shard_map/ppermute | solution.py:395
  37.7 13.4 %copy-start.11 = (f32[42,384]{1,0:T(8,128)S(1)}, f32[42,384]{1,0:T(8,128)}, u32[]{:S(2)}) copy-start(f32[42,384]{1,0:T(8,128)} %param.14) | copy-start | bytes 193540
  37.7 86.8 %copy-start.5 = (f32[42,4096]{1,0:T(8,128)S(1)}, f32[42,4096]{1,0:T(8,128)}, u32[]{:S(2)}) copy-start(f32[42,4096]{1,0:T(8,128)} %basis_ref.1) | copy-start | bytes 2064388
  37.7 86.8 %copy-start.6 = (s32[4096]{0:T(1024)S(1)}, s32[4096]{0:T(1024)}, u32[]{:S(2)}) copy-start(s32[4096]{0:T(1024)} %param.18) | copy-start | bytes 49156
  37.7 86.8 %copy-start.7 = (s32[4096]{0:T(1024)S(1)}, s32[4096]{0:T(1024)}, u32[]{:S(2)}) copy-start(s32[4096]{0:T(1024)} %param.20) | copy-start | bytes 49156
  37.7 86.8 %copy-start.8 = (s32[4096]{0:T(1024)S(1)}, s32[4096]{0:T(1024)}, u32[]{:S(2)}) copy-start(s32[4096]{0:T(1024)} %param.19) | copy-start | bytes 49156
  37.7 86.8 %all-to-all-start = ((bf16[64,64,384]{2,1,0:T(8,128)(2,1)}), bf16[64,64,384]{2,1,0:T(8,128)(2,1)}, u32[]{:S(2)}, u32[]{:S(2)}) async-start(bf16[64,64,384]{2,1,0:T(8,128)(2,1)} %bitcast.7), calls=%async_computation | async-start | bytes 6291456 | tf_op jit(solution)/shard_map/all_to_all | solution.py:445
  165.8 1.6 copy-start.2
  167.4 79.7 %all-to-all-start.1 = ((bf16[64,64,384]{2,1,0:T(8,128)(2,1)}), bf16[64,64,384]{2,1,0:T(8,128)(2,1)S(1)}, u32[]{:S(2)}, u32[]{:S(2)}) async-start(bf16[64,64,384]{2,1,0:T(8,128)(2,1)} %bitcast.17), calls=%async_computation.1 | async-start | bytes 6291456 | tf_op jit(solution)/shard_map/all_to_all | solution.py:457
  173.6 79.9 %collective-permute-start.6 = (bf16[128,384]{1,0:T(8,128)(2,1)}, bf16[128,384]{1,0:T(8,128)(2,1)}, u32[]{:S(2)}, u32[]{:S(2)}) collective-permute-start(bf16[128,384]{1,0:T(8,128)(2,1)} %get-tuple-element.34), channel_id=1, source_target_pairs={{0,1},{1,2},{2,3},{3,0},{4,5},{5,6},{6,7},{7,4},{8,9},{9,10},{10,1... | collective-permute-start | bytes 294920 | tf_op jit(solution)/shard_map/ppermute | solution.py:395
  174.5 80.4 %collective-permute-start.7 = (bf16[128,384]{1,0:T(8,128)(2,1)}, bf16[128,384]{1,0:T(8,128)(2,1)}, u32[]{:S(2)}, u32[]{:S(2)}) collective-permute-start(bf16[128,384]{1,0:T(8,128)(2,1)} %get-tuple-element.35), channel_id=1, source_target_pairs={{0,2},{1,3},{2,0},{3,1},{4,6},{5,7},{6,4},{7,5},{8,10},{9,11},{10,... | collective-permute-start | bytes 294920 | tf_op jit(solution)/shard_map/ppermute | solution.py:395
  176.6 78.3 %collective-permute-start.8 = (bf16[128,384]{1,0:T(8,128)(2,1)}, bf16[128,384]{1,0:T(8,128)(2,1)}, u32[]{:S(2)}, u32[]{:S(2)}) collective-permute-start(bf16[128,384]{1,0:T(8,128)(2,1)} %get-tuple-element.36), channel_id=1, source_target_pairs={{0,3},{1,0},{2,1},{3,2},{4,7},{5,4},{6,5},{7,6},{8,11},{9,8},{10,9... | collective-permute-start | bytes 294920 | tf_op jit(solution)/shard_map/ppermute | solution.py:395
  250.3 5.6 %collective-permute-start.3 = (bf16[128,384]{1,0:T(8,128)(2,1)S(1)}, bf16[128,384]{1,0:T(8,128)(2,1)S(1)}, u32[]{:S(2)}, u32[]{:S(2)}) collective-permute-start(bf16[128,384]{1,0:T(8,128)(2,1)S(1)} %get-tuple-element.30), channel_id=1, source_target_pairs={{0,1},{1,2},{2,3},{3,0},{4,5},{5,6},{6,7},{7,4},{8,9},{9,10},{10,1... | collective-permute-start | bytes 294920 | tf_op jit(solution)/shard_map/ppermute | solution.py:395
  251.3 6.9 %collective-permute-start.4 = (bf16[128,384]{1,0:T(8,128)(2,1)S(1)}, bf16[128,384]{1,0:T(8,128)(2,1)S(1)}, u32[]{:S(2)}, u32[]{:S(2)}) collective-permute-start(bf16[128,384]{1,0:T(8,128)(2,1)S(1)} %get-tuple-element.31), channel_id=1, source_target_pairs={{0,2},{1,3},{2,0},{3,1},{4,6},{5,7},{6,4},{7,5},{8,10},{9,11},{10,... | collective-permute-start | bytes 294920 | tf_op jit(solution)/shard_map/ppermute | solution.py:395
  253.5 4.8 %collective-permute-start.5 = (bf16[128,384]{1,0:T(8,128)(2,1)S(1)}, bf16[128,384]{1,0:T(8,128)(2,1)S(1)}, u32[]{:S(2)}, u32[]{:S(2)}) collective-permute-start(bf16[128,384]{1,0:T(8,128)(2,1)S(1)} %get-tuple-element.32), channel_id=1, source_target_pairs={{0,3},{1,0},{2,1},{3,2},{4,7},{5,4},{6,5},{7,6},{8,11},{9,8},{10,9... | collective-permute-start | bytes 294920 | tf_op jit(solution)/shard_map/ppermute | solution.py:395
  258.3 25.4 %copy-start.9 = (s32[512]{0:T(512)S(1)}, s32[512]{0:T(512)}, u32[]{:S(2)}) copy-start(s32[512]{0:T(512)} %param.21) | copy-start | bytes 6148
  274.9 4.9 %collective-permute-start.9 = (bf16[128,384]{1,0:T(8,128)(2,1)S(1)}, bf16[128,384]{1,0:T(8,128)(2,1)S(1)}, u32[]{:S(2)}, u32[]{:S(2)}) collective-permute-start(bf16[128,384]{1,0:T(8,128)(2,1)S(1)} %get-tuple-element.39), channel_id=1, source_target_pairs={{0,1},{1,2},{2,3},{3,0},{4,5},{5,6},{6,7},{7,4},{8,9},{9,10},{10,1... | collective-permute-start | bytes 294920 | tf_op jit(solution)/shard_map/ppermute | solution.py:395
  277.2 5.7 %collective-permute-start.10 = (bf16[128,384]{1,0:T(8,128)(2,1)S(1)}, bf16[128,384]{1,0:T(8,128)(2,1)S(1)}, u32[]{:S(2)}, u32[]{:S(2)}) collective-permute-start(bf16[128,384]{1,0:T(8,128)(2,1)S(1)} %get-tuple-element.40), channel_id=1, source_target_pairs={{0,2},{1,3},{2,0},{3,1},{4,6},{5,7},{6,4},{7,5},{8,10},{9,11},{10,... | collective-permute-start | bytes 294920 | tf_op jit(solution)/shard_map/ppermute | solution.py:395
  278.9 4.7 %collective-permute-start.11 = (bf16[128,384]{1,0:T(8,128)(2,1)S(1)}, bf16[128,384]{1,0:T(8,128)(2,1)S(1)}, u32[]{:S(2)}, u32[]{:S(2)}) collective-permute-start(bf16[128,384]{1,0:T(8,128)(2,1)S(1)} %get-tuple-element.41), channel_id=1, source_target_pairs={{0,3},{1,0},{2,1},{3,2},{4,7},{5,4},{6,5},{7,6},{8,11},{9,8},{10,9... | collective-permute-start | bytes 294920 | tf_op jit(solution)/shard_map/ppermute | solution.py:395
  284.9 3.5 collective-permute-start.12
  288.7 58.0 %copy-start.1 = (bf16[384,384]{1,0:T(8,128)(2,1)S(1)}, bf16[384,384]{1,0:T(8,128)(2,1)}, u32[]{:S(2)}) copy-start(bf16[384,384]{1,0:T(8,128)(2,1)} %param.15) | copy-start | bytes 884740
  315.5 31.2 %copy-start.10 = (bf16[32,384]{1,0:T(8,128)(2,1)}, bf16[32,384]{1,0:T(8,128)(2,1)S(1)}, u32[]{:S(2)}) copy-start(bf16[32,384]{1,0:T(8,128)(2,1)S(1)} %multiply_convert_fusion) | copy-start | bytes 73732
  337.3 7.1 %collective-permute-start.13 = (bf16[1024,384]{1,0:T(8,128)(2,1)S(1)}, bf16[1024,384]{1,0:T(8,128)(2,1)S(1)}, u32[]{:S(2)}, u32[]{:S(2)}) collective-permute-start(bf16[1024,384]{1,0:T(8,128)(2,1)S(1)} %bitcast.18), channel_id=1, source_target_pairs={{0,4},{4,0},{1,5},{5,1},{2,6},{6,2},{3,7},{7,3},{8,12},{12,8},{9,1... | collective-permute-start | bytes 2359304 | tf_op jit(solution)/shard_map/ppermute | solution.py:395
Sparse Core Ops, SparseCore 0:
  37.8 146.7 all-gather.2

commit v2 on v1

--- a/solution.py
+++ b/solution.py
@@ -50,13 +50,19 @@
     return jnp.where(mask, jnp.ones((), F32), jnp.zeros((), F32)).astype(BF16)
 
 
-def picks(row, count, first):
-    n = row.shape[1]
-    column = jnp.broadcast_to(row, (128, n)).T
-    lane = lax.broadcasted_iota(I32, (n, 128), 1)
+def column_of(row):
+    return jnp.broadcast_to(row, (128, row.shape[1])).T
+
+
+def picks_of(column, count):
+    lane = lax.broadcasted_iota(I32, column.shape, 1)
     return jnp.concatenate(
-        [ones_where(column == lane + (first + k)) for k in range(0, count, 128)], axis=1
-    )
+        [ones_where(column == lane + k) for k in range(0, count, 128)], axis=1
+    )
+
+
+def picks(row, count):
+    return picks_of(column_of(row), count)
 
 
 def members(row, count, first):
@@ -112,7 +118,7 @@
         total = total + (c_ref[...].astype(F32) + d_ref[...].astype(F32))
         table[...] = total.astype(BF16)
 
-    out_ref[...] = product(picks(list_ref[...], EDGE_DEV, 0), table[...]).astype(BF16)
+    out_ref[...] = product(picks(list_ref[...], EDGE_DEV), table[...]).astype(BF16)
 
 
 def send(lists, partials):
@@ -132,17 +138,22 @@
 
 
 TRIP_STEPS = TRIPS // BLOCK
-CHUNK = 1024
+HALF_SLOTS = SLOTS // 2
+SLOT_BLOCK = 256
+SLOT_STEPS = HALF_SLOTS // SLOT_BLOCK
+FEATURE_BLOCKS = range(0, TRIP, 128)
 
 
 def triplet_kernel(
-    in_ref, live_ref, to_ref, basis_ref, weight_ref, table_ref, out_ref, values, padded
+    in_ref, live_ref, to_ref, basis_ref, weight_ref, table_ref, out_ref, table, values, padded
 ):
     step = pl.program_id(0)
 
     @pl.when(step == 0)
     def _():
         padded[...] = jnp.zeros_like(padded)
+        table[:, :TRIP] = table_ref[:HALF_SLOTS, :]
+        table[:, TRIP:] = table_ref[HALF_SLOTS:, :]
 
     @pl.when(step < TRIP_STEPS)
     def _():
@@ -154,29 +165,32 @@
         coef = lax.dot_general(
             stacked, weight_ref[...], (((0,), (0,)), ((), ())), preferred_element_type=F32
         )
-        row = in_ref[...]
-        gathered = product(picks(row, CHUNK, 0), table_ref[0:CHUNK, :])
-        for k in range(CHUNK, SLOTS, CHUNK):
-            gathered = gathered + product(picks(row, CHUNK, k), table_ref[k : k + CHUNK, :])
         place = pl.multiple_of(step * BLOCK, BLOCK)
-        values[pl.ds(place, BLOCK), :] = (gathered * coef).astype(BF16)
+        source = column_of(in_ref[...])
+        target = column_of(to_ref[:, pl.ds(place, BLOCK)])
+        near = source < HALF_SLOTS
+        first = target < HALF_SLOTS
+        both = product(picks_of(source & (HALF_SLOTS - 1), HALF_SLOTS), table[...])
+        for k in FEATURE_BLOCKS:
+            at, far = slice(k, k + 128), slice(TRIP + k, TRIP + k + 128)
+            value = jnp.where(near, both[:, at], both[:, far]) * coef[:, at]
+            values[pl.ds(place, BLOCK), at] = jnp.where(first, value, 0.0).astype(BF16)
+            values[pl.ds(place, BLOCK), far] = jnp.where(first, 0.0, value).astype(BF16)
 
     @pl.when(step >= TRIP_STEPS)
     def _():
-        first = (step - TRIP_STEPS) * BLOCK
-        total = product(members(to_ref[:, 0:CHUNK], BLOCK, first), values[0:CHUNK, :])
-        for k in range(CHUNK, TRIPS, CHUNK):
-            total = total + product(
-                members(to_ref[:, k : k + CHUNK], BLOCK, first), values[k : k + CHUNK, :]
-            )
-        out_ref[...] = total.astype(BF16)
+        row = to_ref[...] & (HALF_SLOTS - 1)
+        chosen = members(row, SLOT_BLOCK, (step - TRIP_STEPS) * SLOT_BLOCK)
+        total = product(chosen, values[...]).astype(BF16)
+        out_ref[0] = total[:, :TRIP]
+        out_ref[1] = total[:, TRIP:]
 
 
 def triplets(trip_in, trip_live, trip_out, basis, weight, table):
     gather_step = lambda i: (0, jnp.minimum(i, TRIP_STEPS - 1))
     return pl.pallas_call(
         triplet_kernel,
-        grid=(TRIP_STEPS + SLOTS // BLOCK,),
+        grid=(TRIP_STEPS + SLOT_STEPS,),
         in_specs=[
             pl.BlockSpec((1, BLOCK), gather_step),
             pl.BlockSpec((1, BLOCK), gather_step),
@@ -185,10 +199,16 @@
             whole((3 * BASIS_PAD, TRIP)),
             whole((SLOTS, TRIP)),
         ],
-        out_specs=pl.BlockSpec((BLOCK, TRIP), lambda i: (jnp.maximum(i - TRIP_STEPS, 0), 0)),
-        out_shape=shape_of(SLOTS, TRIP),
-        scratch_shapes=[pltpu.VMEM((TRIPS, TRIP), BF16), pltpu.VMEM((BASIS_PAD, BLOCK), F32)],
-        compiler_params=params(48),
+        out_specs=pl.BlockSpec(
+            (2, SLOT_BLOCK, TRIP), lambda i: (0, jnp.maximum(i - TRIP_STEPS, 0), 0)
+        ),
+        out_shape=shape_of(2, HALF_SLOTS, TRIP),
+        scratch_shapes=[
+            pltpu.VMEM((HALF_SLOTS, 2 * TRIP), BF16),
+            pltpu.VMEM((TRIPS, 2 * TRIP), BF16),
+            pltpu.VMEM((BASIS_PAD, BLOCK), F32),
+        ],
+        compiler_params=params(60),
         name="triplets",
         cost_estimate=pl.CostEstimate(
             flops=4 * TRIPS * SLOTS * TRIP, bytes_accessed=7000000, transcendentals=0
@@ -239,7 +259,7 @@
     )(mp, lists, returned)
 
 
-SIDE = 2
+SIDE = 4
 MAP_STEPS = N_MP // SIDE
 
 
@@ -315,7 +335,7 @@
             pltpu.VMEM((ROWS, D), BF16),
             pltpu.VMEM((ROWS, D), BF16),
         ],
-        compiler_params=params(32),
+        compiler_params=params(40),
         name="layers",
         cost_estimate=pl.CostEstimate(
             flops=2 * ROWS * D * D * MAPS,
@@ -358,6 +378,28 @@
     )(mp, core, edge_atom, *hiddens)
 
 
+def meet_kernel(x_ref, keep_ref, got_ref, *outs):
+    for k, out_ref in enumerate(outs):
+        place = lax.rem(x_ref[0] + k, N_X) * (HALF_ATOMS // N_X)
+        rows = pl.ds(pl.multiple_of(place, HALF_ATOMS // N_X), HALF_ATOMS // N_X)
+        out_ref[...] = (keep_ref[rows, :].astype(F32) + got_ref[rows, :].astype(F32)).astype(BF16)
+
+
+def meet(x, keep, got):
+    return pl.pallas_call(
+        meet_kernel,
+        grid=(1,),
+        in_specs=[SCALAR] + [whole((HALF_ATOMS, COLS))] * 2,
+        out_specs=[whole((HALF_ATOMS // N_X, COLS))] * N_X,
+        out_shape=[shape_of(HALF_ATOMS // N_X, COLS)] * N_X,
+        compiler_params=params(24),
+        name="meet",
+        cost_estimate=pl.CostEstimate(
+            flops=HALF_ATOMS * COLS, bytes_accessed=2400000, transcendentals=0
+        ),
+    )(x, keep, got)
+
+
 def final_kernel(mp_ref, core_ref, atom_ref, h0, h1, h2, h3, mine_ref, other_ref, out_ref):
     me, core = mp_ref[0], core_ref[0]
     for k, hidden_ref in enumerate((h0, h1, h2, h3)):
@@ -366,8 +408,8 @@
         spot = (group // N_CORE) * ATOM_DEV + row % ATOM_DEV
         near = jnp.where(group % N_CORE == core, spot, -1)
         far = jnp.where(group % N_CORE == core, -1, spot)
-        taken = product(picks(near, HALF_ATOMS, 0), mine_ref[...])
-        taken = taken + product(picks(far, HALF_ATOMS, 0), other_ref[...])
+        taken = product(picks(near, HALF_ATOMS), mine_ref[...])
+        taken = taken + product(picks(far, HALF_ATOMS), other_ref[...])
         place = lax.rem(me + N_MP - k, N_MP) * ROWS
         out_ref[pl.ds(pl.multiple_of(place, ROWS), ROWS), :] = (
             hidden_ref[...].astype(F32) + taken
@@ -460,9 +502,11 @@
     updates = turned(edges(mp, lists, returned.reshape(SLOTS, TRIP)), "mp")
     hiddens = turned(layers(mp, updates, states, gathered), "mp")
     keep, give = atoms(mp, core, atom_row, hiddens)
-    part = keep.astype(F32) + turn(give, "graph_2", N_CORE, 1).astype(F32)
-    part = part.astype(BF16).reshape(N_X, HALF_ATOMS // N_X, COLS)
-    part = summed(lax.all_to_all(part, "graph_0", 0, 0, tiled=True))
+    x = jnp.full((1,), lax.axis_index("graph_0"), I32)
+    parts = turned(meet(x, keep, turn(give, "graph_2", N_CORE, 1)), "graph_0")
+    part = (parts[0].astype(F32) + parts[1].astype(F32)) + (
+        parts[2].astype(F32) + parts[3].astype(F32)
+    )
     part = part.astype(BF16).reshape(N_Z, ATOM_DEV, COLS)
     atom_sum = summed(lax.all_to_all(part, "graph_1", 0, 0, tiled=True))
     atom_out = jax.nn.silu(atom_scale * atom_sum).astype(BF16)

time: 354 us -> 346 us (0.977)
  blocking collectives: 48.3 us -> 34.7 us
  waiting for transfers between devices: 164 us -> 175 us
  Pallas kernels: 71.3 us -> 61.3 us
    all_to_all x1 -> x0, blocking collectives: 14.4 us -> none  [local(): part = summed(lax.all_to_all(part, 'graph_0', 0, 0, tiled=True))]
    ppermute x14 -> x17, waiting for transfers between devices: 21.7 us -> 33 us  [turn(): lax.ppermute(array, axis, [(i, (i + shift) % count) for i in range(count)])]
    pallas_call x1 -> x2, Pallas kernels: 41.3 us -> 34.8 us  [the longest x1 34.6 us: triplets(): pl.pallas_call(triplet_kernel, grid=(TRIP_STEPS + SLOT_STEPS,), in_specs=...]
    pallas_call x1, Pallas kernels: 16.6 us -> 13 us  [layers(): pl.pallas_call(layers_kernel, grid=(MAPS * MAP_STEPS,), in_specs=[SCALAR]...]
    ppermute x14 -> x17, starting transfers between devices: 26.3 us -> 28.2 us  [turn(): lax.ppermute(array, axis, [(i, (i + shift) % count) for i in range(count)])]
  transfers between devices with their start and end apart: 17 -> 20, of which waited for: 11 -> 13; matrix products, arithmetic and copies ran while one was open for 2% -> 2% of each run, Pallas kernels for 13% -> 11%
where the time goes in v2:
time: 346 us; the launch traced here: 345 us
  waiting for transfers between devices  175 us (51%)
  Pallas kernels  61.3 us (18%)
  starting transfers between devices  47.7 us (14%)
  blocking collectives  34.7 us (10%)
  between operations  14.2 us (4%)
  local copies, waits for them, and re-layouts  9.12 us (3%)
    all_to_all x1, waiting for transfers between devices, local(): lax.all_to_all(outgoing.reshape(N_GRAPH, CAP, TRIP), GRAPH, split_axis=0,...  72.8 us
    all_to_all x1, waiting for transfers between devices, local(): lax.all_to_all(slot_sums.reshape(N_GRAPH, CAP, TRIP), GRAPH, split_axis=0...  69.1 us
    pallas_call x1, Pallas kernels, triplets(): pl.pallas_call(triplet_kernel, grid=(TRIP_STEPS + SLOT_STEPS,), in_specs=...  34.6 us
    ppermute x17, waiting for transfers between devices, turn(): lax.ppermute(array, axis, [(i, (i + shift) % count) for i in range(count)])  33 us
    ppermute x17, starting transfers between devices, turn(): lax.ppermute(array, axis, [(i, (i + shift) % count) for i in range(count)])  28.2 us
    all_to_all x1, starting transfers between devices, local(): lax.all_to_all(outgoing.reshape(N_GRAPH, CAP, TRIP), GRAPH, split_axis=0,...  13.2 us
    pallas_call x1, Pallas kernels, layers(): pl.pallas_call(layers_kernel, grid=(MAPS * MAP_STEPS,), in_specs=[SCALAR]...  13 us
    all_to_all x1, blocking collectives, local(): atom_sum = summed(lax.all_to_all(part, 'graph_1', 0, 0, tiled=True))  11.9 us
  transfers between devices with their start and end apart: 20, of which 13 were waited for; matrix products, arithmetic and copies ran while one was open for 2% of the time, Pallas kernels for 11%

profile of v2, /device:TPU:1, one launch (start us, length us, event | category | flops | bytes accessed | tf_op | source)
XLA Modules:
  0.0 344.9 jit_solution(8429286390984674862)
XLA Ops:
  7.2 0.0 copy-start
  7.2 0.0 all-gather.3.cloned.1.call-start
  7.2 1.0 copy-done.2
  8.3 1.0 copy-done.3
  9.2 1.0 project.1
  10.3 0.6 copy-done.6
  10.9 2.1 collective-permute-start
  13.0 2.6 collective-permute-start.1
  15.6 1.1 collective-permute-start.2
  16.7 0.8 reshape.51.list_ref
  17.6 2.4 constant_dynamic-slice_fusion.1
  20.0 2.2 pad_maximum_fusion
  22.1 0.0 collective-permute-done.b_ref
  22.1 10.5 %collective-permute-done.1.c_ref = bf16[512,384]{1,0:T(8,128)(2,1)S(1)} collective-permute-done((bf16[512,384]{1,0:T(8,128)(2,1)S(1)}, bf16[512,384]{1,0:T(8,128)(2,1)S(1)}, u32[]{:S(2)}, u32[]{:S(2)}) %collective-permute-start.1) | collective-permute-done | bytes 393248 | tf_op jit(solution)/shard_map/ppermute | solution.py:437
  32.6 5.7 %send.1 = bf16[4096,384]{1,0:T(8,128)(2,1)} custom-call(s32[1,4096]{1,0:T(1,128)S(1)} %reshape.51.list_ref, bf16[512,384]{1,0:T(8,128)(2,1)S(1)} %get-tuple-element.27.a_ref, bf16[512,384]{1,0:T(8,128)(2,1)S(1)} %collective-permute-done.b_ref, bf16[512,384]{1,0:T(8,128)(2,1)S(1)} %collective-permute-done.1.c_ref, ...), custom_call_target="tpu_custom_call" | custom-call | flops 1610612736 | bytes 4700000 | tf_op jit(solution)/shard_map/send/pallas_call | solution.py:125
  38.3 0.0 all-gather.3.cloned.1.call-update
  38.3 0.0 copy-start.10
  38.3 13.2 %all-to-all-start = ((bf16[64,64,384]{2,1,0:T(8,128)(2,1)}), bf16[64,64,384]{2,1,0:T(8,128)(2,1)S(1)}, u32[]{:S(2)}, u32[]{:S(2)}) async-start(bf16[64,64,384]{2,1,0:T(8,128)(2,1)} %bitcast.7), calls=%async_computation | async-start | bytes 6291456 | tf_op jit(solution)/shard_map/all_to_all | solution.py:487
  51.5 0.7 fusion.1.weight_ref
  52.2 72.8 %all-to-all-done = bf16[64,64,384]{2,1,0:T(8,128)(2,1)S(1)} async-done(((bf16[64,64,384]{2,1,0:T(8,128)(2,1)}), bf16[64,64,384]{2,1,0:T(8,128)(2,1)S(1)}, u32[]{:S(2)}, u32[]{:S(2)}) %all-to-all-start) | async-done | bytes 3145760 | tf_op jit(solution)/shard_map/all_to_all | solution.py:487
  125.0 1.6 copy-done.8
  126.6 34.6 %triplets.1 = bf16[2,2048,384]{2,1,0:T(8,128)(2,1)} custom-call(s32[1,4096]{1,0:T(1,128)} %bitcast.28, s32[1,4096]{1,0:T(1,128)} %bitcast.29, s32[1,4096]{1,0:T(1,128)} %bitcast.30, f32[42,4096]{1,0:T(8,128)} %basis_ref.1, bf16[144,384]{1,0:T(8,128)(2,1)} %fusion.1.weight_ref, bf16[4096,384]{1,0:T(8,128)(2,1)} %bitcast.23), custom_call_target="tpu_custom_call" | custom-call | flops 25769803776 | bytes 7000000 | tf_op jit(solution)/shard_map/triplets/pallas_call | solution.py:191
  161.3 6.3 %all-to-all-start.1 = ((bf16[64,64,384]{2,1,0:T(8,128)(2,1)}), bf16[64,64,384]{2,1,0:T(8,128)(2,1)S(1)}, u32[]{:S(2)}, u32[]{:S(2)}) async-start(bf16[64,64,384]{2,1,0:T(8,128)(2,1)} %bitcast.24), calls=%async_computation.1 | async-start | bytes 6291456 | tf_op jit(solution)/shard_map/all_to_all | solution.py:499
  167.6 0.9 collective-permute-start.6
  168.5 2.1 collective-permute-start.7
  170.6 1.4 collective-permute-start.8
  172.0 69.1 %all-to-all-done.1 = bf16[64,64,384]{2,1,0:T(8,128)(2,1)S(1)} async-done(((bf16[64,64,384]{2,1,0:T(8,128)(2,1)}), bf16[64,64,384]{2,1,0:T(8,128)(2,1)S(1)}, u32[]{:S(2)}, u32[]{:S(2)}) %all-to-all-start.1) | async-done | bytes 3145760 | tf_op jit(solution)/shard_map/all_to_all | solution.py:499
  241.1 3.2 edges.1
  244.3 0.0 copy-start.4
  244.3 0.6 copy-done.4
  244.9 0.8 collective-permute-start.3
  245.8 2.1 collective-permute-start.4
  247.9 1.4 collective-permute-start.5
  249.3 0.0 collective-permute-done.7.s2
  249.3 0.0 collective-permute-done.8.s3
  249.3 1.0 collective-permute-done.3.u1
  250.3 2.3 collective-permute-done.4.u2
  252.6 0.0 collective-permute-done.5.u3
  252.7 0.9 copy-done.5
  253.6 13.0 %layers.1 = (bf16[128,384]{1,0:T(8,128)(2,1)S(1)}, bf16[128,384]{1,0:T(8,128)(2,1)S(1)}, bf16[128,384]{1,0:T(8,128)(2,1)S(1)}, bf16[128,384]{1,0:T(8,128)(2,1)S(1)}) custom-call(s32[1]{0:T(128)} %bitcast.mp_ref, bf16[128,384]{1,0:T(8,128)(2,1)S(1)} %copy-done.5, bf16[128,384]{1,0:T(8,128)(2,1)S(1)} %collective-permute-done.3.u1, ...), custom_call_target="tpu_custom_call" | custom-call | flops 3623878656 | bytes 28311552 | tf_op jit(solution)/shard_map/layers/pallas_call | solution.py:319
  266.6 2.2 collective-permute-start.9
  268.8 1.9 collective-permute-start.10
  270.7 0.6 collective-permute-start.11
  271.3 0.2 collective-permute-done.9.h1
  271.5 3.0 collective-permute-done.10.h2
  274.5 0.9 collective-permute-done.11.h3
  275.4 1.3 atoms.1
  276.7 1.6 collective-permute-start.12
  278.3 1.9 collective-permute-done.12.got_ref
  280.2 0.2 meet.1
  280.4 1.9 collective-permute-start.15
  282.3 1.3 collective-permute-start.14
  283.6 3.0 collective-permute-done.15
  286.6 3.0 collective-permute-done.14
  289.6 5.2 %collective-permute-done.13 = bf16[256,384]{1,0:T(8,128)(2,1)S(1)} collective-permute-done((bf16[256,384]{1,0:T(8,128)(2,1)S(1)}, bf16[256,384]{1,0:T(8,128)(2,1)S(1)}, u32[]{:S(2)}, u32[]{:S(2)}) %collective-permute-start.13) | collective-permute-done | bytes 196640 | tf_op jit(solution)/shard_map/ppermute | solution.py:437
  294.8 0.1 add_convert_fusion
  294.9 11.9 %all_to_all.25 = bf16[8,32,384]{2,1,0:T(8,128)(2,1)S(1)} all-to-all(bf16[8,32,384]{2,1,0:T(8,128)(2,1)S(1)} %bitcast.26), channel_id=1, replica_groups=mesh['graph_0'=4,'graph_1'=8,'graph_2'=2,'mp'=4] {'graph_1'}, dimensions={0} | all-to-all | bytes 393216 | tf_op jit(solution)/shard_map/all_to_all | solution.py:511
  306.9 0.0 copy-start.9
  306.9 11.1 %all_to_all.26 = bf16[8,32,384]{2,1,0:T(8,128)(2,1)S(1)} all-to-all(bf16[8,32,384]{2,1,0:T(8,128)(2,1)S(1)} %broadcast_in_dim.25), channel_id=1, replica_groups=mesh['graph_0'=4,'graph_1'=8,'graph_2'=2,'mp'=4] {'graph_1'}, dimensions={0} | all-to-all | bytes 393216 | tf_op jit(solution)/shard_map/all_to_all | solution.py:513
  318.0 0.1 broadcast_in_dim.27
  318.1 11.7 %all_to_all.27 = bf16[4,256,384]{2,1,0:T(8,128)(2,1)S(1)} all-to-all(bf16[4,256,384]{2,1,0:T(8,128)(2,1)S(1)} %broadcast_in_dim.27), channel_id=1, replica_groups=mesh['graph_0'=4,'graph_1'=8,'graph_2'=2,'mp'=4] {'graph_0'}, dimensions={0} | all-to-all | bytes 1572864 | tf_op jit(solution)/shard_map/all_to_all | solution.py:516
  329.8 4.1 %collective-permute-start.16 = (bf16[1024,384]{1,0:T(8,128)(2,1)S(1)}, bf16[1024,384]{1,0:T(8,128)(2,1)S(1)}, u32[]{:S(2)}, u32[]{:S(2)}) collective-permute-start(bf16[1024,384]{1,0:T(8,128)(2,1)S(1)} %bitcast.17), channel_id=1, source_target_pairs={{0,4},{4,0},{1,5},{5,1},{2,6},{6,2},{3,7},{7,3},{8,12},{12,8},{9,1... | collective-permute-start | bytes 2359304 | tf_op jit(solution)/shard_map/ppermute | solution.py:437
  333.9 1.9 collective-permute-done.16.other_ref
  335.8 2.3 final.1
  (22 shorter events, 0.2 us)
Async XLA Ops:
  7.2 10.4 %copy-start = (bf16[384,384]{1,0:T(8,128)(2,1)S(1)}, bf16[384,384]{1,0:T(8,128)(2,1)}, u32[]{:S(2)}) copy-start(bf16[384,384]{1,0:T(8,128)(2,1)} %param.15) | copy-start | bytes 884740
  7.2 245.5 %all-gather.3.cloned.1.call-start = ((), (), s32[]{:S(2)}) async-start(), calls=%async_computation.5 | async-start | bytes 33177600 | tf_op jit(solution)/shard_map/all_gather | solution.py:486
  7.2 1.0 copy-start.2
  8.3 1.0 copy-start.3
  10.3 0.6 copy-start.6
  10.9 11.2 %collective-permute-start = (bf16[512,384]{1,0:T(8,128)(2,1)S(1)}, bf16[512,384]{1,0:T(8,128)(2,1)S(1)}, u32[]{:S(2)}, u32[]{:S(2)}) collective-permute-start(bf16[512,384]{1,0:T(8,128)(2,1)S(1)} %get-tuple-element.27.a_ref), channel_id=1, source_target_pairs={{0,1},{1,2},{2,3},{3,0},{4,5},{5,6},{6,7},{7,4},{8,9},{9,10},{10,1... | collective-permute-start | bytes 1179656 | tf_op jit(solution)/shard_map/ppermute | solution.py:437
  13.0 19.6 %collective-permute-start.1 = (bf16[512,384]{1,0:T(8,128)(2,1)S(1)}, bf16[512,384]{1,0:T(8,128)(2,1)S(1)}, u32[]{:S(2)}, u32[]{:S(2)}) collective-permute-start(bf16[512,384]{1,0:T(8,128)(2,1)S(1)} %get-tuple-element.27.a_ref), channel_id=1, source_target_pairs={{0,2},{1,3},{2,0},{3,1},{4,6},{5,7},{6,4},{7,5},{8,10},{9,11},{10,... | collective-permute-start | bytes 1179656 | tf_op jit(solution)/shard_map/ppermute | solution.py:437
  15.6 16.9 %collective-permute-start.2 = (bf16[512,384]{1,0:T(8,128)(2,1)S(1)}, bf16[512,384]{1,0:T(8,128)(2,1)S(1)}, u32[]{:S(2)}, u32[]{:S(2)}) collective-permute-start(bf16[512,384]{1,0:T(8,128)(2,1)S(1)} %get-tuple-element.27.a_ref), channel_id=1, source_target_pairs={{0,3},{1,0},{2,1},{3,2},{4,7},{5,4},{6,5},{7,6},{8,11},{9,8},{10,9... | collective-permute-start | bytes 1179656 | tf_op jit(solution)/shard_map/ppermute | solution.py:437
  38.3 13.2 %copy-start.10 = (f32[42,384]{1,0:T(8,128)S(1)}, f32[42,384]{1,0:T(8,128)}, u32[]{:S(2)}) copy-start(f32[42,384]{1,0:T(8,128)} %param.14) | copy-start | bytes 193540
  38.3 86.7 %all-to-all-start = ((bf16[64,64,384]{2,1,0:T(8,128)(2,1)}), bf16[64,64,384]{2,1,0:T(8,128)(2,1)S(1)}, u32[]{:S(2)}, u32[]{:S(2)}) async-start(bf16[64,64,384]{2,1,0:T(8,128)(2,1)} %bitcast.7), calls=%async_computation | async-start | bytes 6291456 | tf_op jit(solution)/shard_map/all_to_all | solution.py:487
  125.0 1.6 copy-start.8
  161.3 79.8 %all-to-all-start.1 = ((bf16[64,64,384]{2,1,0:T(8,128)(2,1)}), bf16[64,64,384]{2,1,0:T(8,128)(2,1)S(1)}, u32[]{:S(2)}, u32[]{:S(2)}) async-start(bf16[64,64,384]{2,1,0:T(8,128)(2,1)} %bitcast.24), calls=%async_computation.1 | async-start | bytes 6291456 | tf_op jit(solution)/shard_map/all_to_all | solution.py:499
  167.6 80.3 %collective-permute-start.6 = (bf16[128,384]{1,0:T(8,128)(2,1)}, bf16[128,384]{1,0:T(8,128)(2,1)S(1)}, u32[]{:S(2)}, u32[]{:S(2)}) collective-permute-start(bf16[128,384]{1,0:T(8,128)(2,1)} %get-tuple-element.38), channel_id=1, source_target_pairs={{0,1},{1,2},{2,3},{3,0},{4,5},{5,6},{6,7},{7,4},{8,9},{9,10},{10,1... | collective-permute-start | bytes 294920 | tf_op jit(solution)/shard_map/ppermute | solution.py:437
  168.5 80.8 %collective-permute-start.7 = (bf16[128,384]{1,0:T(8,128)(2,1)}, bf16[128,384]{1,0:T(8,128)(2,1)S(1)}, u32[]{:S(2)}, u32[]{:S(2)}) collective-permute-start(bf16[128,384]{1,0:T(8,128)(2,1)} %get-tuple-element.39), channel_id=1, source_target_pairs={{0,2},{1,3},{2,0},{3,1},{4,6},{5,7},{6,4},{7,5},{8,10},{9,11},{10,... | collective-permute-start | bytes 294920 | tf_op jit(solution)/shard_map/ppermute | solution.py:437
  170.6 78.7 %collective-permute-start.8 = (bf16[128,384]{1,0:T(8,128)(2,1)}, bf16[128,384]{1,0:T(8,128)(2,1)S(1)}, u32[]{:S(2)}, u32[]{:S(2)}) collective-permute-start(bf16[128,384]{1,0:T(8,128)(2,1)} %copy-done.6), channel_id=1, source_target_pairs={{0,3},{1,0},{2,1},{3,2},{4,7},{5,4},{6,5},{7,6},{8,11},{9,8},{10,9... | collective-permute-start | bytes 294920 | tf_op jit(solution)/shard_map/ppermute | solution.py:437
  244.3 0.6 copy-start.4
  244.9 5.4 %collective-permute-start.3 = (bf16[128,384]{1,0:T(8,128)(2,1)S(1)}, bf16[128,384]{1,0:T(8,128)(2,1)S(1)}, u32[]{:S(2)}, u32[]{:S(2)}) collective-permute-start(bf16[128,384]{1,0:T(8,128)(2,1)S(1)} %get-tuple-element.34), channel_id=1, source_target_pairs={{0,1},{1,2},{2,3},{3,0},{4,5},{5,6},{6,7},{7,4},{8,9},{9,10},{10,1... | collective-permute-start | bytes 294920 | tf_op jit(solution)/shard_map/ppermute | solution.py:437
  245.8 6.9 %collective-permute-start.4 = (bf16[128,384]{1,0:T(8,128)(2,1)S(1)}, bf16[128,384]{1,0:T(8,128)(2,1)S(1)}, u32[]{:S(2)}, u32[]{:S(2)}) collective-permute-start(bf16[128,384]{1,0:T(8,128)(2,1)S(1)} %get-tuple-element.35), channel_id=1, source_target_pairs={{0,2},{1,3},{2,0},{3,1},{4,6},{5,7},{6,4},{7,5},{8,10},{9,11},{10,... | collective-permute-start | bytes 294920 | tf_op jit(solution)/shard_map/ppermute | solution.py:437
  247.9 4.8 %collective-permute-start.5 = (bf16[128,384]{1,0:T(8,128)(2,1)S(1)}, bf16[128,384]{1,0:T(8,128)(2,1)S(1)}, u32[]{:S(2)}, u32[]{:S(2)}) collective-permute-start(bf16[128,384]{1,0:T(8,128)(2,1)S(1)} %get-tuple-element.36), channel_id=1, source_target_pairs={{0,3},{1,0},{2,1},{3,2},{4,7},{5,4},{6,5},{7,6},{8,11},{9,8},{10,9... | collective-permute-start | bytes 294920 | tf_op jit(solution)/shard_map/ppermute | solution.py:437
  252.7 0.9 copy-start.5
  253.6 21.8 %copy-start.7 = (s32[512]{0:T(512)S(1)}, s32[512]{0:T(512)}, u32[]{:S(2)}) copy-start(s32[512]{0:T(512)} %param.21) | copy-start | bytes 6148
  266.6 4.9 %collective-permute-start.9 = (bf16[128,384]{1,0:T(8,128)(2,1)S(1)}, bf16[128,384]{1,0:T(8,128)(2,1)S(1)}, u32[]{:S(2)}, u32[]{:S(2)}) collective-permute-start(bf16[128,384]{1,0:T(8,128)(2,1)S(1)} %get-tuple-element.43), channel_id=1, source_target_pairs={{0,1},{1,2},{2,3},{3,0},{4,5},{5,6},{6,7},{7,4},{8,9},{9,10},{10,1... | collective-permute-start | bytes 294920 | tf_op jit(solution)/shard_map/ppermute | solution.py:437
  268.8 5.7 %collective-permute-start.10 = (bf16[128,384]{1,0:T(8,128)(2,1)S(1)}, bf16[128,384]{1,0:T(8,128)(2,1)S(1)}, u32[]{:S(2)}, u32[]{:S(2)}) collective-permute-start(bf16[128,384]{1,0:T(8,128)(2,1)S(1)} %get-tuple-element.44), channel_id=1, source_target_pairs={{0,2},{1,3},{2,0},{3,1},{4,6},{5,7},{6,4},{7,5},{8,10},{9,11},{10,... | collective-permute-start | bytes 294920 | tf_op jit(solution)/shard_map/ppermute | solution.py:437
  270.7 4.7 %collective-permute-start.11 = (bf16[128,384]{1,0:T(8,128)(2,1)S(1)}, bf16[128,384]{1,0:T(8,128)(2,1)S(1)}, u32[]{:S(2)}, u32[]{:S(2)}) collective-permute-start(bf16[128,384]{1,0:T(8,128)(2,1)S(1)} %get-tuple-element.45), channel_id=1, source_target_pairs={{0,3},{1,0},{2,1},{3,2},{4,7},{5,4},{6,5},{7,6},{8,11},{9,8},{10,9... | collective-permute-start | bytes 294920 | tf_op jit(solution)/shard_map/ppermute | solution.py:437
  276.7 3.5 %collective-permute-start.12 = (bf16[1024,384]{1,0:T(8,128)(2,1)S(1)}, bf16[1024,384]{1,0:T(8,128)(2,1)S(1)}, u32[]{:S(2)}, u32[]{:S(2)}) collective-permute-start(bf16[1024,384]{1,0:T(8,128)(2,1)S(1)} %get-tuple-element.47), channel_id=1, source_target_pairs={{0,4},{4,0},{1,5},{5,1},{2,6},{6,2},{3,7},{7,3},{8,12},{12,8},{9,1... | collective-permute-start | bytes 2359304 | tf_op jit(solution)/shard_map/ppermute | solution.py:437
  280.4 6.2 %collective-permute-start.15 = (bf16[256,384]{1,0:T(8,128)(2,1)S(1)}, bf16[256,384]{1,0:T(8,128)(2,1)S(1)}, u32[]{:S(2)}, u32[]{:S(2)}) collective-permute-start(bf16[256,384]{1,0:T(8,128)(2,1)S(1)} %get-tuple-element.51), channel_id=1, source_target_pairs={{0,192},{64,0},{128,64},{192,128},{1,193},{65,1},{129,65},{193,129... | collective-permute-start | bytes 589832 | tf_op jit(solution)/shard_map/ppermute | solution.py:437
  282.3 7.3 %collective-permute-start.14 = (bf16[256,384]{1,0:T(8,128)(2,1)S(1)}, bf16[256,384]{1,0:T(8,128)(2,1)S(1)}, u32[]{:S(2)}, u32[]{:S(2)}) collective-permute-start(bf16[256,384]{1,0:T(8,128)(2,1)S(1)} %get-tuple-element.50), channel_id=1, source_target_pairs={{0,128},{64,192},{128,0},{192,64},{1,129},{65,193},{129,1},{193,65... | collective-permute-start | bytes 589832 | tf_op jit(solution)/shard_map/ppermute | solution.py:437
  283.6 11.2 %collective-permute-start.13 = (bf16[256,384]{1,0:T(8,128)(2,1)S(1)}, bf16[256,384]{1,0:T(8,128)(2,1)S(1)}, u32[]{:S(2)}, u32[]{:S(2)}) collective-permute-start(bf16[256,384]{1,0:T(8,128)(2,1)S(1)} %get-tuple-element.49), channel_id=1, source_target_pairs={{0,64},{64,128},{128,192},{192,0},{1,65},{65,129},{129,193},{193,1... | collective-permute-start | bytes 589832 | tf_op jit(solution)/shard_map/ppermute | solution.py:437
  294.8 43.2 %copy-start.1 = (bf16[384,384]{1,0:T(8,128)(2,1)S(1)}, bf16[384,384]{1,0:T(8,128)(2,1)}, u32[]{:S(2)}) copy-start(bf16[384,384]{1,0:T(8,128)(2,1)} %param.15) | copy-start | bytes 884740
  306.9 31.2 %copy-start.9 = (bf16[32,384]{1,0:T(8,128)(2,1)}, bf16[32,384]{1,0:T(8,128)(2,1)S(1)}, u32[]{:S(2)}) copy-start(bf16[32,384]{1,0:T(8,128)(2,1)S(1)} %multiply_convert_fusion) | copy-start | bytes 73732
  329.8 6.0 %collective-permute-start.16 = (bf16[1024,384]{1,0:T(8,128)(2,1)S(1)}, bf16[1024,384]{1,0:T(8,128)(2,1)S(1)}, u32[]{:S(2)}, u32[]{:S(2)}) collective-permute-start(bf16[1024,384]{1,0:T(8,128)(2,1)S(1)} %bitcast.17), channel_id=1, source_target_pairs={{0,4},{4,0},{1,5},{5,1},{2,6},{6,2},{3,7},{7,3},{8,12},{12,8},{9,1... | collective-permute-start | bytes 2359304 | tf_op jit(solution)/shard_map/ppermute | solution.py:437
Sparse Core Ops, SparseCore 0:
  38.4 149.0 all-gather.2

commit v3 on v2

--- a/solution.py
+++ b/solution.py
@@ -29,6 +29,7 @@
 ATOMS = ATOM_DEV * N_GRAPH
 HALF_ATOMS = ATOMS // N_CORE
 BLOCK = 512
+PARTS = ((0, 128), (128, 384))
 
 F32 = jnp.float32
 BF16 = jnp.bfloat16
@@ -89,20 +90,23 @@
 SCALAR = pl.BlockSpec(memory_space=pltpu.SMEM)
 
 
-def project_kernel(mp_ref, state_ref, weight_ref, partial_ref, *turned_refs):
-    partial_ref[...] = product(state_ref[...], weight_ref[...]).astype(BF16)
-    for k, turned_ref in enumerate(turned_refs):
+def project_kernel(mp_ref, state_ref, weight_ref, *refs):
+    partial = product(state_ref[...], weight_ref[...]).astype(BF16)
+    for partial_ref, (low, high) in zip(refs, PARTS):
+        partial_ref[...] = partial[:, low:high]
+    for k, turned_ref in enumerate(refs[len(PARTS) :]):
         place = lax.rem(mp_ref[0] + k, N_MP) * ROWS
         turned_ref[...] = state_ref[pl.ds(pl.multiple_of(place, ROWS), ROWS), :]
 
 
 def project(mp, edge_state, down_weight):
+    widths = [high - low for low, high in PARTS]
     return pl.pallas_call(
         project_kernel,
         grid=(1,),
         in_specs=[SCALAR, whole((EDGE_DEV, COLS)), whole((COLS, TRIP))],
-        out_specs=[whole((EDGE_DEV, TRIP))] + [whole((ROWS, COLS))] * N_MP,
-        out_shape=[shape_of(EDGE_DEV, TRIP)] + [shape_of(ROWS, COLS)] * N_MP,
+        out_specs=[whole((EDGE_DEV, w)) for w in widths] + [whole((ROWS, COLS))] * N_MP,
+        out_shape=[shape_of(EDGE_DEV, w) for w in widths] + [shape_of(ROWS, COLS)] * N_MP,
         compiler_params=params(24),
         name="project",
         cost_estimate=pl.CostEstimate(
@@ -121,39 +125,44 @@
     out_ref[...] = product(picks(list_ref[...], EDGE_DEV), table[...]).astype(BF16)
 
 
+SEND_BLOCK = 256
+
+
 def send(lists, partials):
+    width = partials[0].shape[1]
     return pl.pallas_call(
         send_kernel,
-        grid=(SLOTS // BLOCK,),
-        in_specs=[pl.BlockSpec((1, BLOCK), lambda i: (0, i))] + [whole((EDGE_DEV, TRIP))] * N_MP,
-        out_specs=pl.BlockSpec((BLOCK, TRIP), lambda i: (i, 0)),
-        out_shape=shape_of(SLOTS, TRIP),
-        scratch_shapes=[pltpu.VMEM((EDGE_DEV, TRIP), BF16)],
+        grid=(SLOTS // SEND_BLOCK,),
+        in_specs=[pl.BlockSpec((1, SEND_BLOCK), lambda i: (0, i))] + [whole((EDGE_DEV, width))] * N_MP,
+        out_specs=pl.BlockSpec((SEND_BLOCK, width), lambda i: (i, 0)),
+        out_shape=shape_of(SLOTS, width),
+        scratch_shapes=[pltpu.VMEM((EDGE_DEV, width), BF16)],
         compiler_params=params(24),
         name="send",
         cost_estimate=pl.CostEstimate(
-            flops=2 * SLOTS * EDGE_DEV * TRIP, bytes_accessed=4700000, transcendentals=0
+            flops=2 * SLOTS * EDGE_DEV * width, bytes_accessed=12000 * width, transcendentals=0
         ),
     )(lists, *partials)
 
 
-TRIP_STEPS = TRIPS // BLOCK
-HALF_SLOTS = SLOTS // 2
+TRIP_BLOCK = 256
+TRIP_STEPS = TRIPS // TRIP_BLOCK
 SLOT_BLOCK = 256
-SLOT_STEPS = HALF_SLOTS // SLOT_BLOCK
-FEATURE_BLOCKS = range(0, TRIP, 128)
+SUM_CHUNK = 2048
 
 
 def triplet_kernel(
-    in_ref, live_ref, to_ref, basis_ref, weight_ref, table_ref, out_ref, table, values, padded
+    groups, in_ref, live_ref, to_ref, basis_ref, weight_ref, table_ref, out_ref, table, values, padded
 ):
     step = pl.program_id(0)
+    width = table_ref.shape[1]
+    deep = SLOTS // groups
 
     @pl.when(step == 0)
     def _():
         padded[...] = jnp.zeros_like(padded)
-        table[:, :TRIP] = table_ref[:HALF_SLOTS, :]
-        table[:, TRIP:] = table_ref[HALF_SLOTS:, :]
+        for h in range(groups):
+            table[:, h * width : (h + 1) * width] = table_ref[h * deep : (h + 1) * deep, :]
 
     @pl.when(step < TRIP_STEPS)
     def _():
@@ -165,53 +174,67 @@
         coef = lax.dot_general(
             stacked, weight_ref[...], (((0,), (0,)), ((), ())), preferred_element_type=F32
         )
-        place = pl.multiple_of(step * BLOCK, BLOCK)
+        place = pl.multiple_of(step * TRIP_BLOCK, TRIP_BLOCK)
         source = column_of(in_ref[...])
-        target = column_of(to_ref[:, pl.ds(place, BLOCK)])
-        near = source < HALF_SLOTS
-        first = target < HALF_SLOTS
-        both = product(picks_of(source & (HALF_SLOTS - 1), HALF_SLOTS), table[...])
-        for k in FEATURE_BLOCKS:
-            at, far = slice(k, k + 128), slice(TRIP + k, TRIP + k + 128)
-            value = jnp.where(near, both[:, at], both[:, far]) * coef[:, at]
-            values[pl.ds(place, BLOCK), at] = jnp.where(first, value, 0.0).astype(BF16)
-            values[pl.ds(place, BLOCK), far] = jnp.where(first, 0.0, value).astype(BF16)
+        target = column_of(to_ref[:, pl.ds(place, TRIP_BLOCK)])
+        candidates = product(picks_of(source & (deep - 1), deep), table[...])
+        for k in range(0, width, 128):
+            value = candidates[:, k : k + 128]
+            for h in range(1, groups):
+                at = h * width + k
+                value = jnp.where(source >= h * deep, candidates[:, at : at + 128], value)
+            value = value * coef[:, k : k + 128]
+            for h in range(groups):
+                at = h * width + k
+                here = (target >= h * deep) & (target < (h + 1) * deep)
+                values[pl.ds(place, TRIP_BLOCK), at : at + 128] = jnp.where(here, value, 0.0).astype(
+                    BF16
+                )
 
     @pl.when(step >= TRIP_STEPS)
     def _():
-        row = to_ref[...] & (HALF_SLOTS - 1)
-        chosen = members(row, SLOT_BLOCK, (step - TRIP_STEPS) * SLOT_BLOCK)
-        total = product(chosen, values[...]).astype(BF16)
-        out_ref[0] = total[:, :TRIP]
-        out_ref[1] = total[:, TRIP:]
+        first = (step - TRIP_STEPS) * SLOT_BLOCK
+
+        def more(i, total):
+            rows = pl.ds(pl.multiple_of(i * SUM_CHUNK, SUM_CHUNK), SUM_CHUNK)
+            chosen = members(to_ref[:, rows] & (deep - 1), SLOT_BLOCK, first)
+            return total + product(chosen, values[rows, :])
+
+        empty = jnp.zeros((SLOT_BLOCK, groups * width), F32)
+        total = lax.fori_loop(0, TRIPS // SUM_CHUNK, more, empty).astype(BF16)
+        for h in range(groups):
+            out_ref[h] = total[:, h * width : (h + 1) * width]
 
 
 def triplets(trip_in, trip_live, trip_out, basis, weight, table):
+    width = table.shape[1]
+    groups = 512 // width
+    deep = SLOTS // groups
     gather_step = lambda i: (0, jnp.minimum(i, TRIP_STEPS - 1))
     return pl.pallas_call(
-        triplet_kernel,
-        grid=(TRIP_STEPS + SLOT_STEPS,),
+        functools.partial(triplet_kernel, groups),
+        grid=(TRIP_STEPS + deep // SLOT_BLOCK,),
         in_specs=[
-            pl.BlockSpec((1, BLOCK), gather_step),
-            pl.BlockSpec((1, BLOCK), gather_step),
+            pl.BlockSpec((1, TRIP_BLOCK), gather_step),
+            pl.BlockSpec((1, TRIP_BLOCK), gather_step),
             whole((1, TRIPS)),
-            pl.BlockSpec((NSBF, BLOCK), gather_step),
-            whole((3 * BASIS_PAD, TRIP)),
-            whole((SLOTS, TRIP)),
+            pl.BlockSpec((NSBF, TRIP_BLOCK), gather_step),
+            whole((3 * BASIS_PAD, width)),
+            whole((SLOTS, width)),
         ],
         out_specs=pl.BlockSpec(
-            (2, SLOT_BLOCK, TRIP), lambda i: (0, jnp.maximum(i - TRIP_STEPS, 0), 0)
-        ),
-        out_shape=shape_of(2, HALF_SLOTS, TRIP),
+            (groups, SLOT_BLOCK, width), lambda i: (0, jnp.maximum(i - TRIP_STEPS, 0), 0)
+        ),
+        out_shape=shape_of(groups, deep, width),
         scratch_shapes=[
-            pltpu.VMEM((HALF_SLOTS, 2 * TRIP), BF16),
-            pltpu.VMEM((TRIPS, 2 * TRIP), BF16),
-            pltpu.VMEM((BASIS_PAD, BLOCK), F32),
+            pltpu.VMEM((deep, groups * width), BF16),
+            pltpu.VMEM((TRIPS, groups * width), BF16),
+            pltpu.VMEM((BASIS_PAD, TRIP_BLOCK), F32),
         ],
-        compiler_params=params(60),
+        compiler_params=params(48),
         name="triplets",
         cost_estimate=pl.CostEstimate(
-            flops=4 * TRIPS * SLOTS * TRIP, bytes_accessed=7000000, transcendentals=0
+            flops=4 * TRIPS * SLOTS * width, bytes_accessed=18000 * width, transcendentals=0
         ),
     )(trip_in, trip_live, trip_out, basis, weight, table)
 
@@ -220,7 +243,7 @@
 
 
 def edges_kernel(mp_ref, list_ref, table_ref, *refs):
-    outs, total = refs[:N_MP], refs[N_MP]
+    earlier, outs, total = refs[: -N_MP - 1], refs[-N_MP - 1 : -1], refs[-1]
     step = pl.program_id(0)
     part = product(members(list_ref[...], EDGE_DEV, 0), table_ref[...])
 
@@ -236,34 +259,44 @@
     def _():
         for k, out_ref in enumerate(outs):
             place = lax.rem(mp_ref[0] + k, N_MP) * ROWS
-            out_ref[...] = total[pl.ds(pl.multiple_of(place, ROWS), ROWS), :].astype(BF16)
-
-
-def edges(mp, lists, returned):
+            low = 0
+            if earlier:
+                low = earlier[k].shape[1]
+                out_ref[:, :low] = earlier[k][...]
+            out_ref[:, low:] = total[pl.ds(pl.multiple_of(place, ROWS), ROWS), :].astype(BF16)
+
+
+def edges(mp, lists, returned, earlier):
+    width = returned.shape[1]
+    before = [block.shape[1] for block in earlier]
+    full = width + (before[0] if before else 0)
     return pl.pallas_call(
         edges_kernel,
         grid=(SLOTS // EDGE_CHUNK,),
         in_specs=[
             SCALAR,
             pl.BlockSpec((1, EDGE_CHUNK), lambda i: (0, i)),
-            pl.BlockSpec((EDGE_CHUNK, TRIP), lambda i: (i, 0)),
-        ],
-        out_specs=[whole((ROWS, TRIP))] * N_MP,
-        out_shape=[shape_of(ROWS, TRIP)] * N_MP,
-        scratch_shapes=[pltpu.VMEM((EDGE_DEV, TRIP), F32)],
+            pl.BlockSpec((EDGE_CHUNK, width), lambda i: (i, 0)),
+        ]
+        + [whole((ROWS, w)) for w in before],
+        out_specs=[whole((ROWS, full))] * N_MP,
+        out_shape=[shape_of(ROWS, full)] * N_MP,
+        scratch_shapes=[pltpu.VMEM((EDGE_DEV, width), F32)],
         compiler_params=params(24),
         name="edges",
         cost_estimate=pl.CostEstimate(
-            flops=2 * SLOTS * EDGE_DEV * TRIP, bytes_accessed=3500000, transcendentals=0
-        ),
-    )(mp, lists, returned)
+            flops=2 * SLOTS * EDGE_DEV * width, bytes_accessed=9000 * width, transcendentals=0
+        ),
+    )(mp, lists, returned, *earlier)
 
 
 SIDE = 4
 MAP_STEPS = N_MP // SIDE
 
 
-def layers_kernel(mp_ref, u0, u1, u2, u3, s0, s1, s2, s3, up_ref, weight_ref, *refs):
+def layers_kernel(mp_ref, *refs):
+    updates, refs = refs[:N_MP], refs[N_MP:]
+    states, (up_ref, weight_ref), refs = refs[:N_MP], refs[N_MP : N_MP + 2], refs[N_MP + 2 :]
     outs = refs[:N_MP]
     hidden, given, inner = refs[N_MP:]
     step = pl.program_id(0)
@@ -276,10 +309,9 @@
 
     @pl.when(step == 0)
     def _():
-        total = u0[...].astype(F32) + u1[...].astype(F32)
-        total = total + (u2[...].astype(F32) + u3[...].astype(F32))
-        update = total.astype(BF16)
-        for k, state_ref in enumerate((s0, s1, s2, s3)):
+        a, b, c, d = (ref[...].astype(F32) for ref in updates)
+        update = ((a + b) + (c + d)).astype(BF16)
+        for k, state_ref in enumerate(states):
             hidden[:, columns(lax.rem(me + N_MP - k, N_MP))] = state_ref[...].astype(F32)
         for block in range(N_MP):
             added = product(update[:, :UP_HALF], up_ref[block])
@@ -292,17 +324,25 @@
     @pl.when(lax.rem(which, 2) == 0)
     def _():
         x = given[...]
-        for j in range(SIDE):
+
+        def one(j, carry):
             inner[:, columns(side + j)] = silu(product(x, weight_ref[j])).astype(BF16)
+            return carry
+
+        lax.fori_loop(0, SIDE, one, 0)
 
     @pl.when(lax.rem(which, 2) == 1)
     def _():
         x = inner[...]
-        for j in range(SIDE):
+
+        def one(j, carry):
             at = columns(side + j)
             fresh = (hidden[:, at] + silu(product(x, weight_ref[j]))) * inv_root_two
             hidden[:, at] = fresh
             given[:, at] = fresh.astype(BF16)
+            return carry
+
+        lax.fori_loop(0, SIDE, one, 0)
 
     @pl.when(step == MAPS * MAP_STEPS - 1)
     def _():
@@ -479,27 +519,34 @@
         axis=0,
     )
 
-    partial, *state_blocks = project(mp, edge_state, down_weight)
-    partials = turned([partial] * N_MP, "mp")
-    outgoing = send(lists, partials)
-    outgoing, half, *state_blocks = lax.optimization_barrier((outgoing, half, *state_blocks))
+    trip_in = trip_in.reshape(1, TRIPS)
+    trip_live = trip_live.reshape(1, TRIPS)
+    trip_out = trip_out.reshape(1, TRIPS)
+    first, second, *state_blocks = project(mp, edge_state, down_weight)
+    exchange = functools.partial(
+        lax.all_to_all, axis_name=GRAPH, split_axis=0, concat_axis=0, tiled=True
+    )
+
+    def sums(received, part):
+        low, high = part
+        table = received.reshape(SLOTS, high - low)
+        weight = coef_weight[:, low:high]
+        total = triplets(trip_in, trip_live, trip_out, basis, weight, table)
+        return total.reshape(N_GRAPH, CAP, high - low)
+
+    first = send(lists, turned([first] * N_MP, "mp")).reshape(N_GRAPH, CAP, -1)
+    first, second = lax.optimization_barrier((first, second))
+    partials = turned([second] * N_MP, "mp")
+    first = exchange(first)
+    first, half, *partials = lax.optimization_barrier((first, half, *partials))
+    second = exchange(send(lists, partials).reshape(N_GRAPH, CAP, -1))
     gathered = lax.all_gather(half, ("graph_2", "mp"), axis=0, tiled=False)
-    received = lax.all_to_all(
-        outgoing.reshape(N_GRAPH, CAP, TRIP), GRAPH, split_axis=0, concat_axis=0, tiled=True
-    )
     states = turned(state_blocks, "mp")
-    slot_sums = triplets(
-        trip_in.reshape(1, TRIPS),
-        trip_live.reshape(1, TRIPS),
-        trip_out.reshape(1, TRIPS),
-        basis,
-        coef_weight,
-        received.reshape(SLOTS, TRIP),
-    )
-    returned = lax.all_to_all(
-        slot_sums.reshape(N_GRAPH, CAP, TRIP), GRAPH, split_axis=0, concat_axis=0, tiled=True
-    )
-    updates = turned(edges(mp, lists, returned.reshape(SLOTS, TRIP)), "mp")
+    first = exchange(sums(first, PARTS[0]))
+    second = exchange(sums(second, PARTS[1]))
+    blocks = edges(mp, lists, first.reshape(SLOTS, -1), [])
+    blocks = edges(mp, lists, second.reshape(SLOTS, -1), blocks)
+    updates = turned(blocks, "mp")
     hiddens = turned(layers(mp, updates, states, gathered), "mp")
     keep, give = atoms(mp, core, atom_row, hiddens)
     x = jnp.full((1,), lax.axis_index("graph_0"), I32)

time: 346 us -> 333 us (0.962)
  waiting for transfers between devices: 175 us -> 123 us
  starting transfers between devices: 47.7 us -> 67.9 us
  Pallas kernels: 61.3 us -> 79.6 us
    all_to_all x2 -> x4, waiting for transfers between devices: 142 us -> 87.8 us  [the longest x1 44.9 us: local(): second = exchange(sums(second, PARTS[1]))]
    all_to_all x2 -> x4, starting transfers between devices: 19.5 us -> 35.7 us  [the longest x1 13 us: local(): first = exchange(first)]
    pallas_call x2 -> x4, Pallas kernels: 40.3 us -> 55.9 us  [the longest x2 43.6 us: triplets(): pl.pallas_call(functools.partial(triplet_kernel, groups), grid=(TRIP_STEP...]
    ppermute x17 -> x20, starting transfers between devices: 28.2 us -> 32.1 us  [turn(): lax.ppermute(array, axis, [(i, (i + shift) % count) for i in range(count)])]
    unnamed x22 -> x30, local copies, waits for them, and re-layouts: 5.8 us -> 7.96 us
    ppermute x17 -> x20, waiting for transfers between devices: 33 us -> 34.7 us  [turn(): lax.ppermute(array, axis, [(i, (i + shift) % count) for i in range(count)])]
  transfers between devices with their start and end apart: 20 -> 25, of which waited for: 13 -> 18; matrix products, arithmetic and copies ran while one was open for 2% -> 2% of each run, Pallas kernels for 11% -> 14%
where the time goes in v3:
time: 333 us; the launch traced here: 332 us
  waiting for transfers between devices  123 us (37%)
  Pallas kernels  79.6 us (24%)
  starting transfers between devices  67.9 us (20%)
  blocking collectives  34.5 us (10%)
  between operations  14.4 us (4%)
  local copies, waits for them, and re-layouts  11.3 us (3%)
    all_to_all x1, waiting for transfers between devices, local(): second = exchange(sums(second, PARTS[1]))  44.9 us
    pallas_call x2, Pallas kernels, triplets(): pl.pallas_call(functools.partial(triplet_kernel, groups), grid=(TRIP_STEP...  43.6 us
    ppermute x20, waiting for transfers between devices, turn(): lax.ppermute(array, axis, [(i, (i + shift) % count) for i in range(count)])  34.7 us
    ppermute x20, starting transfers between devices, turn(): lax.ppermute(array, axis, [(i, (i + shift) % count) for i in range(count)])  32.1 us
    all_to_all x1, waiting for transfers between devices, local(): second = exchange(send(lists, partials).reshape(N_GRAPH, CAP, -1))  31.5 us
    pallas_call x1, Pallas kernels, layers(): pl.pallas_call(layers_kernel, grid=(MAPS * MAP_STEPS,), in_specs=[SCALAR]...  15 us
    all_to_all x1, starting transfers between devices, local(): first = exchange(first)  13 us
    pallas_call x2, Pallas kernels, send(): pl.pallas_call(send_kernel, grid=(SLOTS // SEND_BLOCK,), in_specs=[pl.Blo...  12.3 us
  transfers between devices with their start and end apart: 25, of which 18 were waited for; matrix products, arithmetic and copies ran while one was open for 2% of the time, Pallas kernels for 14%

profile of v3, /device:TPU:1, one launch (start us, length us, event | category | flops | bytes accessed | tf_op | source)
XLA Modules:
  0.0 332.5 jit_solution(2960468140300610004)
XLA Ops:
  7.2 1.0 copy-done.5
  8.2 1.0 copy-done.6
  9.2 1.0 project.1
  10.2 2.1 collective-permute-start
  12.3 2.6 collective-permute-start.1
  15.0 1.1 collective-permute-start.2
  16.0 0.8 reshape.63.list_ref
  16.9 3.8 %collective-permute-done.1.c_ref = bf16[512,128]{1,0:T(8,128)(2,1)S(1)} collective-permute-done((bf16[512,128]{1,0:T(8,128)(2,1)S(1)}, bf16[512,128]{1,0:T(8,128)(2,1)S(1)}, u32[]{:S(2)}, u32[]{:S(2)}) %collective-permute-start.1) | collective-permute-done | bytes 131104 | tf_op jit(solution)/shard_map/ppermute | solution.py:477
  20.7 7.6 %send.2 = bf16[4096,128]{1,0:T(8,128)(2,1)} custom-call(s32[1,4096]{1,0:T(1,128)S(1)} %reshape.63.list_ref, bf16[512,128]{1,0:T(8,128)(2,1)S(1)} %get-tuple-element.34.a_ref, bf16[512,128]{1,0:T(8,128)(2,1)S(1)} %collective-permute-done.b_ref, bf16[512,128]{1,0:T(8,128)(2,1)S(1)} %collective-permute-done.1.c_ref, ...), custom_call_target="tpu_custom_call" | custom-call | flops 536870912 | bytes 1536000 | tf_op jit(solution)/shard_map/send/pallas_call | solution.py:133
  28.3 13.0 %all-to-all-start = ((bf16[64,64,128]{2,1,0:T(8,128)(2,1)}), bf16[64,64,128]{2,1,0:T(8,128)(2,1)S(1)}, u32[]{:S(2)}, u32[]{:S(2)}) async-start(bf16[64,64,128]{2,1,0:T(8,128)(2,1)} %bitcast.6), calls=%async_computation | async-start | bytes 2097152 | tf_op jit(solution)/shard_map/all_to_all | solution.py:540
  41.4 2.4 constant_dynamic-slice_fusion.1
  43.8 0.9 collective-permute-start.3
  44.7 2.1 collective-permute-start.4
  46.8 1.4 collective-permute-start.5
  48.2 2.2 pad_maximum_fusion
  50.4 2.1 collective-permute-done.3.b_ref
  52.5 5.9 %collective-permute-done.4.c_ref = bf16[512,256]{1,0:T(8,128)(2,1)S(1)} collective-permute-done((bf16[512,256]{1,0:T(8,128)(2,1)S(1)}, bf16[512,256]{1,0:T(8,128)(2,1)S(1)}, u32[]{:S(2)}, u32[]{:S(2)}) %collective-permute-start.4) | collective-permute-done | bytes 262176 | tf_op jit(solution)/shard_map/ppermute | solution.py:477
  58.5 11.4 %all-to-all-done = bf16[64,64,128]{2,1,0:T(8,128)(2,1)S(1)} async-done(((bf16[64,64,128]{2,1,0:T(8,128)(2,1)}), bf16[64,64,128]{2,1,0:T(8,128)(2,1)S(1)}, u32[]{:S(2)}, u32[]{:S(2)}) %all-to-all-start) | async-done | bytes 1048608 | tf_op jit(solution)/shard_map/all_to_all | solution.py:540
  69.9 4.7 %send.3 = bf16[4096,256]{1,0:T(8,128)(2,1)S(1)} custom-call(s32[1,4096]{1,0:T(1,128)S(1)} %reshape.63.list_ref, bf16[512,256]{1,0:T(8,128)(2,1)S(1)} %get-tuple-element.38.a_ref, bf16[512,256]{1,0:T(8,128)(2,1)S(1)} %collective-permute-done.3.b_ref, bf16[512,256]{1,0:T(8,128)(2,1)S(1)} %collective-permute-done.4.c_ref, ...), custom_call_target="tpu_custom_call" | custom-call | flops 1073741824 | bytes 3072000 | tf_op jit(solution)/shard_map/send/pallas_call | solution.py:133
  74.6 1.3 copy-done.3
  75.9 6.3 %all-to-all-start.1 = ((bf16[64,64,256]{2,1,0:T(8,128)(2,1)}), bf16[64,64,256]{2,1,0:T(8,128)(2,1)S(1)}, u32[]{:S(2)}, u32[]{:S(2)}) async-start(bf16[64,64,256]{2,1,0:T(8,128)(2,1)} %bitcast.23), calls=%async_computation.1 | async-start | bytes 4194304 | tf_op jit(solution)/shard_map/all_to_all | solution.py:542
  82.4 1.2 copy-done.7
  83.6 17.4 %triplets.3 = bf16[4,1024,128]{2,1,0:T(8,128)(2,1)S(1)} custom-call(s32[1,4096]{1,0:T(1,128)S(1)} %bitcast.29, s32[1,4096]{1,0:T(1,128)S(1)} %bitcast.31, s32[1,4096]{1,0:T(1,128)S(1)} %bitcast.33, f32[42,4096]{1,0:T(8,128)S(1)} %copy-done.7, bf16[144,128]{1,0:T(8,128)(2,1)S(1)} %slice.9.weight_ref, bf16[4096,128]{1,0:T(8,128)(2,1)S(1)} %bitcast.24), custom_call_target="tpu_custom_call" | custom-call | flops 8589934592 | bytes 2304000 | tf_op jit(solution)/shard_map/triplets/pallas_call | solution.py:214
  101.0 1.0 copy-done.4
  102.0 31.5 %all-to-all-done.1 = bf16[64,64,256]{2,1,0:T(8,128)(2,1)S(1)} async-done(((bf16[64,64,256]{2,1,0:T(8,128)(2,1)}), bf16[64,64,256]{2,1,0:T(8,128)(2,1)S(1)}, u32[]{:S(2)}, u32[]{:S(2)}) %all-to-all-start.1) | async-done | bytes 2097184 | tf_op jit(solution)/shard_map/all_to_all | solution.py:542
  133.5 5.8 %all-to-all-start.3 = ((bf16[64,64,128]{2,1,0:T(8,128)(2,1)}), bf16[64,64,128]{2,1,0:T(8,128)(2,1)S(1)}, u32[]{:S(2)}, u32[]{:S(2)}) async-start(bf16[64,64,128]{2,1,0:T(8,128)(2,1)} %bitcast.26), calls=%async_computation.3 | async-start | bytes 2097152 | tf_op jit(solution)/shard_map/all_to_all | solution.py:545
  139.3 1.1 copy-done.8
  140.5 26.2 %triplets.2 = bf16[2,2048,256]{2,1,0:T(8,128)(2,1)S(1)} custom-call(s32[1,4096]{1,0:T(1,128)S(1)} %bitcast.30, s32[1,4096]{1,0:T(1,128)S(1)} %bitcast.32, s32[1,4096]{1,0:T(1,128)S(1)} %bitcast.34, f32[42,4096]{1,0:T(8,128)S(1)} %copy-done.8, bf16[144,256]{1,0:T(8,128)(2,1)S(1)} %slice.8.weight_ref, bf16[4096,256]{1,0:T(8,128)(2,1)S(1)} %bitcast.21), custom_call_target="tpu_custom_call" | custom-call | flops 17179869184 | bytes 4608000 | tf_op jit(solution)/shard_map/triplets/pallas_call | solution.py:214
  166.7 1.3 copy-done.2
  168.0 10.5 %all-to-all-start.2 = ((bf16[64,64,256]{2,1,0:T(8,128)(2,1)}), bf16[64,64,256]{2,1,0:T(8,128)(2,1)S(1)}, u32[]{:S(2)}, u32[]{:S(2)}) async-start(bf16[64,64,256]{2,1,0:T(8,128)(2,1)} %bitcast.22), calls=%async_computation.2 | async-start | bytes 4194304 | tf_op jit(solution)/shard_map/all_to_all | solution.py:546
  178.5 0.9 collective-permute-start.9
  179.4 2.1 collective-permute-start.10
  181.5 1.4 collective-permute-start.11
  182.9 1.9 edges.2
  184.8 44.9 %all-to-all-done.2 = bf16[64,64,256]{2,1,0:T(8,128)(2,1)S(1)} async-done(((bf16[64,64,256]{2,1,0:T(8,128)(2,1)}), bf16[64,64,256]{2,1,0:T(8,128)(2,1)S(1)}, u32[]{:S(2)}, u32[]{:S(2)}) %all-to-all-start.2) | async-done | bytes 2097184 | tf_op jit(solution)/shard_map/all_to_all | solution.py:546
  229.7 2.0 edges.3
  231.8 0.9 collective-permute-start.6
  232.7 2.1 collective-permute-start.7
  234.8 1.4 collective-permute-start.8
  236.2 0.8 collective-permute-done.6.refs_1_
  237.0 2.4 collective-permute-done.7.refs_2_
  239.4 0.2 collective-permute-done.8.refs_3_
  239.6 15.0 %layers.1 = (bf16[128,384]{1,0:T(8,128)(2,1)S(1)}, bf16[128,384]{1,0:T(8,128)(2,1)S(1)}, bf16[128,384]{1,0:T(8,128)(2,1)S(1)}, bf16[128,384]{1,0:T(8,128)(2,1)S(1)}) custom-call(s32[1]{0:T(128)} %bitcast.mp_ref, bf16[128,384]{1,0:T(8,128)(2,1)S(1)} %get-tuple-element.47.refs_0_, bf16[128,384]{1,0:T(8,128)(2,1)S(1)} %collective-permute-done.6.refs_1_, ...), custom_call_target="tpu_custom_call" | custom-call | flops 3623878656 | bytes 28311552 | tf_op jit(solution)/shard_map/layers/pallas_call | solution.py:359
  254.7 2.1 collective-permute-start.12
  256.8 1.9 collective-permute-start.13
  258.7 0.6 collective-permute-start.14
  259.3 0.2 collective-permute-done.12.h1
  259.5 2.8 collective-permute-done.13.h2
  262.4 1.1 collective-permute-done.14.h3
  263.5 1.3 atoms.1
  264.8 1.6 collective-permute-start.15
  266.4 1.9 collective-permute-done.15.got_ref
  268.3 0.2 meet.1
  268.5 1.6 collective-permute-start.18
  270.1 1.1 collective-permute-start.17
  271.2 3.5 %collective-permute-done.18 = bf16[256,384]{1,0:T(8,128)(2,1)S(1)} collective-permute-done((bf16[256,384]{1,0:T(8,128)(2,1)S(1)}, bf16[256,384]{1,0:T(8,128)(2,1)S(1)}, u32[]{:S(2)}, u32[]{:S(2)}) %collective-permute-start.18) | collective-permute-done | bytes 196640 | tf_op jit(solution)/shard_map/ppermute | solution.py:477
  274.7 2.8 collective-permute-done.17
  277.4 5.2 %collective-permute-done.16 = bf16[256,384]{1,0:T(8,128)(2,1)S(1)} collective-permute-done((bf16[256,384]{1,0:T(8,128)(2,1)S(1)}, bf16[256,384]{1,0:T(8,128)(2,1)S(1)}, u32[]{:S(2)}, u32[]{:S(2)}) %collective-permute-start.16) | collective-permute-done | bytes 196640 | tf_op jit(solution)/shard_map/ppermute | solution.py:477
  282.7 11.6 %all_to_all.35 = bf16[8,32,384]{2,1,0:T(8,128)(2,1)S(1)} all-to-all(bf16[8,32,384]{2,1,0:T(8,128)(2,1)S(1)} %bitcast.40), channel_id=1, replica_groups=mesh['graph_0'=4,'graph_1'=8,'graph_2'=2,'mp'=4] {'graph_1'}, dimensions={0} | all-to-all | bytes 393216 | tf_op jit(solution)/shard_map/all_to_all | solution.py:558
  294.5 11.3 %all_to_all.36 = bf16[8,32,384]{2,1,0:T(8,128)(2,1)S(1)} all-to-all(bf16[8,32,384]{2,1,0:T(8,128)(2,1)S(1)} %broadcast_in_dim.25), channel_id=1, replica_groups=mesh['graph_0'=4,'graph_1'=8,'graph_2'=2,'mp'=4] {'graph_1'}, dimensions={0} | all-to-all | bytes 393216 | tf_op jit(solution)/shard_map/all_to_all | solution.py:560
  305.8 11.6 %all_to_all.37 = bf16[4,256,384]{2,1,0:T(8,128)(2,1)S(1)} all-to-all(bf16[4,256,384]{2,1,0:T(8,128)(2,1)S(1)} %broadcast_in_dim.27), channel_id=1, replica_groups=mesh['graph_0'=4,'graph_1'=8,'graph_2'=2,'mp'=4] {'graph_0'}, dimensions={0} | all-to-all | bytes 1572864 | tf_op jit(solution)/shard_map/all_to_all | solution.py:563
  317.4 4.0 %collective-permute-start.19 = (bf16[1024,384]{1,0:T(8,128)(2,1)S(1)}, bf16[1024,384]{1,0:T(8,128)(2,1)S(1)}, u32[]{:S(2)}, u32[]{:S(2)}) collective-permute-start(bf16[1024,384]{1,0:T(8,128)(2,1)S(1)} %bitcast.27), channel_id=1, source_target_pairs={{0,4},{4,0},{1,5},{5,1},{2,6},{6,2},{3,7},{7,3},{8,12},{12,8},{9,1... | collective-permute-start | bytes 2359304 | tf_op jit(solution)/shard_map/ppermute | solution.py:477
  321.5 1.9 collective-permute-done.19.other_ref
  323.4 2.2 final.1
  (45 shorter events, 0.5 us)
Async XLA Ops:
  7.2 34.2 %copy-start = (bf16[384,384]{1,0:T(8,128)(2,1)S(1)}, bf16[384,384]{1,0:T(8,128)(2,1)}, u32[]{:S(2)}) copy-start(bf16[384,384]{1,0:T(8,128)(2,1)} %param.15) | copy-start | bytes 884740
  7.2 1.0 copy-start.5
  8.2 1.0 copy-start.6
  10.2 6.7 %collective-permute-start = (bf16[512,128]{1,0:T(8,128)(2,1)S(1)}, bf16[512,128]{1,0:T(8,128)(2,1)S(1)}, u32[]{:S(2)}, u32[]{:S(2)}) collective-permute-start(bf16[512,128]{1,0:T(8,128)(2,1)S(1)} %get-tuple-element.34.a_ref), channel_id=1, source_target_pairs={{0,1},{1,2},{2,3},{3,0},{4,5},{5,6},{6,7},{7,4},{8,9},{9,10},{10,1... | collective-permute-start | bytes 393224 | tf_op jit(solution)/shard_map/ppermute | solution.py:477
  12.3 8.3 %collective-permute-start.1 = (bf16[512,128]{1,0:T(8,128)(2,1)S(1)}, bf16[512,128]{1,0:T(8,128)(2,1)S(1)}, u32[]{:S(2)}, u32[]{:S(2)}) collective-permute-start(bf16[512,128]{1,0:T(8,128)(2,1)S(1)} %get-tuple-element.34.a_ref), channel_id=1, source_target_pairs={{0,2},{1,3},{2,0},{3,1},{4,6},{5,7},{6,4},{7,5},{8,10},{9,11},{10,... | collective-permute-start | bytes 393224 | tf_op jit(solution)/shard_map/ppermute | solution.py:477
  15.0 5.7 %collective-permute-start.2 = (bf16[512,128]{1,0:T(8,128)(2,1)S(1)}, bf16[512,128]{1,0:T(8,128)(2,1)S(1)}, u32[]{:S(2)}, u32[]{:S(2)}) collective-permute-start(bf16[512,128]{1,0:T(8,128)(2,1)S(1)} %get-tuple-element.34.a_ref), channel_id=1, source_target_pairs={{0,3},{1,0},{2,1},{3,2},{4,7},{5,4},{6,5},{7,6},{8,11},{9,8},{10,9... | collective-permute-start | bytes 393224 | tf_op jit(solution)/shard_map/ppermute | solution.py:477
  28.3 41.6 %all-to-all-start = ((bf16[64,64,128]{2,1,0:T(8,128)(2,1)}), bf16[64,64,128]{2,1,0:T(8,128)(2,1)S(1)}, u32[]{:S(2)}, u32[]{:S(2)}) async-start(bf16[64,64,128]{2,1,0:T(8,128)(2,1)} %bitcast.6), calls=%async_computation | async-start | bytes 2097152 | tf_op jit(solution)/shard_map/all_to_all | solution.py:540
  41.3 198.3 %all-gather.3.cloned.1.call-start = ((), (), s32[]{:S(2)}) async-start(), calls=%async_computation.7 | async-start | bytes 33177600 | tf_op jit(solution)/shard_map/all_gather | solution.py:543
  43.8 8.7 %collective-permute-start.3 = (bf16[512,256]{1,0:T(8,128)(2,1)S(1)}, bf16[512,256]{1,0:T(8,128)(2,1)S(1)}, u32[]{:S(2)}, u32[]{:S(2)}) collective-permute-start(bf16[512,256]{1,0:T(8,128)(2,1)S(1)} %get-tuple-element.38.a_ref), channel_id=1, source_target_pairs={{0,1},{1,2},{2,3},{3,0},{4,5},{5,6},{6,7},{7,4},{8,9},{9,10},{10,1... | collective-permute-start | bytes 786440 | tf_op jit(solution)/shard_map/ppermute | solution.py:477
  44.7 13.7 %collective-permute-start.4 = (bf16[512,256]{1,0:T(8,128)(2,1)S(1)}, bf16[512,256]{1,0:T(8,128)(2,1)S(1)}, u32[]{:S(2)}, u32[]{:S(2)}) collective-permute-start(bf16[512,256]{1,0:T(8,128)(2,1)S(1)} %get-tuple-element.38.a_ref), channel_id=1, source_target_pairs={{0,2},{1,3},{2,0},{3,1},{4,6},{5,7},{6,4},{7,5},{8,10},{9,11},{10,... | collective-permute-start | bytes 786440 | tf_op jit(solution)/shard_map/ppermute | solution.py:477
  46.8 11.6 %collective-permute-start.5 = (bf16[512,256]{1,0:T(8,128)(2,1)S(1)}, bf16[512,256]{1,0:T(8,128)(2,1)S(1)}, u32[]{:S(2)}, u32[]{:S(2)}) collective-permute-start(bf16[512,256]{1,0:T(8,128)(2,1)S(1)} %get-tuple-element.38.a_ref), channel_id=1, source_target_pairs={{0,3},{1,0},{2,1},{3,2},{4,7},{5,4},{6,5},{7,6},{8,11},{9,8},{10,9... | collective-permute-start | bytes 786440 | tf_op jit(solution)/shard_map/ppermute | solution.py:477
  69.9 12.4 %copy-start.9 = (s32[4096]{0:T(1024)S(1)}, s32[4096]{0:T(1024)}, u32[]{:S(2)}) copy-start(s32[4096]{0:T(1024)} %param.18) | copy-start | bytes 49156
  69.9 12.4 %copy-start.10 = (s32[4096]{0:T(1024)S(1)}, s32[4096]{0:T(1024)}, u32[]{:S(2)}) copy-start(s32[4096]{0:T(1024)} %param.20) | copy-start | bytes 49156
  74.6 1.3 copy-start.3
  75.9 6.3 %copy-start.14 = (f32[42,384]{1,0:T(8,128)S(1)}, f32[42,384]{1,0:T(8,128)}, u32[]{:S(2)}) copy-start(f32[42,384]{1,0:T(8,128)} %param.14) | copy-start | bytes 193540
  75.9 6.4 %copy-start.11 = (s32[4096]{0:T(1024)S(1)}, s32[4096]{0:T(1024)}, u32[]{:S(2)}) copy-start(s32[4096]{0:T(1024)} %param.19) | copy-start | bytes 49156
  75.9 57.6 %all-to-all-start.1 = ((bf16[64,64,256]{2,1,0:T(8,128)(2,1)}), bf16[64,64,256]{2,1,0:T(8,128)(2,1)S(1)}, u32[]{:S(2)}, u32[]{:S(2)}) async-start(bf16[64,64,256]{2,1,0:T(8,128)(2,1)} %bitcast.23), calls=%async_computation.1 | async-start | bytes 4194304 | tf_op jit(solution)/shard_map/all_to_all | solution.py:542
  82.3 1.2 copy-start.7
  101.0 1.0 copy-start.4
  133.5 34.5 %all-to-all-start.3 = ((bf16[64,64,128]{2,1,0:T(8,128)(2,1)}), bf16[64,64,128]{2,1,0:T(8,128)(2,1)S(1)}, u32[]{:S(2)}, u32[]{:S(2)}) async-start(bf16[64,64,128]{2,1,0:T(8,128)(2,1)} %bitcast.26), calls=%async_computation.3 | async-start | bytes 2097152 | tf_op jit(solution)/shard_map/all_to_all | solution.py:545
  139.3 1.2 copy-start.8
  166.7 1.3 copy-start.2
  168.0 61.8 %all-to-all-start.2 = ((bf16[64,64,256]{2,1,0:T(8,128)(2,1)}), bf16[64,64,256]{2,1,0:T(8,128)(2,1)S(1)}, u32[]{:S(2)}, u32[]{:S(2)}) async-start(bf16[64,64,256]{2,1,0:T(8,128)(2,1)} %bitcast.22), calls=%async_computation.2 | async-start | bytes 4194304 | tf_op jit(solution)/shard_map/all_to_all | solution.py:546
  178.5 56.3 %collective-permute-start.9 = (bf16[128,384]{1,0:T(8,128)(2,1)}, bf16[128,384]{1,0:T(8,128)(2,1)}, u32[]{:S(2)}, u32[]{:S(2)}) collective-permute-start(bf16[128,384]{1,0:T(8,128)(2,1)} %get-tuple-element.52), channel_id=1, source_target_pairs={{0,1},{1,2},{2,3},{3,0},{4,5},{5,6},{6,7},{7,4},{8,9},{9,10},{10,1... | collective-permute-start | bytes 294920 | tf_op jit(solution)/shard_map/ppermute | solution.py:477
  179.4 56.8 %collective-permute-start.10 = (bf16[128,384]{1,0:T(8,128)(2,1)}, bf16[128,384]{1,0:T(8,128)(2,1)}, u32[]{:S(2)}, u32[]{:S(2)}) collective-permute-start(bf16[128,384]{1,0:T(8,128)(2,1)} %get-tuple-element.53), channel_id=1, source_target_pairs={{0,2},{1,3},{2,0},{3,1},{4,6},{5,7},{6,4},{7,5},{8,10},{9,11},{10,... | collective-permute-start | bytes 294920 | tf_op jit(solution)/shard_map/ppermute | solution.py:477
  181.5 54.7 %collective-permute-start.11 = (bf16[128,384]{1,0:T(8,128)(2,1)}, bf16[128,384]{1,0:T(8,128)(2,1)}, u32[]{:S(2)}, u32[]{:S(2)}) collective-permute-start(bf16[128,384]{1,0:T(8,128)(2,1)} %get-tuple-element.54), channel_id=1, source_target_pairs={{0,3},{1,0},{2,1},{3,2},{4,7},{5,4},{6,5},{7,6},{8,11},{9,8},{10,9... | collective-permute-start | bytes 294920 | tf_op jit(solution)/shard_map/ppermute | solution.py:477
  231.8 5.3 %collective-permute-start.6 = (bf16[128,384]{1,0:T(8,128)(2,1)S(1)}, bf16[128,384]{1,0:T(8,128)(2,1)S(1)}, u32[]{:S(2)}, u32[]{:S(2)}) collective-permute-start(bf16[128,384]{1,0:T(8,128)(2,1)S(1)} %get-tuple-element.48), channel_id=1, source_target_pairs={{0,1},{1,2},{2,3},{3,0},{4,5},{5,6},{6,7},{7,4},{8,9},{9,10},{10,1... | collective-permute-start | bytes 294920 | tf_op jit(solution)/shard_map/ppermute | solution.py:477
  232.7 6.7 %collective-permute-start.7 = (bf16[128,384]{1,0:T(8,128)(2,1)S(1)}, bf16[128,384]{1,0:T(8,128)(2,1)S(1)}, u32[]{:S(2)}, u32[]{:S(2)}) collective-permute-start(bf16[128,384]{1,0:T(8,128)(2,1)S(1)} %get-tuple-element.49), channel_id=1, source_target_pairs={{0,2},{1,3},{2,0},{3,1},{4,6},{5,7},{6,4},{7,5},{8,10},{9,11},{10,... | collective-permute-start | bytes 294920 | tf_op jit(solution)/shard_map/ppermute | solution.py:477
  234.8 4.8 %collective-permute-start.8 = (bf16[128,384]{1,0:T(8,128)(2,1)S(1)}, bf16[128,384]{1,0:T(8,128)(2,1)S(1)}, u32[]{:S(2)}, u32[]{:S(2)}) collective-permute-start(bf16[128,384]{1,0:T(8,128)(2,1)S(1)} %get-tuple-element.50), channel_id=1, source_target_pairs={{0,3},{1,0},{2,1},{3,2},{4,7},{5,4},{6,5},{7,6},{8,11},{9,8},{10,9... | collective-permute-start | bytes 294920 | tf_op jit(solution)/shard_map/ppermute | solution.py:477
  239.6 23.9 %copy-start.12 = (s32[512]{0:T(512)S(1)}, s32[512]{0:T(512)}, u32[]{:S(2)}) copy-start(s32[512]{0:T(512)} %param.21) | copy-start | bytes 6148
  254.7 4.9 %collective-permute-start.12 = (bf16[128,384]{1,0:T(8,128)(2,1)S(1)}, bf16[128,384]{1,0:T(8,128)(2,1)S(1)}, u32[]{:S(2)}, u32[]{:S(2)}) collective-permute-start(bf16[128,384]{1,0:T(8,128)(2,1)S(1)} %get-tuple-element.57), channel_id=1, source_target_pairs={{0,1},{1,2},{2,3},{3,0},{4,5},{5,6},{6,7},{7,4},{8,9},{9,10},{10,1... | collective-permute-start | bytes 294920 | tf_op jit(solution)/shard_map/ppermute | solution.py:477
  256.8 5.6 %collective-permute-start.13 = (bf16[128,384]{1,0:T(8,128)(2,1)S(1)}, bf16[128,384]{1,0:T(8,128)(2,1)S(1)}, u32[]{:S(2)}, u32[]{:S(2)}) collective-permute-start(bf16[128,384]{1,0:T(8,128)(2,1)S(1)} %get-tuple-element.58), channel_id=1, source_target_pairs={{0,2},{1,3},{2,0},{3,1},{4,6},{5,7},{6,4},{7,5},{8,10},{9,11},{10,... | collective-permute-start | bytes 294920 | tf_op jit(solution)/shard_map/ppermute | solution.py:477
  258.7 4.8 %collective-permute-start.14 = (bf16[128,384]{1,0:T(8,128)(2,1)S(1)}, bf16[128,384]{1,0:T(8,128)(2,1)S(1)}, u32[]{:S(2)}, u32[]{:S(2)}) collective-permute-start(bf16[128,384]{1,0:T(8,128)(2,1)S(1)} %get-tuple-element.59), channel_id=1, source_target_pairs={{0,3},{1,0},{2,1},{3,2},{4,7},{5,4},{6,5},{7,6},{8,11},{9,8},{10,9... | collective-permute-start | bytes 294920 | tf_op jit(solution)/shard_map/ppermute | solution.py:477
  264.8 3.5 %collective-permute-start.15 = (bf16[1024,384]{1,0:T(8,128)(2,1)S(1)}, bf16[1024,384]{1,0:T(8,128)(2,1)S(1)}, u32[]{:S(2)}, u32[]{:S(2)}) collective-permute-start(bf16[1024,384]{1,0:T(8,128)(2,1)S(1)} %get-tuple-element.61), channel_id=1, source_target_pairs={{0,4},{4,0},{1,5},{5,1},{2,6},{6,2},{3,7},{7,3},{8,12},{12,8},{9,1... | collective-permute-start | bytes 2359304 | tf_op jit(solution)/shard_map/ppermute | solution.py:477
  268.5 6.2 %collective-permute-start.18 = (bf16[256,384]{1,0:T(8,128)(2,1)S(1)}, bf16[256,384]{1,0:T(8,128)(2,1)S(1)}, u32[]{:S(2)}, u32[]{:S(2)}) collective-permute-start(bf16[256,384]{1,0:T(8,128)(2,1)S(1)} %get-tuple-element.65), channel_id=1, source_target_pairs={{0,192},{64,0},{128,64},{192,128},{1,193},{65,1},{129,65},{193,129... | collective-permute-start | bytes 589832 | tf_op jit(solution)/shard_map/ppermute | solution.py:477
  270.1 7.3 %collective-permute-start.17 = (bf16[256,384]{1,0:T(8,128)(2,1)S(1)}, bf16[256,384]{1,0:T(8,128)(2,1)S(1)}, u32[]{:S(2)}, u32[]{:S(2)}) collective-permute-start(bf16[256,384]{1,0:T(8,128)(2,1)S(1)} %get-tuple-element.64), channel_id=1, source_target_pairs={{0,128},{64,192},{128,0},{192,64},{1,129},{65,193},{129,1},{193,65... | collective-permute-start | bytes 589832 | tf_op jit(solution)/shard_map/ppermute | solution.py:477
  271.2 11.4 %collective-permute-start.16 = (bf16[256,384]{1,0:T(8,128)(2,1)S(1)}, bf16[256,384]{1,0:T(8,128)(2,1)S(1)}, u32[]{:S(2)}, u32[]{:S(2)}) collective-permute-start(bf16[256,384]{1,0:T(8,128)(2,1)S(1)} %get-tuple-element.63), channel_id=1, source_target_pairs={{0,64},{64,128},{128,192},{192,0},{1,65},{65,129},{129,193},{193,1... | collective-permute-start | bytes 589832 | tf_op jit(solution)/shard_map/ppermute | solution.py:477
  282.6 43.0 %copy-start.1 = (bf16[384,384]{1,0:T(8,128)(2,1)S(1)}, bf16[384,384]{1,0:T(8,128)(2,1)}, u32[]{:S(2)}) copy-start(bf16[384,384]{1,0:T(8,128)(2,1)} %param.15) | copy-start | bytes 884740
  294.4 31.2 %copy-start.13 = (bf16[32,384]{1,0:T(8,128)(2,1)}, bf16[32,384]{1,0:T(8,128)(2,1)S(1)}, u32[]{:S(2)}) copy-start(bf16[32,384]{1,0:T(8,128)(2,1)S(1)} %multiply_convert_fusion) | copy-start | bytes 73732
  317.4 6.0 %collective-permute-start.19 = (bf16[1024,384]{1,0:T(8,128)(2,1)S(1)}, bf16[1024,384]{1,0:T(8,128)(2,1)S(1)}, u32[]{:S(2)}, u32[]{:S(2)}) collective-permute-start(bf16[1024,384]{1,0:T(8,128)(2,1)S(1)} %bitcast.27), channel_id=1, source_target_pairs={{0,4},{4,0},{1,5},{5,1},{2,6},{6,2},{3,7},{7,3},{8,12},{12,8},{9,1... | collective-permute-start | bytes 2359304 | tf_op jit(solution)/shard_map/ppermute | solution.py:477
Sparse Core Ops, SparseCore 0:
  70.0 142.2 all-gather.2

commit v4 on v3

--- a/solution.py
+++ b/solution.py
@@ -28,7 +28,7 @@
 UP_HALF = TRIP // N_CORE
 ATOMS = ATOM_DEV * N_GRAPH
 HALF_ATOMS = ATOMS // N_CORE
-BLOCK = 512
+ATOM_BLOCK = 256
 PARTS = ((0, 128), (128, 384))
 
 F32 = jnp.float32
@@ -107,7 +107,7 @@
         in_specs=[SCALAR, whole((EDGE_DEV, COLS)), whole((COLS, TRIP))],
         out_specs=[whole((EDGE_DEV, w)) for w in widths] + [whole((ROWS, COLS))] * N_MP,
         out_shape=[shape_of(EDGE_DEV, w) for w in widths] + [shape_of(ROWS, COLS)] * N_MP,
-        compiler_params=params(24),
+        compiler_params=params(62),
         name="project",
         cost_estimate=pl.CostEstimate(
             flops=2 * EDGE_DEV * COLS * TRIP, bytes_accessed=1500000, transcendentals=0
@@ -125,7 +125,7 @@
     out_ref[...] = product(picks(list_ref[...], EDGE_DEV), table[...]).astype(BF16)
 
 
-SEND_BLOCK = 256
+SEND_BLOCK = 1024
 
 
 def send(lists, partials):
@@ -329,7 +329,7 @@
             inner[:, columns(side + j)] = silu(product(x, weight_ref[j])).astype(BF16)
             return carry
 
-        lax.fori_loop(0, SIDE, one, 0)
+        lax.fori_loop(0, SIDE, one, 0, unroll=True)
 
     @pl.when(lax.rem(which, 2) == 1)
     def _():
@@ -342,7 +342,7 @@
             given[:, at] = fresh.astype(BF16)
             return carry
 
-        lax.fori_loop(0, SIDE, one, 0)
+        lax.fori_loop(0, SIDE, one, 0, unroll=True)
 
     @pl.when(step == MAPS * MAP_STEPS - 1)
     def _():
@@ -398,9 +398,14 @@
     spot = (group // N_CORE) * ATOM_DEV + row % ATOM_DEV
     for out_ref, owner in ((keep_ref, core), (give_ref, 1 - core)):
         mine = jnp.where(group % N_CORE == owner, spot, -1)
-        for first in range(0, HALF_ATOMS, BLOCK):
-            part = product(members(mine, BLOCK, first), hidden)
-            out_ref[first : first + BLOCK, :] = part.astype(BF16)
+
+        def one(i, carry):
+            first = pl.multiple_of(i * ATOM_BLOCK, ATOM_BLOCK)
+            part = product(members(mine, ATOM_BLOCK, first), hidden)
+            out_ref[pl.ds(first, ATOM_BLOCK), :] = part.astype(BF16)
+            return carry
+
+        lax.fori_loop(0, HALF_ATOMS // ATOM_BLOCK, one, 0)
 
 
 def atoms(mp, core, edge_atom, hiddens):
@@ -538,8 +543,9 @@
     first, second = lax.optimization_barrier((first, second))
     partials = turned([second] * N_MP, "mp")
     first = exchange(first)
-    first, half, *partials = lax.optimization_barrier((first, half, *partials))
-    second = exchange(send(lists, partials).reshape(N_GRAPH, CAP, -1))
+    second = send(lists, partials).reshape(N_GRAPH, CAP, -1)
+    first, second, half = lax.optimization_barrier((first, second, half))
+    second = exchange(second)
     gathered = lax.all_gather(half, ("graph_2", "mp"), axis=0, tiled=False)
     states = turned(state_blocks, "mp")
     first = exchange(sums(first, PARTS[0]))

time: 333 us -> 322 us (0.967)
  Pallas kernels: 79.6 us -> 74 us
  waiting for transfers between devices: 123 us -> 119 us
    pallas_call x2, Pallas kernels: 12.3 us -> 6.14 us  [send(): pl.pallas_call(send_kernel, grid=(SLOTS // SEND_BLOCK,), in_specs=[pl.Blo...]
  transfers between devices with their start and end apart: 25 -> 25, of which waited for: 18 -> 17; matrix products, arithmetic and copies ran while one was open for 2% -> 2% of each run, Pallas kernels for 14% -> 15%
where the time goes in v4:
time: 322 us; the launch traced here: 321 us
  waiting for transfers between devices  119 us (37%)
  Pallas kernels  74 us (23%)
  starting transfers between devices  67.7 us (21%)
  blocking collectives  34.5 us (11%)
  between operations  14.4 us (4%)
  local copies, waits for them, and re-layouts  8.85 us (3%)
    all_to_all x1, waiting for transfers between devices, local(): second = exchange(sums(second, PARTS[1]))  44.9 us
    pallas_call x2, Pallas kernels, triplets(): pl.pallas_call(functools.partial(triplet_kernel, groups), grid=(TRIP_STEP...  43.6 us
    ppermute x20, waiting for transfers between devices, turn(): lax.ppermute(array, axis, [(i, (i + shift) % count) for i in range(count)])  34.9 us
    ppermute x20, starting transfers between devices, turn(): lax.ppermute(array, axis, [(i, (i + shift) % count) for i in range(count)])  32.2 us
    all_to_all x1, waiting for transfers between devices, local(): second = exchange(second)  31.6 us
    pallas_call x1, Pallas kernels, layers(): pl.pallas_call(layers_kernel, grid=(MAPS * MAP_STEPS,), in_specs=[SCALAR]...  13.2 us
    all_to_all x1, starting transfers between devices, local(): first = exchange(first)  13 us
    all_to_all x1, blocking collectives, local(): atom_sum = summed(lax.all_to_all(part, 'graph_1', 0, 0, tiled=True))  11.7 us
  transfers between devices with their start and end apart: 25, of which 17 were waited for; matrix products, arithmetic and copies ran while one was open for 2% of the time, Pallas kernels for 15%

profile of v4, /device:TPU:1, one launch (start us, length us, event | category | flops | bytes accessed | tf_op | source)
XLA Modules:
  0.0 321.3 jit_solution(17098351896122649732)
XLA Ops:
  7.2 2.3 project.1
  9.5 2.1 collective-permute-start
  11.6 2.6 collective-permute-start.1
  14.2 1.1 collective-permute-start.2
  15.3 0.8 reshape.63.list_ref
  16.2 4.0 %collective-permute-done.1.c_ref = bf16[512,128]{1,0:T(8,128)(2,1)S(1)} collective-permute-done((bf16[512,128]{1,0:T(8,128)(2,1)}, bf16[512,128]{1,0:T(8,128)(2,1)S(1)}, u32[]{:S(2)}, u32[]{:S(2)}) %collective-permute-start.1) | collective-permute-done | bytes 131104 | tf_op jit(solution)/shard_map/ppermute | solution.py:482
  20.2 0.9 copy-done.8
  21.1 2.9 send.2
  24.0 13.0 %all-to-all-start = ((bf16[64,64,128]{2,1,0:T(8,128)(2,1)}), bf16[64,64,128]{2,1,0:T(8,128)(2,1)S(1)}, u32[]{:S(2)}, u32[]{:S(2)}) async-start(bf16[64,64,128]{2,1,0:T(8,128)(2,1)} %bitcast.6), calls=%async_computation | async-start | bytes 2097152 | tf_op jit(solution)/shard_map/all_to_all | solution.py:545
  37.2 2.4 constant_dynamic-slice_fusion.1
  39.6 1.0 collective-permute-start.3
  40.6 2.1 collective-permute-start.4
  42.7 1.3 collective-permute-start.5
  44.0 2.2 pad_maximum_fusion
  46.2 2.1 collective-permute-done.3.b_ref
  48.3 6.0 %collective-permute-done.4.c_ref = bf16[512,256]{1,0:T(8,128)(2,1)S(1)} collective-permute-done((bf16[512,256]{1,0:T(8,128)(2,1)S(1)}, bf16[512,256]{1,0:T(8,128)(2,1)S(1)}, u32[]{:S(2)}, u32[]{:S(2)}) %collective-permute-start.4) | collective-permute-done | bytes 262176 | tf_op jit(solution)/shard_map/ppermute | solution.py:482
  54.3 3.2 send.3
  57.5 8.1 %all-to-all-done = bf16[64,64,128]{2,1,0:T(8,128)(2,1)S(1)} async-done(((bf16[64,64,128]{2,1,0:T(8,128)(2,1)}), bf16[64,64,128]{2,1,0:T(8,128)(2,1)S(1)}, u32[]{:S(2)}, u32[]{:S(2)}) %all-to-all-start) | async-done | bytes 1048608 | tf_op jit(solution)/shard_map/all_to_all | solution.py:545
  65.6 6.3 %all-to-all-start.1 = ((bf16[64,64,256]{2,1,0:T(8,128)(2,1)}), bf16[64,64,256]{2,1,0:T(8,128)(2,1)S(1)}, u32[]{:S(2)}, u32[]{:S(2)}) async-start(bf16[64,64,256]{2,1,0:T(8,128)(2,1)} %bitcast.7), calls=%async_computation.1 | async-start | bytes 4194304 | tf_op jit(solution)/shard_map/all_to_all | solution.py:548
  72.1 1.1 copy-done.5
  73.2 17.4 %triplets.3 = bf16[4,1024,128]{2,1,0:T(8,128)(2,1)S(1)} custom-call(s32[1,4096]{1,0:T(1,128)S(1)} %bitcast.28, s32[1,4096]{1,0:T(1,128)S(1)} %bitcast.30, s32[1,4096]{1,0:T(1,128)S(1)} %bitcast.32, f32[42,4096]{1,0:T(8,128)S(1)} %copy-done.5, bf16[144,128]{1,0:T(8,128)(2,1)S(1)} %slice.9.weight_ref, bf16[4096,128]{1,0:T(8,128)(2,1)S(1)} %bitcast.23), custom_call_target="tpu_custom_call" | custom-call | flops 8589934592 | bytes 2304000 | tf_op jit(solution)/shard_map/triplets/pallas_call | solution.py:214
  90.7 1.0 copy-done.3
  91.7 31.6 %all-to-all-done.1 = bf16[64,64,256]{2,1,0:T(8,128)(2,1)S(1)} async-done(((bf16[64,64,256]{2,1,0:T(8,128)(2,1)}), bf16[64,64,256]{2,1,0:T(8,128)(2,1)S(1)}, u32[]{:S(2)}, u32[]{:S(2)}) %all-to-all-start.1) | async-done | bytes 2097184 | tf_op jit(solution)/shard_map/all_to_all | solution.py:548
  123.2 5.8 %all-to-all-start.3 = ((bf16[64,64,128]{2,1,0:T(8,128)(2,1)}), bf16[64,64,128]{2,1,0:T(8,128)(2,1)S(1)}, u32[]{:S(2)}, u32[]{:S(2)}) async-start(bf16[64,64,128]{2,1,0:T(8,128)(2,1)} %bitcast.25), calls=%async_computation.3 | async-start | bytes 2097152 | tf_op jit(solution)/shard_map/all_to_all | solution.py:551
  129.1 1.1 copy-done.6
  130.2 26.2 %triplets.2 = bf16[2,2048,256]{2,1,0:T(8,128)(2,1)S(1)} custom-call(s32[1,4096]{1,0:T(1,128)S(1)} %bitcast.29, s32[1,4096]{1,0:T(1,128)S(1)} %bitcast.31, s32[1,4096]{1,0:T(1,128)S(1)} %bitcast.33, f32[42,4096]{1,0:T(8,128)S(1)} %copy-done.6, bf16[144,256]{1,0:T(8,128)(2,1)S(1)} %slice.8.weight_ref, bf16[4096,256]{1,0:T(8,128)(2,1)S(1)} %bitcast.21), custom_call_target="tpu_custom_call" | custom-call | flops 17179869184 | bytes 4608000 | tf_op jit(solution)/shard_map/triplets/pallas_call | solution.py:214
  156.4 1.3 copy-done.2
  157.7 10.3 %all-to-all-start.2 = ((bf16[64,64,256]{2,1,0:T(8,128)(2,1)}), bf16[64,64,256]{2,1,0:T(8,128)(2,1)S(1)}, u32[]{:S(2)}, u32[]{:S(2)}) async-start(bf16[64,64,256]{2,1,0:T(8,128)(2,1)} %bitcast.22), calls=%async_computation.2 | async-start | bytes 4194304 | tf_op jit(solution)/shard_map/all_to_all | solution.py:552
  168.0 1.0 collective-permute-start.9
  169.1 2.1 collective-permute-start.10
  171.2 1.3 collective-permute-start.11
  172.5 1.9 edges.2
  174.4 44.9 %all-to-all-done.2 = bf16[64,64,256]{2,1,0:T(8,128)(2,1)S(1)} async-done(((bf16[64,64,256]{2,1,0:T(8,128)(2,1)}), bf16[64,64,256]{2,1,0:T(8,128)(2,1)S(1)}, u32[]{:S(2)}, u32[]{:S(2)}) %all-to-all-start.2) | async-done | bytes 2097184 | tf_op jit(solution)/shard_map/all_to_all | solution.py:552
  219.3 2.0 edges.3
  221.3 1.0 collective-permute-start.6
  222.3 2.1 collective-permute-start.7
  224.5 1.3 collective-permute-start.8
  225.8 0.8 collective-permute-done.6.refs_1_
  226.6 2.5 collective-permute-done.7.refs_2_
  229.1 0.2 collective-permute-done.8.refs_3_
  229.3 13.2 %layers.1 = (bf16[128,384]{1,0:T(8,128)(2,1)S(1)}, bf16[128,384]{1,0:T(8,128)(2,1)S(1)}, bf16[128,384]{1,0:T(8,128)(2,1)S(1)}, bf16[128,384]{1,0:T(8,128)(2,1)S(1)}) custom-call(s32[1]{0:T(128)} %bitcast.mp_ref, bf16[128,384]{1,0:T(8,128)(2,1)S(1)} %get-tuple-element.41.refs_0_, bf16[128,384]{1,0:T(8,128)(2,1)S(1)} %collective-permute-done.6.refs_1_, ...), custom_call_target="tpu_custom_call" | custom-call | flops 3623878656 | bytes 28311552 | tf_op jit(solution)/shard_map/layers/pallas_call | solution.py:359
  242.4 2.1 collective-permute-start.12
  244.5 1.8 collective-permute-start.13
  246.3 0.7 collective-permute-start.14
  247.0 0.2 collective-permute-done.12.h1
  247.2 2.9 collective-permute-done.13.h2
  250.1 1.0 collective-permute-done.14.h3
  251.1 2.4 atoms.1
  253.5 1.6 collective-permute-start.15
  255.2 1.9 collective-permute-done.15.got_ref
  257.1 0.2 meet.1
  257.3 1.6 collective-permute-start.18
  258.9 1.2 collective-permute-start.17
  260.1 3.4 %collective-permute-done.18 = bf16[256,384]{1,0:T(8,128)(2,1)S(1)} collective-permute-done((bf16[256,384]{1,0:T(8,128)(2,1)S(1)}, bf16[256,384]{1,0:T(8,128)(2,1)S(1)}, u32[]{:S(2)}, u32[]{:S(2)}) %collective-permute-start.18) | collective-permute-done | bytes 196640 | tf_op jit(solution)/shard_map/ppermute | solution.py:482
  263.5 2.8 collective-permute-done.17
  266.2 5.2 %collective-permute-done.16 = bf16[256,384]{1,0:T(8,128)(2,1)S(1)} collective-permute-done((bf16[256,384]{1,0:T(8,128)(2,1)S(1)}, bf16[256,384]{1,0:T(8,128)(2,1)S(1)}, u32[]{:S(2)}, u32[]{:S(2)}) %collective-permute-start.16) | collective-permute-done | bytes 196640 | tf_op jit(solution)/shard_map/ppermute | solution.py:482
  271.4 0.1 add_convert_fusion
  271.6 11.7 %all_to_all.35 = bf16[8,32,384]{2,1,0:T(8,128)(2,1)S(1)} all-to-all(bf16[8,32,384]{2,1,0:T(8,128)(2,1)S(1)} %bitcast.39), channel_id=1, replica_groups=mesh['graph_0'=4,'graph_1'=8,'graph_2'=2,'mp'=4] {'graph_1'}, dimensions={0} | all-to-all | bytes 393216 | tf_op jit(solution)/shard_map/all_to_all | solution.py:564
  283.3 11.3 %all_to_all.36 = bf16[8,32,384]{2,1,0:T(8,128)(2,1)S(1)} all-to-all(bf16[8,32,384]{2,1,0:T(8,128)(2,1)S(1)} %broadcast_in_dim.25), channel_id=1, replica_groups=mesh['graph_0'=4,'graph_1'=8,'graph_2'=2,'mp'=4] {'graph_1'}, dimensions={0} | all-to-all | bytes 393216 | tf_op jit(solution)/shard_map/all_to_all | solution.py:566
  294.6 0.1 broadcast_in_dim.27
  294.7 11.6 %all_to_all.37 = bf16[4,256,384]{2,1,0:T(8,128)(2,1)S(1)} all-to-all(bf16[4,256,384]{2,1,0:T(8,128)(2,1)S(1)} %broadcast_in_dim.27), channel_id=1, replica_groups=mesh['graph_0'=4,'graph_1'=8,'graph_2'=2,'mp'=4] {'graph_0'}, dimensions={0} | all-to-all | bytes 1572864 | tf_op jit(solution)/shard_map/all_to_all | solution.py:569
  306.3 4.1 %collective-permute-start.19 = (bf16[1024,384]{1,0:T(8,128)(2,1)S(1)}, bf16[1024,384]{1,0:T(8,128)(2,1)S(1)}, u32[]{:S(2)}, u32[]{:S(2)}) collective-permute-start(bf16[1024,384]{1,0:T(8,128)(2,1)S(1)} %bitcast.26), channel_id=1, source_target_pairs={{0,4},{4,0},{1,5},{5,1},{2,6},{6,2},{3,7},{7,3},{8,12},{12,8},{9,1... | collective-permute-start | bytes 2359304 | tf_op jit(solution)/shard_map/ppermute | solution.py:482
  310.3 1.9 collective-permute-done.19.other_ref
  312.2 2.2 final.1
  (45 shorter events, 0.3 us)
Async XLA Ops:
  7.2 29.9 %copy-start = (bf16[384,384]{1,0:T(8,128)(2,1)S(1)}, bf16[384,384]{1,0:T(8,128)(2,1)}, u32[]{:S(2)}) copy-start(bf16[384,384]{1,0:T(8,128)(2,1)} %param.15) | copy-start | bytes 884740
  9.5 6.7 %collective-permute-start = (bf16[512,128]{1,0:T(8,128)(2,1)}, bf16[512,128]{1,0:T(8,128)(2,1)S(1)}, u32[]{:S(2)}, u32[]{:S(2)}) collective-permute-start(bf16[512,128]{1,0:T(8,128)(2,1)} %get-tuple-element.31.a_ref), channel_id=1, source_target_pairs={{0,1},{1,2},{2,3},{3,0},{4,5},{5,6},{6,7},{7,4},{8,9},{9,10},{10,1... | collective-permute-start | bytes 393224 | tf_op jit(solution)/shard_map/ppermute | solution.py:482
  11.6 8.5 %collective-permute-start.1 = (bf16[512,128]{1,0:T(8,128)(2,1)}, bf16[512,128]{1,0:T(8,128)(2,1)S(1)}, u32[]{:S(2)}, u32[]{:S(2)}) collective-permute-start(bf16[512,128]{1,0:T(8,128)(2,1)} %get-tuple-element.31.a_ref), channel_id=1, source_target_pairs={{0,2},{1,3},{2,0},{3,1},{4,6},{5,7},{6,4},{7,5},{8,10},{9,11},{10,... | collective-permute-start | bytes 393224 | tf_op jit(solution)/shard_map/ppermute | solution.py:482
  14.2 5.9 %collective-permute-start.2 = (bf16[512,128]{1,0:T(8,128)(2,1)}, bf16[512,128]{1,0:T(8,128)(2,1)S(1)}, u32[]{:S(2)}, u32[]{:S(2)}) collective-permute-start(bf16[512,128]{1,0:T(8,128)(2,1)} %get-tuple-element.31.a_ref), channel_id=1, source_target_pairs={{0,3},{1,0},{2,1},{3,2},{4,7},{5,4},{6,5},{7,6},{8,11},{9,8},{10,9... | collective-permute-start | bytes 393224 | tf_op jit(solution)/shard_map/ppermute | solution.py:482
  20.2 0.9 copy-start.8
  24.0 41.6 %all-to-all-start = ((bf16[64,64,128]{2,1,0:T(8,128)(2,1)}), bf16[64,64,128]{2,1,0:T(8,128)(2,1)S(1)}, u32[]{:S(2)}, u32[]{:S(2)}) async-start(bf16[64,64,128]{2,1,0:T(8,128)(2,1)} %bitcast.6), calls=%async_computation | async-start | bytes 2097152 | tf_op jit(solution)/shard_map/all_to_all | solution.py:545
  37.0 192.2 %all-gather.3.cloned.1.call-start = ((), (), s32[]{:S(2)}) async-start(), calls=%async_computation.7 | async-start | bytes 33177600 | tf_op jit(solution)/shard_map/all_gather | solution.py:549
  37.1 2.4 copy-start.7
  39.6 8.7 %collective-permute-start.3 = (bf16[512,256]{1,0:T(8,128)(2,1)S(1)}, bf16[512,256]{1,0:T(8,128)(2,1)S(1)}, u32[]{:S(2)}, u32[]{:S(2)}) collective-permute-start(bf16[512,256]{1,0:T(8,128)(2,1)S(1)} %copy-done.7), channel_id=1, source_target_pairs={{0,1},{1,2},{2,3},{3,0},{4,5},{5,6},{6,7},{7,4},{8,9},{9,10},{10,1... | collective-permute-start | bytes 786440 | tf_op jit(solution)/shard_map/ppermute | solution.py:482
  40.6 13.7 %collective-permute-start.4 = (bf16[512,256]{1,0:T(8,128)(2,1)S(1)}, bf16[512,256]{1,0:T(8,128)(2,1)S(1)}, u32[]{:S(2)}, u32[]{:S(2)}) collective-permute-start(bf16[512,256]{1,0:T(8,128)(2,1)S(1)} %copy-done.7), channel_id=1, source_target_pairs={{0,2},{1,3},{2,0},{3,1},{4,6},{5,7},{6,4},{7,5},{8,10},{9,11},{10,... | collective-permute-start | bytes 786440 | tf_op jit(solution)/shard_map/ppermute | solution.py:482
  42.7 11.6 %collective-permute-start.5 = (bf16[512,256]{1,0:T(8,128)(2,1)S(1)}, bf16[512,256]{1,0:T(8,128)(2,1)S(1)}, u32[]{:S(2)}, u32[]{:S(2)}) collective-permute-start(bf16[512,256]{1,0:T(8,128)(2,1)S(1)} %copy-done.7), channel_id=1, source_target_pairs={{0,3},{1,0},{2,1},{3,2},{4,7},{5,4},{6,5},{7,6},{8,11},{9,8},{10,9... | collective-permute-start | bytes 786440 | tf_op jit(solution)/shard_map/ppermute | solution.py:482
  65.6 6.4 %copy-start.14 = (f32[42,384]{1,0:T(8,128)S(1)}, f32[42,384]{1,0:T(8,128)}, u32[]{:S(2)}) copy-start(f32[42,384]{1,0:T(8,128)} %param.14) | copy-start | bytes 193540
  65.6 6.5 %copy-start.9 = (s32[4096]{0:T(1024)S(1)}, s32[4096]{0:T(1024)}, u32[]{:S(2)}) copy-start(s32[4096]{0:T(1024)} %param.18) | copy-start | bytes 49156
  65.6 6.5 %copy-start.10 = (s32[4096]{0:T(1024)S(1)}, s32[4096]{0:T(1024)}, u32[]{:S(2)}) copy-start(s32[4096]{0:T(1024)} %param.20) | copy-start | bytes 49156
  65.6 6.5 %copy-start.11 = (s32[4096]{0:T(1024)S(1)}, s32[4096]{0:T(1024)}, u32[]{:S(2)}) copy-start(s32[4096]{0:T(1024)} %param.19) | copy-start | bytes 49156
  65.6 57.6 %all-to-all-start.1 = ((bf16[64,64,256]{2,1,0:T(8,128)(2,1)}), bf16[64,64,256]{2,1,0:T(8,128)(2,1)S(1)}, u32[]{:S(2)}, u32[]{:S(2)}) async-start(bf16[64,64,256]{2,1,0:T(8,128)(2,1)} %bitcast.7), calls=%async_computation.1 | async-start | bytes 4194304 | tf_op jit(solution)/shard_map/all_to_all | solution.py:548
  72.1 1.1 copy-start.5
  90.7 1.0 copy-start.3
  123.2 34.5 %all-to-all-start.3 = ((bf16[64,64,128]{2,1,0:T(8,128)(2,1)}), bf16[64,64,128]{2,1,0:T(8,128)(2,1)S(1)}, u32[]{:S(2)}, u32[]{:S(2)}) async-start(bf16[64,64,128]{2,1,0:T(8,128)(2,1)} %bitcast.25), calls=%async_computation.3 | async-start | bytes 2097152 | tf_op jit(solution)/shard_map/all_to_all | solution.py:551
  129.1 1.1 copy-start.6
  156.4 1.3 copy-start.2
  157.7 61.6 %all-to-all-start.2 = ((bf16[64,64,256]{2,1,0:T(8,128)(2,1)}), bf16[64,64,256]{2,1,0:T(8,128)(2,1)S(1)}, u32[]{:S(2)}, u32[]{:S(2)}) async-start(bf16[64,64,256]{2,1,0:T(8,128)(2,1)} %bitcast.22), calls=%async_computation.2 | async-start | bytes 4194304 | tf_op jit(solution)/shard_map/all_to_all | solution.py:552
  168.0 61.2 %copy-start.4 = (bf16[128,384]{1,0:T(8,128)(2,1)S(1)}, bf16[128,384]{1,0:T(8,128)(2,1)}, u32[]{:S(2)}) copy-start(bf16[128,384]{1,0:T(8,128)(2,1)} %get-tuple-element.45.refs_4_) | copy-start | bytes 294916
  168.0 56.4 %collective-permute-start.9 = (bf16[128,384]{1,0:T(8,128)(2,1)}, bf16[128,384]{1,0:T(8,128)(2,1)}, u32[]{:S(2)}, u32[]{:S(2)}) collective-permute-start(bf16[128,384]{1,0:T(8,128)(2,1)} %get-tuple-element.46), channel_id=1, source_target_pairs={{0,1},{1,2},{2,3},{3,0},{4,5},{5,6},{6,7},{7,4},{8,9},{9,10},{10,1... | collective-permute-start | bytes 294920 | tf_op jit(solution)/shard_map/ppermute | solution.py:482
  169.1 56.7 %collective-permute-start.10 = (bf16[128,384]{1,0:T(8,128)(2,1)}, bf16[128,384]{1,0:T(8,128)(2,1)}, u32[]{:S(2)}, u32[]{:S(2)}) collective-permute-start(bf16[128,384]{1,0:T(8,128)(2,1)} %get-tuple-element.47), channel_id=1, source_target_pairs={{0,2},{1,3},{2,0},{3,1},{4,6},{5,7},{6,4},{7,5},{8,10},{9,11},{10,... | collective-permute-start | bytes 294920 | tf_op jit(solution)/shard_map/ppermute | solution.py:482
  171.2 54.6 %collective-permute-start.11 = (bf16[128,384]{1,0:T(8,128)(2,1)}, bf16[128,384]{1,0:T(8,128)(2,1)}, u32[]{:S(2)}, u32[]{:S(2)}) collective-permute-start(bf16[128,384]{1,0:T(8,128)(2,1)} %get-tuple-element.48), channel_id=1, source_target_pairs={{0,3},{1,0},{2,1},{3,2},{4,7},{5,4},{6,5},{7,6},{8,11},{9,8},{10,9... | collective-permute-start | bytes 294920 | tf_op jit(solution)/shard_map/ppermute | solution.py:482
  221.3 5.3 %collective-permute-start.6 = (bf16[128,384]{1,0:T(8,128)(2,1)S(1)}, bf16[128,384]{1,0:T(8,128)(2,1)S(1)}, u32[]{:S(2)}, u32[]{:S(2)}) collective-permute-start(bf16[128,384]{1,0:T(8,128)(2,1)S(1)} %get-tuple-element.42), channel_id=1, source_target_pairs={{0,1},{1,2},{2,3},{3,0},{4,5},{5,6},{6,7},{7,4},{8,9},{9,10},{10,1... | collective-permute-start | bytes 294920 | tf_op jit(solution)/shard_map/ppermute | solution.py:482
  222.3 6.7 %collective-permute-start.7 = (bf16[128,384]{1,0:T(8,128)(2,1)S(1)}, bf16[128,384]{1,0:T(8,128)(2,1)S(1)}, u32[]{:S(2)}, u32[]{:S(2)}) collective-permute-start(bf16[128,384]{1,0:T(8,128)(2,1)S(1)} %get-tuple-element.43), channel_id=1, source_target_pairs={{0,2},{1,3},{2,0},{3,1},{4,6},{5,7},{6,4},{7,5},{8,10},{9,11},{10,... | collective-permute-start | bytes 294920 | tf_op jit(solution)/shard_map/ppermute | solution.py:482
  224.5 4.8 %collective-permute-start.8 = (bf16[128,384]{1,0:T(8,128)(2,1)S(1)}, bf16[128,384]{1,0:T(8,128)(2,1)S(1)}, u32[]{:S(2)}, u32[]{:S(2)}) collective-permute-start(bf16[128,384]{1,0:T(8,128)(2,1)S(1)} %get-tuple-element.44), channel_id=1, source_target_pairs={{0,3},{1,0},{2,1},{3,2},{4,7},{5,4},{6,5},{7,6},{8,11},{9,8},{10,9... | collective-permute-start | bytes 294920 | tf_op jit(solution)/shard_map/ppermute | solution.py:482
  229.3 21.8 %copy-start.12 = (s32[512]{0:T(512)S(1)}, s32[512]{0:T(512)}, u32[]{:S(2)}) copy-start(s32[512]{0:T(512)} %param.21) | copy-start | bytes 6148
  242.4 4.8 %collective-permute-start.12 = (bf16[128,384]{1,0:T(8,128)(2,1)S(1)}, bf16[128,384]{1,0:T(8,128)(2,1)S(1)}, u32[]{:S(2)}, u32[]{:S(2)}) collective-permute-start(bf16[128,384]{1,0:T(8,128)(2,1)S(1)} %get-tuple-element.51), channel_id=1, source_target_pairs={{0,1},{1,2},{2,3},{3,0},{4,5},{5,6},{6,7},{7,4},{8,9},{9,10},{10,1... | collective-permute-start | bytes 294920 | tf_op jit(solution)/shard_map/ppermute | solution.py:482
  244.5 5.6 %collective-permute-start.13 = (bf16[128,384]{1,0:T(8,128)(2,1)S(1)}, bf16[128,384]{1,0:T(8,128)(2,1)S(1)}, u32[]{:S(2)}, u32[]{:S(2)}) collective-permute-start(bf16[128,384]{1,0:T(8,128)(2,1)S(1)} %get-tuple-element.52), channel_id=1, source_target_pairs={{0,2},{1,3},{2,0},{3,1},{4,6},{5,7},{6,4},{7,5},{8,10},{9,11},{10,... | collective-permute-start | bytes 294920 | tf_op jit(solution)/shard_map/ppermute | solution.py:482
  246.3 4.8 %collective-permute-start.14 = (bf16[128,384]{1,0:T(8,128)(2,1)S(1)}, bf16[128,384]{1,0:T(8,128)(2,1)S(1)}, u32[]{:S(2)}, u32[]{:S(2)}) collective-permute-start(bf16[128,384]{1,0:T(8,128)(2,1)S(1)} %get-tuple-element.53), channel_id=1, source_target_pairs={{0,3},{1,0},{2,1},{3,2},{4,7},{5,4},{6,5},{7,6},{8,11},{9,8},{10,9... | collective-permute-start | bytes 294920 | tf_op jit(solution)/shard_map/ppermute | solution.py:482
  253.5 3.6 %collective-permute-start.15 = (bf16[1024,384]{1,0:T(8,128)(2,1)S(1)}, bf16[1024,384]{1,0:T(8,128)(2,1)S(1)}, u32[]{:S(2)}, u32[]{:S(2)}) collective-permute-start(bf16[1024,384]{1,0:T(8,128)(2,1)S(1)} %get-tuple-element.55), channel_id=1, source_target_pairs={{0,4},{4,0},{1,5},{5,1},{2,6},{6,2},{3,7},{7,3},{8,12},{12,8},{9,1... | collective-permute-start | bytes 2359304 | tf_op jit(solution)/shard_map/ppermute | solution.py:482
  257.3 6.2 %collective-permute-start.18 = (bf16[256,384]{1,0:T(8,128)(2,1)S(1)}, bf16[256,384]{1,0:T(8,128)(2,1)S(1)}, u32[]{:S(2)}, u32[]{:S(2)}) collective-permute-start(bf16[256,384]{1,0:T(8,128)(2,1)S(1)} %get-tuple-element.59), channel_id=1, source_target_pairs={{0,192},{64,0},{128,64},{192,128},{1,193},{65,1},{129,65},{193,129... | collective-permute-start | bytes 589832 | tf_op jit(solution)/shard_map/ppermute | solution.py:482
  258.9 7.3 %collective-permute-start.17 = (bf16[256,384]{1,0:T(8,128)(2,1)S(1)}, bf16[256,384]{1,0:T(8,128)(2,1)S(1)}, u32[]{:S(2)}, u32[]{:S(2)}) collective-permute-start(bf16[256,384]{1,0:T(8,128)(2,1)S(1)} %get-tuple-element.58), channel_id=1, source_target_pairs={{0,128},{64,192},{128,0},{192,64},{1,129},{65,193},{129,1},{193,65... | collective-permute-start | bytes 589832 | tf_op jit(solution)/shard_map/ppermute | solution.py:482
  260.1 11.4 %collective-permute-start.16 = (bf16[256,384]{1,0:T(8,128)(2,1)S(1)}, bf16[256,384]{1,0:T(8,128)(2,1)S(1)}, u32[]{:S(2)}, u32[]{:S(2)}) collective-permute-start(bf16[256,384]{1,0:T(8,128)(2,1)S(1)} %get-tuple-element.57), channel_id=1, source_target_pairs={{0,64},{64,128},{128,192},{192,0},{1,65},{65,129},{129,193},{193,1... | collective-permute-start | bytes 589832 | tf_op jit(solution)/shard_map/ppermute | solution.py:482
  271.4 43.0 %copy-start.1 = (bf16[384,384]{1,0:T(8,128)(2,1)S(1)}, bf16[384,384]{1,0:T(8,128)(2,1)}, u32[]{:S(2)}) copy-start(bf16[384,384]{1,0:T(8,128)(2,1)} %param.15) | copy-start | bytes 884740
  283.3 31.2 %copy-start.13 = (bf16[32,384]{1,0:T(8,128)(2,1)}, bf16[32,384]{1,0:T(8,128)(2,1)S(1)}, u32[]{:S(2)}) copy-start(bf16[32,384]{1,0:T(8,128)(2,1)S(1)} %multiply_convert_fusion) | copy-start | bytes 73732
  306.3 6.0 %collective-permute-start.19 = (bf16[1024,384]{1,0:T(8,128)(2,1)S(1)}, bf16[1024,384]{1,0:T(8,128)(2,1)S(1)}, u32[]{:S(2)}, u32[]{:S(2)}) collective-permute-start(bf16[1024,384]{1,0:T(8,128)(2,1)S(1)} %bitcast.26), channel_id=1, source_target_pairs={{0,4},{4,0},{1,5},{5,1},{2,6},{6,2},{3,7},{7,3},{8,12},{12,8},{9,1... | collective-permute-start | bytes 2359304 | tf_op jit(solution)/shard_map/ppermute | solution.py:482
Sparse Core Ops, SparseCore 0:
  65.8 142.2 all-gather.2

commit v5 on v4

--- a/solution.py
+++ b/solution.py
@@ -28,6 +28,7 @@
 UP_HALF = TRIP // N_CORE
 ATOMS = ATOM_DEV * N_GRAPH
 HALF_ATOMS = ATOMS // N_CORE
+BLOCK = 512
 ATOM_BLOCK = 256
 PARTS = ((0, 128), (128, 384))
 
@@ -145,10 +146,10 @@
     )(lists, *partials)
 
 
-TRIP_BLOCK = 256
+TRIP_BLOCK = 512
 TRIP_STEPS = TRIPS // TRIP_BLOCK
-SLOT_BLOCK = 256
-SUM_CHUNK = 2048
+SLOT_BLOCK = 512
+SUM_CHUNK = 1024
 
 
 def triplet_kernel(
@@ -177,7 +178,17 @@
         place = pl.multiple_of(step * TRIP_BLOCK, TRIP_BLOCK)
         source = column_of(in_ref[...])
         target = column_of(to_ref[:, pl.ds(place, TRIP_BLOCK)])
-        candidates = product(picks_of(source & (deep - 1), deep), table[...])
+        spot = source & (deep - 1)
+
+        def more(i, total):
+            first = pl.multiple_of(i * SUM_CHUNK, SUM_CHUNK)
+            return total + product(
+                picks_of(spot - first, SUM_CHUNK), table[pl.ds(first, SUM_CHUNK), :]
+            )
+
+        candidates = product(picks_of(spot, SUM_CHUNK), table[:SUM_CHUNK, :])
+        if deep > SUM_CHUNK:
+            candidates = lax.fori_loop(1, deep // SUM_CHUNK, more, candidates)
         for k in range(0, width, 128):
             value = candidates[:, k : k + 128]
             for h in range(1, groups):
@@ -239,21 +250,23 @@
     )(trip_in, trip_live, trip_out, basis, weight, table)
 
 
-EDGE_CHUNK = 1024
+EDGE_CHUNK = 2048
 
 
 def edges_kernel(mp_ref, list_ref, table_ref, *refs):
     earlier, outs, total = refs[: -N_MP - 1], refs[-N_MP - 1 : -1], refs[-1]
     step = pl.program_id(0)
-    part = product(members(list_ref[...], EDGE_DEV, 0), table_ref[...])
 
     @pl.when(step == 0)
     def _():
-        total[...] = part
-
-    @pl.when(step > 0)
-    def _():
-        total[...] += part
+        total[...] = jnp.zeros_like(total)
+
+    def more(i, carry):
+        rows = pl.ds(pl.multiple_of(i * BLOCK, BLOCK), BLOCK)
+        total[...] += product(members(list_ref[:, rows], EDGE_DEV, 0), table_ref[rows, :])
+        return carry
+
+    lax.fori_loop(0, EDGE_CHUNK // BLOCK, more, 0)
 
     @pl.when(step == SLOTS // EDGE_CHUNK - 1)
     def _():
@@ -290,99 +303,101 @@
     )(mp, lists, returned, *earlier)
 
 
-SIDE = 4
-MAP_STEPS = N_MP // SIDE
+WIDE = 2 * COLS
 
 
 def layers_kernel(mp_ref, *refs):
-    updates, refs = refs[:N_MP], refs[N_MP:]
-    states, (up_ref, weight_ref), refs = refs[:N_MP], refs[N_MP : N_MP + 2], refs[N_MP + 2 :]
-    outs = refs[:N_MP]
-    hidden, given, inner = refs[N_MP:]
-    step = pl.program_id(0)
+    updates, states, weight_ref = refs[:N_MP], refs[N_MP : 2 * N_MP], refs[2 * N_MP]
+    refs = refs[2 * N_MP + 1 :]
+    outs, (hidden, given, inner, up, weights, up_sem, sems) = refs[:N_MP], refs[N_MP:]
     me = mp_ref[0]
-    which = lax.div(step, MAP_STEPS)
-    side = lax.rem(step, MAP_STEPS) * SIDE
-
-    def columns(block):
-        return pl.ds(pl.multiple_of(block * COLS, 128), COLS)
-
-    @pl.when(step == 0)
-    def _():
-        a, b, c, d = (ref[...].astype(F32) for ref in updates)
-        update = ((a + b) + (c + d)).astype(BF16)
-        for k, state_ref in enumerate(states):
-            hidden[:, columns(lax.rem(me + N_MP - k, N_MP))] = state_ref[...].astype(F32)
-        for block in range(N_MP):
-            added = product(update[:, :UP_HALF], up_ref[block])
-            added = added + product(update[:, UP_HALF:], up_ref[N_MP + block])
-            at = slice(block * COLS, (block + 1) * COLS)
-            fresh = hidden[:, at] + added
+
+    def fetch(i):
+        which, block = i // N_MP, i % N_MP
+        return pltpu.make_async_copy(
+            weight_ref.at[
+                (which // HALF_MAPS) * N_MP + block, pl.ds((which % HALF_MAPS) * D, D), :
+            ],
+            weights.at[which, :, pl.ds(block * COLS, COLS)],
+            sems.at[i],
+        )
+
+    up_fetch = pltpu.make_async_copy(
+        weight_ref.at[:, pl.ds(HALF_MAPS * D, UP_HALF), :], up, up_sem
+    )
+    up_fetch.start()
+    for i in range(MAPS * N_MP):
+        fetch(i).start()
+
+    a, b, c, d = (ref[...].astype(F32) for ref in updates)
+    update = ((a + b) + (c + d)).astype(BF16)
+    for k, state_ref in enumerate(states):
+        place = pl.multiple_of(lax.rem(me + N_MP - k, N_MP) * COLS, 128)
+        hidden[:, pl.ds(place, COLS)] = state_ref[...].astype(F32)
+    up_fetch.wait()
+    for block in range(N_MP):
+        added = product(update[:, :UP_HALF], up[block])
+        added = added + product(update[:, UP_HALF:], up[N_MP + block])
+        at = slice(block * COLS, (block + 1) * COLS)
+        fresh = hidden[:, at] + added
+        hidden[:, at] = fresh
+        given[:, at] = fresh.astype(BF16)
+
+    def arrived(which, side):
+        for j in range(2):
+            i = which * N_MP + side * 2 + j
+            pltpu.make_async_copy(
+                weight_ref.at[0, pl.ds(0, D), :],
+                weights.at[which, :, pl.ds((side * 2 + j) * COLS, COLS)],
+                sems.at[i],
+            ).wait()
+        return weights[which, :, pl.ds(pl.multiple_of(side * WIDE, 128), WIDE)]
+
+    def layer(index, carry):
+        def one(side, carry):
+            at = pl.ds(pl.multiple_of(side * WIDE, 128), WIDE)
+            inner[:, at] = silu(product(given[...], arrived(2 * index, side))).astype(BF16)
+            return carry
+
+        lax.fori_loop(0, 2, one, 0)
+        for side in range(2):
+            at = slice(side * WIDE, (side + 1) * WIDE)
+            outer = silu(product(inner[...], arrived(2 * index + 1, side)))
+            fresh = (hidden[:, at] + outer) * inv_root_two
             hidden[:, at] = fresh
             given[:, at] = fresh.astype(BF16)
-
-    @pl.when(lax.rem(which, 2) == 0)
-    def _():
-        x = given[...]
-
-        def one(j, carry):
-            inner[:, columns(side + j)] = silu(product(x, weight_ref[j])).astype(BF16)
-            return carry
-
-        lax.fori_loop(0, SIDE, one, 0, unroll=True)
-
-    @pl.when(lax.rem(which, 2) == 1)
-    def _():
-        x = inner[...]
-
-        def one(j, carry):
-            at = columns(side + j)
-            fresh = (hidden[:, at] + silu(product(x, weight_ref[j]))) * inv_root_two
-            hidden[:, at] = fresh
-            given[:, at] = fresh.astype(BF16)
-            return carry
-
-        lax.fori_loop(0, SIDE, one, 0, unroll=True)
-
-    @pl.when(step == MAPS * MAP_STEPS - 1)
-    def _():
-        for k, out_ref in enumerate(outs):
-            out_ref[...] = given[:, columns(lax.rem(me + k, N_MP))]
+        return carry
+
+    lax.fori_loop(0, MAPS // 2, layer, 0)
+    for k, out_ref in enumerate(outs):
+        place = pl.multiple_of(lax.rem(me + k, N_MP) * COLS, 128)
+        out_ref[...] = given[:, pl.ds(place, COLS)]
 
 
 def layers(mp, updates, states, gathered):
-    def weight_block(i):
-        which = i // MAP_STEPS
-        side = i % MAP_STEPS
-        return ((which // HALF_MAPS) * MAP_STEPS + side, which % HALF_MAPS, 0)
-
+    vmem = pl.BlockSpec(memory_space=pltpu.VMEM)
     return pl.pallas_call(
         layers_kernel,
-        grid=(MAPS * MAP_STEPS,),
-        in_specs=[SCALAR]
-        + [whole((ROWS, TRIP))] * N_MP
-        + [whole((ROWS, COLS))] * N_MP
-        + [
-            pl.BlockSpec(
-                (N_CORE * N_MP, UP_HALF, COLS), lambda i: (0, HALF_MAPS * D // UP_HALF, 0)
-            ),
-            pl.BlockSpec((SIDE, D, COLS), weight_block),
-        ],
-        out_specs=[whole((ROWS, COLS))] * N_MP,
+        in_specs=[SCALAR] + [vmem] * (2 * N_MP) + [pl.BlockSpec(memory_space=pl.ANY)],
+        out_specs=[vmem] * N_MP,
         out_shape=[shape_of(ROWS, COLS)] * N_MP,
         scratch_shapes=[
             pltpu.VMEM((ROWS, D), F32),
             pltpu.VMEM((ROWS, D), BF16),
             pltpu.VMEM((ROWS, D), BF16),
+            pltpu.VMEM((N_CORE * N_MP, UP_HALF, COLS), BF16),
+            pltpu.VMEM((MAPS, D, D), BF16),
+            pltpu.SemaphoreType.DMA,
+            pltpu.SemaphoreType.DMA((MAPS * N_MP,)),
         ],
-        compiler_params=params(40),
+        compiler_params=pltpu.CompilerParams(vmem_limit_bytes=48 * 1024 * 1024),
         name="layers",
         cost_estimate=pl.CostEstimate(
             flops=2 * ROWS * D * D * MAPS,
             bytes_accessed=2 * D * D * MAPS,
             transcendentals=ROWS * D * MAPS,
         ),
-    )(mp, *updates, *states, gathered, gathered)
+    )(mp, *updates, *states, gathered)
 
 
 def at_block(ref, me, k):
@@ -448,17 +463,22 @@
 def final_kernel(mp_ref, core_ref, atom_ref, h0, h1, h2, h3, mine_ref, other_ref, out_ref):
     me, core = mp_ref[0], core_ref[0]
     for k, hidden_ref in enumerate((h0, h1, h2, h3)):
-        row = at_block(atom_ref, me, k)
+        place = lax.rem(me + N_MP - k, N_MP) * ROWS
+        out_ref[pl.ds(pl.multiple_of(place, ROWS), ROWS), :] = hidden_ref[...]
+
+    def one(i, carry):
+        rows = pl.ds(pl.multiple_of(i * ROWS, ROWS), ROWS)
+        row = atom_ref[:, rows]
         group = row // ATOM_DEV
         spot = (group // N_CORE) * ATOM_DEV + row % ATOM_DEV
         near = jnp.where(group % N_CORE == core, spot, -1)
         far = jnp.where(group % N_CORE == core, -1, spot)
         taken = product(picks(near, HALF_ATOMS), mine_ref[...])
         taken = taken + product(picks(far, HALF_ATOMS), other_ref[...])
-        place = lax.rem(me + N_MP - k, N_MP) * ROWS
-        out_ref[pl.ds(pl.multiple_of(place, ROWS), ROWS), :] = (
-            hidden_ref[...].astype(F32) + taken
-        ).astype(BF16)
+        out_ref[rows, :] = (out_ref[rows, :].astype(F32) + taken).astype(BF16)
+        return carry
+
+    lax.fori_loop(0, N_MP, one, 0)
 
 
 def final(mp, core, edge_atom, hiddens, mine, other):

time: 322 us -> 328 us (1.019)
  Pallas kernels: 74 us -> 77.7 us
    pallas_call x1, Pallas kernels: 13.2 us -> 17.9 us  [layers(): pl.pallas_call(layers_kernel, in_specs=[SCALAR] + [vmem] * (2 * N_MP) + [...]
  transfers between devices with their start and end apart: 25 -> 25, of which waited for: 17 -> 18; matrix products, arithmetic and copies ran while one was open for 2% -> 2% of each run, Pallas kernels for 15% -> 14%
where the time goes in v5:
time: 328 us; the launch traced here: 327 us
  waiting for transfers between devices  122 us (37%)
  Pallas kernels  77.7 us (24%)
  starting transfers between devices  67.5 us (21%)
  blocking collectives  34.5 us (11%)
  between operations  14.4 us (4%)
  local copies, waits for them, and re-layouts  8.85 us (3%)
    all_to_all x1, waiting for transfers between devices, local(): second = exchange(sums(second, PARTS[1]))  44.3 us
    pallas_call x2, Pallas kernels, triplets(): pl.pallas_call(functools.partial(triplet_kernel, groups), grid=(TRIP_STEP...  40.9 us
    ppermute x20, waiting for transfers between devices, turn(): lax.ppermute(array, axis, [(i, (i + shift) % count) for i in range(count)])  34.9 us
    all_to_all x1, waiting for transfers between devices, local(): second = exchange(second)  34.1 us
    ppermute x20, starting transfers between devices, turn(): lax.ppermute(array, axis, [(i, (i + shift) % count) for i in range(count)])  32.2 us
    pallas_call x1, Pallas kernels, layers(): pl.pallas_call(layers_kernel, in_specs=[SCALAR] + [vmem] * (2 * N_MP) + [...  17.9 us
    all_to_all x1, starting transfers between devices, local(): first = exchange(first)  13 us
    all_to_all x1, blocking collectives, local(): atom_sum = summed(lax.all_to_all(part, 'graph_1', 0, 0, tiled=True))  11.7 us
  transfers between devices with their start and end apart: 25, of which 18 were waited for; matrix products, arithmetic and copies ran while one was open for 2% of the time, Pallas kernels for 14%

profile of v5, /device:TPU:1, one launch (start us, length us, event | category | flops | bytes accessed | tf_op | source)
XLA Modules:
  0.0 327.0 jit_solution(7157824990167998641)
XLA Ops:
  7.2 2.3 project.1
  9.5 2.1 collective-permute-start
  11.6 2.6 collective-permute-start.1
  14.2 1.1 collective-permute-start.2
  15.3 0.8 reshape.63.list_ref
  16.2 4.0 %collective-permute-done.1.c_ref = bf16[512,128]{1,0:T(8,128)(2,1)S(1)} collective-permute-done((bf16[512,128]{1,0:T(8,128)(2,1)}, bf16[512,128]{1,0:T(8,128)(2,1)S(1)}, u32[]{:S(2)}, u32[]{:S(2)}) %collective-permute-start.1) | collective-permute-done | bytes 131104 | tf_op jit(solution)/shard_map/ppermute | solution.py:502
  20.2 0.9 copy-done.8
  21.1 2.9 send.2
  24.0 13.0 %all-to-all-start = ((bf16[64,64,128]{2,1,0:T(8,128)(2,1)}), bf16[64,64,128]{2,1,0:T(8,128)(2,1)S(1)}, u32[]{:S(2)}, u32[]{:S(2)}) async-start(bf16[64,64,128]{2,1,0:T(8,128)(2,1)} %bitcast.6), calls=%async_computation | async-start | bytes 2097152 | tf_op jit(solution)/shard_map/all_to_all | solution.py:565
  37.2 2.4 constant_dynamic-slice_fusion.1
  39.6 1.0 collective-permute-start.3
  40.6 2.1 collective-permute-start.4
  42.7 1.3 collective-permute-start.5
  44.0 2.2 pad_maximum_fusion
  46.2 2.1 collective-permute-done.3.b_ref
  48.3 6.0 %collective-permute-done.4.c_ref = bf16[512,256]{1,0:T(8,128)(2,1)S(1)} collective-permute-done((bf16[512,256]{1,0:T(8,128)(2,1)S(1)}, bf16[512,256]{1,0:T(8,128)(2,1)S(1)}, u32[]{:S(2)}, u32[]{:S(2)}) %collective-permute-start.4) | collective-permute-done | bytes 262176 | tf_op jit(solution)/shard_map/ppermute | solution.py:502
  54.3 3.2 send.3
  57.5 8.1 %all-to-all-done = bf16[64,64,128]{2,1,0:T(8,128)(2,1)S(1)} async-done(((bf16[64,64,128]{2,1,0:T(8,128)(2,1)}), bf16[64,64,128]{2,1,0:T(8,128)(2,1)S(1)}, u32[]{:S(2)}, u32[]{:S(2)}) %all-to-all-start) | async-done | bytes 1048608 | tf_op jit(solution)/shard_map/all_to_all | solution.py:565
  65.6 6.3 %all-to-all-start.1 = ((bf16[64,64,256]{2,1,0:T(8,128)(2,1)}), bf16[64,64,256]{2,1,0:T(8,128)(2,1)S(1)}, u32[]{:S(2)}, u32[]{:S(2)}) async-start(bf16[64,64,256]{2,1,0:T(8,128)(2,1)} %bitcast.7), calls=%async_computation.1 | async-start | bytes 4194304 | tf_op jit(solution)/shard_map/all_to_all | solution.py:568
  72.1 1.1 copy-done.5
  73.2 14.9 %triplets.3 = bf16[4,1024,128]{2,1,0:T(8,128)(2,1)S(1)} custom-call(s32[1,4096]{1,0:T(1,128)S(1)} %bitcast.28, s32[1,4096]{1,0:T(1,128)S(1)} %bitcast.30, s32[1,4096]{1,0:T(1,128)S(1)} %bitcast.32, f32[42,4096]{1,0:T(8,128)S(1)} %copy-done.5, bf16[144,128]{1,0:T(8,128)(2,1)S(1)} %slice.9.weight_ref, bf16[4096,128]{1,0:T(8,128)(2,1)S(1)} %bitcast.23), custom_call_target="tpu_custom_call" | custom-call | flops 8589934592 | bytes 2304000 | tf_op jit(solution)/shard_map/triplets/pallas_call | solution.py:225
  88.2 1.0 copy-done.3
  89.2 34.1 %all-to-all-done.1 = bf16[64,64,256]{2,1,0:T(8,128)(2,1)S(1)} async-done(((bf16[64,64,256]{2,1,0:T(8,128)(2,1)}), bf16[64,64,256]{2,1,0:T(8,128)(2,1)S(1)}, u32[]{:S(2)}, u32[]{:S(2)}) %all-to-all-start.1) | async-done | bytes 2097184 | tf_op jit(solution)/shard_map/all_to_all | solution.py:568
  123.2 5.8 %all-to-all-start.3 = ((bf16[64,64,128]{2,1,0:T(8,128)(2,1)}), bf16[64,64,128]{2,1,0:T(8,128)(2,1)S(1)}, u32[]{:S(2)}, u32[]{:S(2)}) async-start(bf16[64,64,128]{2,1,0:T(8,128)(2,1)} %bitcast.25), calls=%async_computation.3 | async-start | bytes 2097152 | tf_op jit(solution)/shard_map/all_to_all | solution.py:571
  129.1 1.1 copy-done.6
  130.2 25.9 %triplets.2 = bf16[2,2048,256]{2,1,0:T(8,128)(2,1)S(1)} custom-call(s32[1,4096]{1,0:T(1,128)S(1)} %bitcast.29, s32[1,4096]{1,0:T(1,128)S(1)} %bitcast.31, s32[1,4096]{1,0:T(1,128)S(1)} %bitcast.33, f32[42,4096]{1,0:T(8,128)S(1)} %copy-done.6, bf16[144,256]{1,0:T(8,128)(2,1)S(1)} %slice.8.weight_ref, bf16[4096,256]{1,0:T(8,128)(2,1)S(1)} %bitcast.21), custom_call_target="tpu_custom_call" | custom-call | flops 17179869184 | bytes 4608000 | tf_op jit(solution)/shard_map/triplets/pallas_call | solution.py:225
  156.1 1.3 copy-done.2
  157.4 0.2 all-to-all-done.3
  157.6 10.1 %all-to-all-start.2 = ((bf16[64,64,256]{2,1,0:T(8,128)(2,1)}), bf16[64,64,256]{2,1,0:T(8,128)(2,1)S(1)}, u32[]{:S(2)}, u32[]{:S(2)}) async-start(bf16[64,64,256]{2,1,0:T(8,128)(2,1)} %bitcast.22), calls=%async_computation.2 | async-start | bytes 4194304 | tf_op jit(solution)/shard_map/all_to_all | solution.py:572
  167.8 1.0 collective-permute-start.9
  168.8 2.1 collective-permute-start.10
  170.9 1.3 collective-permute-start.11
  172.2 2.5 edges.2
  174.7 44.3 %all-to-all-done.2 = bf16[64,64,256]{2,1,0:T(8,128)(2,1)S(1)} async-done(((bf16[64,64,256]{2,1,0:T(8,128)(2,1)}), bf16[64,64,256]{2,1,0:T(8,128)(2,1)S(1)}, u32[]{:S(2)}, u32[]{:S(2)}) %all-to-all-start.2) | async-done | bytes 2097184 | tf_op jit(solution)/shard_map/all_to_all | solution.py:572
  219.0 2.5 edges.3
  221.5 1.0 collective-permute-start.6
  222.5 2.1 collective-permute-start.7
  224.7 1.3 collective-permute-start.8
  226.0 0.8 collective-permute-done.6.refs_1_
  226.8 2.5 collective-permute-done.7.refs_2_
  229.3 0.2 collective-permute-done.8.refs_3_
  229.5 17.9 %layers.1 = (bf16[128,384]{1,0:T(8,128)(2,1)S(1)}, bf16[128,384]{1,0:T(8,128)(2,1)S(1)}, bf16[128,384]{1,0:T(8,128)(2,1)S(1)}, bf16[128,384]{1,0:T(8,128)(2,1)S(1)}) custom-call(s32[1]{0:T(128)} %bitcast.mp_ref, bf16[128,384]{1,0:T(8,128)(2,1)S(1)} %get-tuple-element.41.refs_0_, bf16[128,384]{1,0:T(8,128)(2,1)S(1)} %collective-permute-done.6.refs_1_, ...), custom_call_target="tpu_custom_call" | custom-call | flops 3623878656 | bytes 28311552 | tf_op jit(solution)/shard_map/layers/pallas_call | solution.py:379
  247.4 2.0 collective-permute-start.12
  249.5 1.8 collective-permute-start.13
  251.3 0.6 collective-permute-start.14
  252.0 0.2 collective-permute-done.12.h1
  252.2 2.9 collective-permute-done.13.h2
  255.1 1.0 collective-permute-done.14.h3
  256.1 2.4 atoms.1
  258.5 1.6 collective-permute-start.15
  260.2 1.9 collective-permute-done.15.got_ref
  262.1 0.2 meet.1
  262.3 1.6 collective-permute-start.18
  263.9 1.2 collective-permute-start.17
  265.1 3.4 %collective-permute-done.18 = bf16[256,384]{1,0:T(8,128)(2,1)S(1)} collective-permute-done((bf16[256,384]{1,0:T(8,128)(2,1)S(1)}, bf16[256,384]{1,0:T(8,128)(2,1)S(1)}, u32[]{:S(2)}, u32[]{:S(2)}) %collective-permute-start.18) | collective-permute-done | bytes 196640 | tf_op jit(solution)/shard_map/ppermute | solution.py:502
  268.5 2.8 collective-permute-done.17
  271.2 5.2 %collective-permute-done.16 = bf16[256,384]{1,0:T(8,128)(2,1)S(1)} collective-permute-done((bf16[256,384]{1,0:T(8,128)(2,1)S(1)}, bf16[256,384]{1,0:T(8,128)(2,1)S(1)}, u32[]{:S(2)}, u32[]{:S(2)}) %collective-permute-start.16) | collective-permute-done | bytes 196640 | tf_op jit(solution)/shard_map/ppermute | solution.py:502
  276.4 0.1 add_convert_fusion
  276.6 11.7 %all_to_all.35 = bf16[8,32,384]{2,1,0:T(8,128)(2,1)S(1)} all-to-all(bf16[8,32,384]{2,1,0:T(8,128)(2,1)S(1)} %bitcast.38), channel_id=1, replica_groups=mesh['graph_0'=4,'graph_1'=8,'graph_2'=2,'mp'=4] {'graph_1'}, dimensions={0} | all-to-all | bytes 393216 | tf_op jit(solution)/shard_map/all_to_all | solution.py:584
  288.3 11.3 %all_to_all.36 = bf16[8,32,384]{2,1,0:T(8,128)(2,1)S(1)} all-to-all(bf16[8,32,384]{2,1,0:T(8,128)(2,1)S(1)} %broadcast_in_dim.25), channel_id=1, replica_groups=mesh['graph_0'=4,'graph_1'=8,'graph_2'=2,'mp'=4] {'graph_1'}, dimensions={0} | all-to-all | bytes 393216 | tf_op jit(solution)/shard_map/all_to_all | solution.py:586
  299.7 11.6 %all_to_all.37 = bf16[4,256,384]{2,1,0:T(8,128)(2,1)S(1)} all-to-all(bf16[4,256,384]{2,1,0:T(8,128)(2,1)S(1)} %broadcast_in_dim.27), channel_id=1, replica_groups=mesh['graph_0'=4,'graph_1'=8,'graph_2'=2,'mp'=4] {'graph_0'}, dimensions={0} | all-to-all | bytes 1572864 | tf_op jit(solution)/shard_map/all_to_all | solution.py:589
  311.2 4.1 %collective-permute-start.19 = (bf16[1024,384]{1,0:T(8,128)(2,1)S(1)}, bf16[1024,384]{1,0:T(8,128)(2,1)S(1)}, u32[]{:S(2)}, u32[]{:S(2)}) collective-permute-start(bf16[1024,384]{1,0:T(8,128)(2,1)S(1)} %bitcast.26), channel_id=1, source_target_pairs={{0,4},{4,0},{1,5},{5,1},{2,6},{6,2},{3,7},{7,3},{8,12},{12,8},{9,1... | collective-permute-start | bytes 2359304 | tf_op jit(solution)/shard_map/ppermute | solution.py:502
  315.3 1.9 collective-permute-done.19.other_ref
  317.2 2.9 final.1
  (45 shorter events, 0.4 us)
Async XLA Ops:
  7.2 29.9 %copy-start = (bf16[384,384]{1,0:T(8,128)(2,1)S(1)}, bf16[384,384]{1,0:T(8,128)(2,1)}, u32[]{:S(2)}) copy-start(bf16[384,384]{1,0:T(8,128)(2,1)} %param.15) | copy-start | bytes 884740
  9.5 6.7 %collective-permute-start = (bf16[512,128]{1,0:T(8,128)(2,1)}, bf16[512,128]{1,0:T(8,128)(2,1)S(1)}, u32[]{:S(2)}, u32[]{:S(2)}) collective-permute-start(bf16[512,128]{1,0:T(8,128)(2,1)} %get-tuple-element.31.a_ref), channel_id=1, source_target_pairs={{0,1},{1,2},{2,3},{3,0},{4,5},{5,6},{6,7},{7,4},{8,9},{9,10},{10,1... | collective-permute-start | bytes 393224 | tf_op jit(solution)/shard_map/ppermute | solution.py:502
  11.6 8.5 %collective-permute-start.1 = (bf16[512,128]{1,0:T(8,128)(2,1)}, bf16[512,128]{1,0:T(8,128)(2,1)S(1)}, u32[]{:S(2)}, u32[]{:S(2)}) collective-permute-start(bf16[512,128]{1,0:T(8,128)(2,1)} %get-tuple-element.31.a_ref), channel_id=1, source_target_pairs={{0,2},{1,3},{2,0},{3,1},{4,6},{5,7},{6,4},{7,5},{8,10},{9,11},{10,... | collective-permute-start | bytes 393224 | tf_op jit(solution)/shard_map/ppermute | solution.py:502
  14.2 5.9 %collective-permute-start.2 = (bf16[512,128]{1,0:T(8,128)(2,1)}, bf16[512,128]{1,0:T(8,128)(2,1)S(1)}, u32[]{:S(2)}, u32[]{:S(2)}) collective-permute-start(bf16[512,128]{1,0:T(8,128)(2,1)} %get-tuple-element.31.a_ref), channel_id=1, source_target_pairs={{0,3},{1,0},{2,1},{3,2},{4,7},{5,4},{6,5},{7,6},{8,11},{9,8},{10,9... | collective-permute-start | bytes 393224 | tf_op jit(solution)/shard_map/ppermute | solution.py:502
  20.2 0.9 copy-start.8
  24.0 41.6 %all-to-all-start = ((bf16[64,64,128]{2,1,0:T(8,128)(2,1)}), bf16[64,64,128]{2,1,0:T(8,128)(2,1)S(1)}, u32[]{:S(2)}, u32[]{:S(2)}) async-start(bf16[64,64,128]{2,1,0:T(8,128)(2,1)} %bitcast.6), calls=%async_computation | async-start | bytes 2097152 | tf_op jit(solution)/shard_map/all_to_all | solution.py:565
  37.0 192.4 %all-gather.3.cloned.1.call-start = ((), (), s32[]{:S(2)}) async-start(), calls=%async_computation.7 | async-start | bytes 33177600 | tf_op jit(solution)/shard_map/all_gather | solution.py:569
  37.1 2.4 copy-start.7
  39.6 8.7 %collective-permute-start.3 = (bf16[512,256]{1,0:T(8,128)(2,1)S(1)}, bf16[512,256]{1,0:T(8,128)(2,1)S(1)}, u32[]{:S(2)}, u32[]{:S(2)}) collective-permute-start(bf16[512,256]{1,0:T(8,128)(2,1)S(1)} %copy-done.7), channel_id=1, source_target_pairs={{0,1},{1,2},{2,3},{3,0},{4,5},{5,6},{6,7},{7,4},{8,9},{9,10},{10,1... | collective-permute-start | bytes 786440 | tf_op jit(solution)/shard_map/ppermute | solution.py:502
  40.6 13.7 %collective-permute-start.4 = (bf16[512,256]{1,0:T(8,128)(2,1)S(1)}, bf16[512,256]{1,0:T(8,128)(2,1)S(1)}, u32[]{:S(2)}, u32[]{:S(2)}) collective-permute-start(bf16[512,256]{1,0:T(8,128)(2,1)S(1)} %copy-done.7), channel_id=1, source_target_pairs={{0,2},{1,3},{2,0},{3,1},{4,6},{5,7},{6,4},{7,5},{8,10},{9,11},{10,... | collective-permute-start | bytes 786440 | tf_op jit(solution)/shard_map/ppermute | solution.py:502
  42.7 11.6 %collective-permute-start.5 = (bf16[512,256]{1,0:T(8,128)(2,1)S(1)}, bf16[512,256]{1,0:T(8,128)(2,1)S(1)}, u32[]{:S(2)}, u32[]{:S(2)}) collective-permute-start(bf16[512,256]{1,0:T(8,128)(2,1)S(1)} %copy-done.7), channel_id=1, source_target_pairs={{0,3},{1,0},{2,1},{3,2},{4,7},{5,4},{6,5},{7,6},{8,11},{9,8},{10,9... | collective-permute-start | bytes 786440 | tf_op jit(solution)/shard_map/ppermute | solution.py:502
  65.6 6.4 %copy-start.14 = (f32[42,384]{1,0:T(8,128)S(1)}, f32[42,384]{1,0:T(8,128)}, u32[]{:S(2)}) copy-start(f32[42,384]{1,0:T(8,128)} %param.14) | copy-start | bytes 193540
  65.6 6.5 %copy-start.9 = (s32[4096]{0:T(1024)S(1)}, s32[4096]{0:T(1024)}, u32[]{:S(2)}) copy-start(s32[4096]{0:T(1024)} %param.18) | copy-start | bytes 49156
  65.6 6.5 %copy-start.10 = (s32[4096]{0:T(1024)S(1)}, s32[4096]{0:T(1024)}, u32[]{:S(2)}) copy-start(s32[4096]{0:T(1024)} %param.20) | copy-start | bytes 49156
  65.6 6.5 %copy-start.11 = (s32[4096]{0:T(1024)S(1)}, s32[4096]{0:T(1024)}, u32[]{:S(2)}) copy-start(s32[4096]{0:T(1024)} %param.19) | copy-start | bytes 49156
  65.6 57.6 %all-to-all-start.1 = ((bf16[64,64,256]{2,1,0:T(8,128)(2,1)}), bf16[64,64,256]{2,1,0:T(8,128)(2,1)S(1)}, u32[]{:S(2)}, u32[]{:S(2)}) async-start(bf16[64,64,256]{2,1,0:T(8,128)(2,1)} %bitcast.7), calls=%async_computation.1 | async-start | bytes 4194304 | tf_op jit(solution)/shard_map/all_to_all | solution.py:568
  72.1 1.1 copy-start.5
  88.2 1.0 copy-start.3
  123.2 34.4 %all-to-all-start.3 = ((bf16[64,64,128]{2,1,0:T(8,128)(2,1)}), bf16[64,64,128]{2,1,0:T(8,128)(2,1)S(1)}, u32[]{:S(2)}, u32[]{:S(2)}) async-start(bf16[64,64,128]{2,1,0:T(8,128)(2,1)} %bitcast.25), calls=%async_computation.3 | async-start | bytes 2097152 | tf_op jit(solution)/shard_map/all_to_all | solution.py:571
  129.1 1.1 copy-start.6
  156.1 1.3 copy-start.2
  157.6 61.4 %all-to-all-start.2 = ((bf16[64,64,256]{2,1,0:T(8,128)(2,1)}), bf16[64,64,256]{2,1,0:T(8,128)(2,1)S(1)}, u32[]{:S(2)}, u32[]{:S(2)}) async-start(bf16[64,64,256]{2,1,0:T(8,128)(2,1)} %bitcast.22), calls=%async_computation.2 | async-start | bytes 4194304 | tf_op jit(solution)/shard_map/all_to_all | solution.py:572
  167.8 61.7 %copy-start.4 = (bf16[128,384]{1,0:T(8,128)(2,1)S(1)}, bf16[128,384]{1,0:T(8,128)(2,1)}, u32[]{:S(2)}) copy-start(bf16[128,384]{1,0:T(8,128)(2,1)} %get-tuple-element.45.refs_4_) | copy-start | bytes 294916
  167.8 56.9 %collective-permute-start.9 = (bf16[128,384]{1,0:T(8,128)(2,1)}, bf16[128,384]{1,0:T(8,128)(2,1)}, u32[]{:S(2)}, u32[]{:S(2)}) collective-permute-start(bf16[128,384]{1,0:T(8,128)(2,1)} %get-tuple-element.46), channel_id=1, source_target_pairs={{0,1},{1,2},{2,3},{3,0},{4,5},{5,6},{6,7},{7,4},{8,9},{9,10},{10,1... | collective-permute-start | bytes 294920 | tf_op jit(solution)/shard_map/ppermute | solution.py:502
  168.8 57.2 %collective-permute-start.10 = (bf16[128,384]{1,0:T(8,128)(2,1)}, bf16[128,384]{1,0:T(8,128)(2,1)}, u32[]{:S(2)}, u32[]{:S(2)}) collective-permute-start(bf16[128,384]{1,0:T(8,128)(2,1)} %get-tuple-element.47), channel_id=1, source_target_pairs={{0,2},{1,3},{2,0},{3,1},{4,6},{5,7},{6,4},{7,5},{8,10},{9,11},{10,... | collective-permute-start | bytes 294920 | tf_op jit(solution)/shard_map/ppermute | solution.py:502
  170.9 55.1 %collective-permute-start.11 = (bf16[128,384]{1,0:T(8,128)(2,1)}, bf16[128,384]{1,0:T(8,128)(2,1)}, u32[]{:S(2)}, u32[]{:S(2)}) collective-permute-start(bf16[128,384]{1,0:T(8,128)(2,1)} %get-tuple-element.48), channel_id=1, source_target_pairs={{0,3},{1,0},{2,1},{3,2},{4,7},{5,4},{6,5},{7,6},{8,11},{9,8},{10,9... | collective-permute-start | bytes 294920 | tf_op jit(solution)/shard_map/ppermute | solution.py:502
  221.5 5.3 %collective-permute-start.6 = (bf16[128,384]{1,0:T(8,128)(2,1)S(1)}, bf16[128,384]{1,0:T(8,128)(2,1)S(1)}, u32[]{:S(2)}, u32[]{:S(2)}) collective-permute-start(bf16[128,384]{1,0:T(8,128)(2,1)S(1)} %get-tuple-element.42), channel_id=1, source_target_pairs={{0,1},{1,2},{2,3},{3,0},{4,5},{5,6},{6,7},{7,4},{8,9},{9,10},{10,1... | collective-permute-start | bytes 294920 | tf_op jit(solution)/shard_map/ppermute | solution.py:502
  222.5 6.7 %collective-permute-start.7 = (bf16[128,384]{1,0:T(8,128)(2,1)S(1)}, bf16[128,384]{1,0:T(8,128)(2,1)S(1)}, u32[]{:S(2)}, u32[]{:S(2)}) collective-permute-start(bf16[128,384]{1,0:T(8,128)(2,1)S(1)} %get-tuple-element.43), channel_id=1, source_target_pairs={{0,2},{1,3},{2,0},{3,1},{4,6},{5,7},{6,4},{7,5},{8,10},{9,11},{10,... | collective-permute-start | bytes 294920 | tf_op jit(solution)/shard_map/ppermute | solution.py:502
  224.7 4.8 %collective-permute-start.8 = (bf16[128,384]{1,0:T(8,128)(2,1)S(1)}, bf16[128,384]{1,0:T(8,128)(2,1)S(1)}, u32[]{:S(2)}, u32[]{:S(2)}) collective-permute-start(bf16[128,384]{1,0:T(8,128)(2,1)S(1)} %get-tuple-element.44), channel_id=1, source_target_pairs={{0,3},{1,0},{2,1},{3,2},{4,7},{5,4},{6,5},{7,6},{8,11},{9,8},{10,9... | collective-permute-start | bytes 294920 | tf_op jit(solution)/shard_map/ppermute | solution.py:502
  229.5 26.6 %copy-start.12 = (s32[512]{0:T(512)S(1)}, s32[512]{0:T(512)}, u32[]{:S(2)}) copy-start(s32[512]{0:T(512)} %param.21) | copy-start | bytes 6148
  247.4 4.8 %collective-permute-start.12 = (bf16[128,384]{1,0:T(8,128)(2,1)S(1)}, bf16[128,384]{1,0:T(8,128)(2,1)S(1)}, u32[]{:S(2)}, u32[]{:S(2)}) collective-permute-start(bf16[128,384]{1,0:T(8,128)(2,1)S(1)} %get-tuple-element.51), channel_id=1, source_target_pairs={{0,1},{1,2},{2,3},{3,0},{4,5},{5,6},{6,7},{7,4},{8,9},{9,10},{10,1... | collective-permute-start | bytes 294920 | tf_op jit(solution)/shard_map/ppermute | solution.py:502
  249.5 5.6 %collective-permute-start.13 = (bf16[128,384]{1,0:T(8,128)(2,1)S(1)}, bf16[128,384]{1,0:T(8,128)(2,1)S(1)}, u32[]{:S(2)}, u32[]{:S(2)}) collective-permute-start(bf16[128,384]{1,0:T(8,128)(2,1)S(1)} %get-tuple-element.52), channel_id=1, source_target_pairs={{0,2},{1,3},{2,0},{3,1},{4,6},{5,7},{6,4},{7,5},{8,10},{9,11},{10,... | collective-permute-start | bytes 294920 | tf_op jit(solution)/shard_map/ppermute | solution.py:502
  251.3 4.8 %collective-permute-start.14 = (bf16[128,384]{1,0:T(8,128)(2,1)S(1)}, bf16[128,384]{1,0:T(8,128)(2,1)S(1)}, u32[]{:S(2)}, u32[]{:S(2)}) collective-permute-start(bf16[128,384]{1,0:T(8,128)(2,1)S(1)} %get-tuple-element.53), channel_id=1, source_target_pairs={{0,3},{1,0},{2,1},{3,2},{4,7},{5,4},{6,5},{7,6},{8,11},{9,8},{10,9... | collective-permute-start | bytes 294920 | tf_op jit(solution)/shard_map/ppermute | solution.py:502
  258.5 3.5 %collective-permute-start.15 = (bf16[1024,384]{1,0:T(8,128)(2,1)S(1)}, bf16[1024,384]{1,0:T(8,128)(2,1)S(1)}, u32[]{:S(2)}, u32[]{:S(2)}) collective-permute-start(bf16[1024,384]{1,0:T(8,128)(2,1)S(1)} %get-tuple-element.55), channel_id=1, source_target_pairs={{0,4},{4,0},{1,5},{5,1},{2,6},{6,2},{3,7},{7,3},{8,12},{12,8},{9,1... | collective-permute-start | bytes 2359304 | tf_op jit(solution)/shard_map/ppermute | solution.py:502
  262.3 6.2 %collective-permute-start.18 = (bf16[256,384]{1,0:T(8,128)(2,1)S(1)}, bf16[256,384]{1,0:T(8,128)(2,1)S(1)}, u32[]{:S(2)}, u32[]{:S(2)}) collective-permute-start(bf16[256,384]{1,0:T(8,128)(2,1)S(1)} %get-tuple-element.59), channel_id=1, source_target_pairs={{0,192},{64,0},{128,64},{192,128},{1,193},{65,1},{129,65},{193,129... | collective-permute-start | bytes 589832 | tf_op jit(solution)/shard_map/ppermute | solution.py:502
  263.9 7.3 %collective-permute-start.17 = (bf16[256,384]{1,0:T(8,128)(2,1)S(1)}, bf16[256,384]{1,0:T(8,128)(2,1)S(1)}, u32[]{:S(2)}, u32[]{:S(2)}) collective-permute-start(bf16[256,384]{1,0:T(8,128)(2,1)S(1)} %get-tuple-element.58), channel_id=1, source_target_pairs={{0,128},{64,192},{128,0},{192,64},{1,129},{65,193},{129,1},{193,65... | collective-permute-start | bytes 589832 | tf_op jit(solution)/shard_map/ppermute | solution.py:502
  265.1 11.4 %collective-permute-start.16 = (bf16[256,384]{1,0:T(8,128)(2,1)S(1)}, bf16[256,384]{1,0:T(8,128)(2,1)S(1)}, u32[]{:S(2)}, u32[]{:S(2)}) collective-permute-start(bf16[256,384]{1,0:T(8,128)(2,1)S(1)} %get-tuple-element.57), channel_id=1, source_target_pairs={{0,64},{64,128},{128,192},{192,0},{1,65},{65,129},{129,193},{193,1... | collective-permute-start | bytes 589832 | tf_op jit(solution)/shard_map/ppermute | solution.py:502
  276.4 43.7 %copy-start.1 = (bf16[384,384]{1,0:T(8,128)(2,1)S(1)}, bf16[384,384]{1,0:T(8,128)(2,1)}, u32[]{:S(2)}) copy-start(bf16[384,384]{1,0:T(8,128)(2,1)} %param.15) | copy-start | bytes 884740
  288.3 31.9 %copy-start.13 = (bf16[32,384]{1,0:T(8,128)(2,1)}, bf16[32,384]{1,0:T(8,128)(2,1)S(1)}, u32[]{:S(2)}) copy-start(bf16[32,384]{1,0:T(8,128)(2,1)S(1)} %multiply_convert_fusion) | copy-start | bytes 73732
  311.2 6.0 %collective-permute-start.19 = (bf16[1024,384]{1,0:T(8,128)(2,1)S(1)}, bf16[1024,384]{1,0:T(8,128)(2,1)S(1)}, u32[]{:S(2)}, u32[]{:S(2)}) collective-permute-start(bf16[1024,384]{1,0:T(8,128)(2,1)S(1)} %bitcast.26), channel_id=1, source_target_pairs={{0,4},{4,0},{1,5},{5,1},{2,6},{6,2},{3,7},{7,3},{8,12},{12,8},{9,1... | collective-permute-start | bytes 2359304 | tf_op jit(solution)/shard_map/ppermute | solution.py:502
Sparse Core Ops, SparseCore 0:
  65.8 142.2 all-gather.2

commit v6 on v5

--- a/solution.py
+++ b/solution.py
@@ -250,23 +250,21 @@
     )(trip_in, trip_live, trip_out, basis, weight, table)
 
 
-EDGE_CHUNK = 2048
+EDGE_CHUNK = 1024
 
 
 def edges_kernel(mp_ref, list_ref, table_ref, *refs):
     earlier, outs, total = refs[: -N_MP - 1], refs[-N_MP - 1 : -1], refs[-1]
     step = pl.program_id(0)
+    part = product(members(list_ref[...], EDGE_DEV, 0), table_ref[...])
 
     @pl.when(step == 0)
     def _():
-        total[...] = jnp.zeros_like(total)
-
-    def more(i, carry):
-        rows = pl.ds(pl.multiple_of(i * BLOCK, BLOCK), BLOCK)
-        total[...] += product(members(list_ref[:, rows], EDGE_DEV, 0), table_ref[rows, :])
-        return carry
-
-    lax.fori_loop(0, EDGE_CHUNK // BLOCK, more, 0)
+        total[...] = part
+
+    @pl.when(step > 0)
+    def _():
+        total[...] += part
 
     @pl.when(step == SLOTS // EDGE_CHUNK - 1)
     def _():
@@ -304,6 +302,7 @@
 
 
 WIDE = 2 * COLS
+AHEAD = 6
 
 
 def layers_kernel(mp_ref, *refs):
@@ -313,12 +312,11 @@
     me = mp_ref[0]
 
     def fetch(i):
-        which, block = i // N_MP, i % N_MP
+        which, block = lax.div(i, N_MP), lax.rem(i, N_MP)
+        rows = pl.multiple_of(lax.rem(which, HALF_MAPS) * D, D)
         return pltpu.make_async_copy(
-            weight_ref.at[
-                (which // HALF_MAPS) * N_MP + block, pl.ds((which % HALF_MAPS) * D, D), :
-            ],
-            weights.at[which, :, pl.ds(block * COLS, COLS)],
+            weight_ref.at[lax.div(which, HALF_MAPS) * N_MP + block, pl.ds(rows, D), :],
+            weights.at[which, :, pl.ds(pl.multiple_of(block * COLS, 128), COLS)],
             sems.at[i],
         )
 
@@ -326,7 +324,7 @@
         weight_ref.at[:, pl.ds(HALF_MAPS * D, UP_HALF), :], up, up_sem
     )
     up_fetch.start()
-    for i in range(MAPS * N_MP):
+    for i in range(AHEAD):
         fetch(i).start()
 
     a, b, c, d = (ref[...].astype(F32) for ref in updates)
@@ -346,11 +344,12 @@
     def arrived(which, side):
         for j in range(2):
             i = which * N_MP + side * 2 + j
-            pltpu.make_async_copy(
-                weight_ref.at[0, pl.ds(0, D), :],
-                weights.at[which, :, pl.ds((side * 2 + j) * COLS, COLS)],
-                sems.at[i],
-            ).wait()
+            fetch(i).wait()
+
+            @pl.when(i + AHEAD < MAPS * N_MP)
+            def _():
+                fetch(i + AHEAD).start()
+
         return weights[which, :, pl.ds(pl.multiple_of(side * WIDE, 128), WIDE)]
 
     def layer(index, carry):
@@ -478,7 +477,7 @@
         out_ref[rows, :] = (out_ref[rows, :].astype(F32) + taken).astype(BF16)
         return carry
 
-    lax.fori_loop(0, N_MP, one, 0)
+    lax.fori_loop(0, N_MP, one, 0, unroll=2)
 
 
 def final(mp, core, edge_atom, hiddens, mine, other):

time: 328 us -> 322 us (0.982)
  Pallas kernels: 77.7 us -> 71.1 us
    pallas_call x1, Pallas kernels: 17.9 us -> 12.7 us  [layers(): pl.pallas_call(layers_kernel, in_specs=[SCALAR] + [vmem] * (2 * N_MP) + [...]
where the time goes in v6:
time: 322 us; the launch traced here: 321 us
  waiting for transfers between devices  122 us (38%)
  Pallas kernels  71.1 us (22%)
  starting transfers between devices  67.6 us (21%)
  blocking collectives  34.5 us (11%)
  between operations  14.4 us (4%)
  local copies, waits for them, and re-layouts  8.85 us (3%)
    all_to_all x1, waiting for transfers between devices, local(): second = exchange(sums(second, PARTS[1]))  44.9 us
    pallas_call x2, Pallas kernels, triplets(): pl.pallas_call(functools.partial(triplet_kernel, groups), grid=(TRIP_STEP...  40.9 us
    ppermute x20, waiting for transfers between devices, turn(): lax.ppermute(array, axis, [(i, (i + shift) % count) for i in range(count)])  34.9 us
    all_to_all x1, waiting for transfers between devices, local(): second = exchange(second)  34.1 us
    ppermute x20, starting transfers between devices, turn(): lax.ppermute(array, axis, [(i, (i + shift) % count) for i in range(count)])  32.2 us
    all_to_all x1, starting transfers between devices, local(): first = exchange(first)  13 us
    pallas_call x1, Pallas kernels, layers(): pl.pallas_call(layers_kernel, in_specs=[SCALAR] + [vmem] * (2 * N_MP) + [...  12.7 us
    all_to_all x1, blocking collectives, local(): atom_sum = summed(lax.all_to_all(part, 'graph_1', 0, 0, tiled=True))  11.7 us
  transfers between devices with their start and end apart: 25, of which 18 were waited for; matrix products, arithmetic and copies ran while one was open for 2% of the time, Pallas kernels for 14%

profile of v6, /device:TPU:1, one launch (start us, length us, event | category | flops | bytes accessed | tf_op | source)
XLA Modules:
  0.0 320.9 jit_solution(1381311067562761457)
XLA Ops:
  7.2 2.3 project.1
  9.5 2.1 collective-permute-start
  11.6 2.6 collective-permute-start.1
  14.2 1.1 collective-permute-start.2
  15.3 0.8 reshape.63.list_ref
  16.2 4.0 %collective-permute-done.1.c_ref = bf16[512,128]{1,0:T(8,128)(2,1)S(1)} collective-permute-done((bf16[512,128]{1,0:T(8,128)(2,1)}, bf16[512,128]{1,0:T(8,128)(2,1)S(1)}, u32[]{:S(2)}, u32[]{:S(2)}) %collective-permute-start.1) | collective-permute-done | bytes 131104 | tf_op jit(solution)/shard_map/ppermute | solution.py:501
  20.2 0.9 copy-done.8
  21.1 2.9 send.2
  24.0 13.0 %all-to-all-start = ((bf16[64,64,128]{2,1,0:T(8,128)(2,1)}), bf16[64,64,128]{2,1,0:T(8,128)(2,1)S(1)}, u32[]{:S(2)}, u32[]{:S(2)}) async-start(bf16[64,64,128]{2,1,0:T(8,128)(2,1)} %bitcast.6), calls=%async_computation | async-start | bytes 2097152 | tf_op jit(solution)/shard_map/all_to_all | solution.py:564
  37.2 2.4 constant_dynamic-slice_fusion.1
  39.6 1.0 collective-permute-start.3
  40.6 2.1 collective-permute-start.4
  42.7 1.3 collective-permute-start.5
  44.0 2.2 pad_maximum_fusion
  46.2 2.1 collective-permute-done.3.b_ref
  48.3 6.0 %collective-permute-done.4.c_ref = bf16[512,256]{1,0:T(8,128)(2,1)S(1)} collective-permute-done((bf16[512,256]{1,0:T(8,128)(2,1)S(1)}, bf16[512,256]{1,0:T(8,128)(2,1)S(1)}, u32[]{:S(2)}, u32[]{:S(2)}) %collective-permute-start.4) | collective-permute-done | bytes 262176 | tf_op jit(solution)/shard_map/ppermute | solution.py:501
  54.3 3.2 send.3
  57.5 8.1 %all-to-all-done = bf16[64,64,128]{2,1,0:T(8,128)(2,1)S(1)} async-done(((bf16[64,64,128]{2,1,0:T(8,128)(2,1)}), bf16[64,64,128]{2,1,0:T(8,128)(2,1)S(1)}, u32[]{:S(2)}, u32[]{:S(2)}) %all-to-all-start) | async-done | bytes 1048608 | tf_op jit(solution)/shard_map/all_to_all | solution.py:564
  65.6 6.3 %all-to-all-start.1 = ((bf16[64,64,256]{2,1,0:T(8,128)(2,1)}), bf16[64,64,256]{2,1,0:T(8,128)(2,1)S(1)}, u32[]{:S(2)}, u32[]{:S(2)}) async-start(bf16[64,64,256]{2,1,0:T(8,128)(2,1)} %bitcast.7), calls=%async_computation.1 | async-start | bytes 4194304 | tf_op jit(solution)/shard_map/all_to_all | solution.py:567
  72.1 1.1 copy-done.5
  73.2 14.9 %triplets.3 = bf16[4,1024,128]{2,1,0:T(8,128)(2,1)S(1)} custom-call(s32[1,4096]{1,0:T(1,128)S(1)} %bitcast.28, s32[1,4096]{1,0:T(1,128)S(1)} %bitcast.30, s32[1,4096]{1,0:T(1,128)S(1)} %bitcast.32, f32[42,4096]{1,0:T(8,128)S(1)} %copy-done.5, bf16[144,128]{1,0:T(8,128)(2,1)S(1)} %slice.9.weight_ref, bf16[4096,128]{1,0:T(8,128)(2,1)S(1)} %bitcast.23), custom_call_target="tpu_custom_call" | custom-call | flops 8589934592 | bytes 2304000 | tf_op jit(solution)/shard_map/triplets/pallas_call | solution.py:225
  88.2 1.0 copy-done.3
  89.2 34.1 %all-to-all-done.1 = bf16[64,64,256]{2,1,0:T(8,128)(2,1)S(1)} async-done(((bf16[64,64,256]{2,1,0:T(8,128)(2,1)}), bf16[64,64,256]{2,1,0:T(8,128)(2,1)S(1)}, u32[]{:S(2)}, u32[]{:S(2)}) %all-to-all-start.1) | async-done | bytes 2097184 | tf_op jit(solution)/shard_map/all_to_all | solution.py:567
  123.2 5.8 %all-to-all-start.3 = ((bf16[64,64,128]{2,1,0:T(8,128)(2,1)}), bf16[64,64,128]{2,1,0:T(8,128)(2,1)S(1)}, u32[]{:S(2)}, u32[]{:S(2)}) async-start(bf16[64,64,128]{2,1,0:T(8,128)(2,1)} %bitcast.25), calls=%async_computation.3 | async-start | bytes 2097152 | tf_op jit(solution)/shard_map/all_to_all | solution.py:570
  129.1 1.1 copy-done.6
  130.2 25.9 %triplets.2 = bf16[2,2048,256]{2,1,0:T(8,128)(2,1)S(1)} custom-call(s32[1,4096]{1,0:T(1,128)S(1)} %bitcast.29, s32[1,4096]{1,0:T(1,128)S(1)} %bitcast.31, s32[1,4096]{1,0:T(1,128)S(1)} %bitcast.33, f32[42,4096]{1,0:T(8,128)S(1)} %copy-done.6, bf16[144,256]{1,0:T(8,128)(2,1)S(1)} %slice.8.weight_ref, bf16[4096,256]{1,0:T(8,128)(2,1)S(1)} %bitcast.21), custom_call_target="tpu_custom_call" | custom-call | flops 17179869184 | bytes 4608000 | tf_op jit(solution)/shard_map/triplets/pallas_call | solution.py:225
  156.1 1.3 copy-done.2
  157.4 0.2 all-to-all-done.3
  157.6 10.1 %all-to-all-start.2 = ((bf16[64,64,256]{2,1,0:T(8,128)(2,1)}), bf16[64,64,256]{2,1,0:T(8,128)(2,1)S(1)}, u32[]{:S(2)}, u32[]{:S(2)}) async-start(bf16[64,64,256]{2,1,0:T(8,128)(2,1)} %bitcast.22), calls=%async_computation.2 | async-start | bytes 4194304 | tf_op jit(solution)/shard_map/all_to_all | solution.py:571
  167.8 1.0 collective-permute-start.9
  168.8 2.1 collective-permute-start.10
  170.9 1.3 collective-permute-start.11
  172.2 1.9 edges.2
  174.1 44.9 %all-to-all-done.2 = bf16[64,64,256]{2,1,0:T(8,128)(2,1)S(1)} async-done(((bf16[64,64,256]{2,1,0:T(8,128)(2,1)}), bf16[64,64,256]{2,1,0:T(8,128)(2,1)S(1)}, u32[]{:S(2)}, u32[]{:S(2)}) %all-to-all-start.2) | async-done | bytes 2097184 | tf_op jit(solution)/shard_map/all_to_all | solution.py:571
  219.0 2.0 edges.3
  221.0 1.0 collective-permute-start.6
  222.1 2.1 collective-permute-start.7
  224.2 1.3 collective-permute-start.8
  225.5 0.8 collective-permute-done.6.refs_1_
  226.3 2.5 collective-permute-done.7.refs_2_
  228.8 0.2 collective-permute-done.8.refs_3_
  229.0 12.7 %layers.1 = (bf16[128,384]{1,0:T(8,128)(2,1)S(1)}, bf16[128,384]{1,0:T(8,128)(2,1)S(1)}, bf16[128,384]{1,0:T(8,128)(2,1)S(1)}, bf16[128,384]{1,0:T(8,128)(2,1)S(1)}) custom-call(s32[1]{0:T(128)} %bitcast.mp_ref, bf16[128,384]{1,0:T(8,128)(2,1)S(1)} %get-tuple-element.41.refs_0_, bf16[128,384]{1,0:T(8,128)(2,1)S(1)} %collective-permute-done.6.refs_1_, ...), custom_call_target="tpu_custom_call" | custom-call | flops 3623878656 | bytes 28311552 | tf_op jit(solution)/shard_map/layers/pallas_call | solution.py:378
  241.7 2.1 collective-permute-start.12
  243.8 1.8 collective-permute-start.13
  245.6 0.7 collective-permute-start.14
  246.3 0.2 collective-permute-done.12.h1
  246.5 2.9 collective-permute-done.13.h2
  249.4 1.0 collective-permute-done.14.h3
  250.4 2.4 atoms.1
  252.8 1.7 collective-permute-start.15
  254.5 1.9 collective-permute-done.15.got_ref
  256.4 0.2 meet.1
  256.6 1.6 collective-permute-start.18
  258.2 1.2 collective-permute-start.17
  259.4 3.4 %collective-permute-done.18 = bf16[256,384]{1,0:T(8,128)(2,1)S(1)} collective-permute-done((bf16[256,384]{1,0:T(8,128)(2,1)S(1)}, bf16[256,384]{1,0:T(8,128)(2,1)S(1)}, u32[]{:S(2)}, u32[]{:S(2)}) %collective-permute-start.18) | collective-permute-done | bytes 196640 | tf_op jit(solution)/shard_map/ppermute | solution.py:501
  262.8 2.8 collective-permute-done.17
  265.5 5.2 %collective-permute-done.16 = bf16[256,384]{1,0:T(8,128)(2,1)S(1)} collective-permute-done((bf16[256,384]{1,0:T(8,128)(2,1)S(1)}, bf16[256,384]{1,0:T(8,128)(2,1)S(1)}, u32[]{:S(2)}, u32[]{:S(2)}) %collective-permute-start.16) | collective-permute-done | bytes 196640 | tf_op jit(solution)/shard_map/ppermute | solution.py:501
  270.7 0.1 add_convert_fusion
  270.8 11.7 %all_to_all.35 = bf16[8,32,384]{2,1,0:T(8,128)(2,1)S(1)} all-to-all(bf16[8,32,384]{2,1,0:T(8,128)(2,1)S(1)} %bitcast.38), channel_id=1, replica_groups=mesh['graph_0'=4,'graph_1'=8,'graph_2'=2,'mp'=4] {'graph_1'}, dimensions={0} | all-to-all | bytes 393216 | tf_op jit(solution)/shard_map/all_to_all | solution.py:583
  282.6 11.3 %all_to_all.36 = bf16[8,32,384]{2,1,0:T(8,128)(2,1)S(1)} all-to-all(bf16[8,32,384]{2,1,0:T(8,128)(2,1)S(1)} %broadcast_in_dim.25), channel_id=1, replica_groups=mesh['graph_0'=4,'graph_1'=8,'graph_2'=2,'mp'=4] {'graph_1'}, dimensions={0} | all-to-all | bytes 393216 | tf_op jit(solution)/shard_map/all_to_all | solution.py:585
  294.0 11.6 %all_to_all.37 = bf16[4,256,384]{2,1,0:T(8,128)(2,1)S(1)} all-to-all(bf16[4,256,384]{2,1,0:T(8,128)(2,1)S(1)} %broadcast_in_dim.27), channel_id=1, replica_groups=mesh['graph_0'=4,'graph_1'=8,'graph_2'=2,'mp'=4] {'graph_0'}, dimensions={0} | all-to-all | bytes 1572864 | tf_op jit(solution)/shard_map/all_to_all | solution.py:588
  305.6 4.1 %collective-permute-start.19 = (bf16[1024,384]{1,0:T(8,128)(2,1)S(1)}, bf16[1024,384]{1,0:T(8,128)(2,1)S(1)}, u32[]{:S(2)}, u32[]{:S(2)}) collective-permute-start(bf16[1024,384]{1,0:T(8,128)(2,1)S(1)} %bitcast.26), channel_id=1, source_target_pairs={{0,4},{4,0},{1,5},{5,1},{2,6},{6,2},{3,7},{7,3},{8,12},{12,8},{9,1... | collective-permute-start | bytes 2359304 | tf_op jit(solution)/shard_map/ppermute | solution.py:501
  309.6 1.9 collective-permute-done.19.other_ref
  311.5 2.5 final.1
  (45 shorter events, 0.4 us)
Async XLA Ops:
  7.2 29.9 %copy-start = (bf16[384,384]{1,0:T(8,128)(2,1)S(1)}, bf16[384,384]{1,0:T(8,128)(2,1)}, u32[]{:S(2)}) copy-start(bf16[384,384]{1,0:T(8,128)(2,1)} %param.15) | copy-start | bytes 884740
  9.5 6.7 %collective-permute-start = (bf16[512,128]{1,0:T(8,128)(2,1)}, bf16[512,128]{1,0:T(8,128)(2,1)S(1)}, u32[]{:S(2)}, u32[]{:S(2)}) collective-permute-start(bf16[512,128]{1,0:T(8,128)(2,1)} %get-tuple-element.31.a_ref), channel_id=1, source_target_pairs={{0,1},{1,2},{2,3},{3,0},{4,5},{5,6},{6,7},{7,4},{8,9},{9,10},{10,1... | collective-permute-start | bytes 393224 | tf_op jit(solution)/shard_map/ppermute | solution.py:501
  11.6 8.5 %collective-permute-start.1 = (bf16[512,128]{1,0:T(8,128)(2,1)}, bf16[512,128]{1,0:T(8,128)(2,1)S(1)}, u32[]{:S(2)}, u32[]{:S(2)}) collective-permute-start(bf16[512,128]{1,0:T(8,128)(2,1)} %get-tuple-element.31.a_ref), channel_id=1, source_target_pairs={{0,2},{1,3},{2,0},{3,1},{4,6},{5,7},{6,4},{7,5},{8,10},{9,11},{10,... | collective-permute-start | bytes 393224 | tf_op jit(solution)/shard_map/ppermute | solution.py:501
  14.2 5.9 %collective-permute-start.2 = (bf16[512,128]{1,0:T(8,128)(2,1)}, bf16[512,128]{1,0:T(8,128)(2,1)S(1)}, u32[]{:S(2)}, u32[]{:S(2)}) collective-permute-start(bf16[512,128]{1,0:T(8,128)(2,1)} %get-tuple-element.31.a_ref), channel_id=1, source_target_pairs={{0,3},{1,0},{2,1},{3,2},{4,7},{5,4},{6,5},{7,6},{8,11},{9,8},{10,9... | collective-permute-start | bytes 393224 | tf_op jit(solution)/shard_map/ppermute | solution.py:501
  20.2 0.9 copy-start.8
  24.0 41.6 %all-to-all-start = ((bf16[64,64,128]{2,1,0:T(8,128)(2,1)}), bf16[64,64,128]{2,1,0:T(8,128)(2,1)S(1)}, u32[]{:S(2)}, u32[]{:S(2)}) async-start(bf16[64,64,128]{2,1,0:T(8,128)(2,1)} %bitcast.6), calls=%async_computation | async-start | bytes 2097152 | tf_op jit(solution)/shard_map/all_to_all | solution.py:564
  37.0 191.9 %all-gather.3.cloned.1.call-start = ((), (), s32[]{:S(2)}) async-start(), calls=%async_computation.7 | async-start | bytes 33177600 | tf_op jit(solution)/shard_map/all_gather | solution.py:568
  37.1 2.4 copy-start.7
  39.6 8.7 %collective-permute-start.3 = (bf16[512,256]{1,0:T(8,128)(2,1)S(1)}, bf16[512,256]{1,0:T(8,128)(2,1)S(1)}, u32[]{:S(2)}, u32[]{:S(2)}) collective-permute-start(bf16[512,256]{1,0:T(8,128)(2,1)S(1)} %copy-done.7), channel_id=1, source_target_pairs={{0,1},{1,2},{2,3},{3,0},{4,5},{5,6},{6,7},{7,4},{8,9},{9,10},{10,1... | collective-permute-start | bytes 786440 | tf_op jit(solution)/shard_map/ppermute | solution.py:501
  40.6 13.7 %collective-permute-start.4 = (bf16[512,256]{1,0:T(8,128)(2,1)S(1)}, bf16[512,256]{1,0:T(8,128)(2,1)S(1)}, u32[]{:S(2)}, u32[]{:S(2)}) collective-permute-start(bf16[512,256]{1,0:T(8,128)(2,1)S(1)} %copy-done.7), channel_id=1, source_target_pairs={{0,2},{1,3},{2,0},{3,1},{4,6},{5,7},{6,4},{7,5},{8,10},{9,11},{10,... | collective-permute-start | bytes 786440 | tf_op jit(solution)/shard_map/ppermute | solution.py:501
  42.7 11.6 %collective-permute-start.5 = (bf16[512,256]{1,0:T(8,128)(2,1)S(1)}, bf16[512,256]{1,0:T(8,128)(2,1)S(1)}, u32[]{:S(2)}, u32[]{:S(2)}) collective-permute-start(bf16[512,256]{1,0:T(8,128)(2,1)S(1)} %copy-done.7), channel_id=1, source_target_pairs={{0,3},{1,0},{2,1},{3,2},{4,7},{5,4},{6,5},{7,6},{8,11},{9,8},{10,9... | collective-permute-start | bytes 786440 | tf_op jit(solution)/shard_map/ppermute | solution.py:501
  65.6 6.4 %copy-start.14 = (f32[42,384]{1,0:T(8,128)S(1)}, f32[42,384]{1,0:T(8,128)}, u32[]{:S(2)}) copy-start(f32[42,384]{1,0:T(8,128)} %param.14) | copy-start | bytes 193540
  65.6 6.5 %copy-start.9 = (s32[4096]{0:T(1024)S(1)}, s32[4096]{0:T(1024)}, u32[]{:S(2)}) copy-start(s32[4096]{0:T(1024)} %param.18) | copy-start | bytes 49156
  65.6 6.5 %copy-start.10 = (s32[4096]{0:T(1024)S(1)}, s32[4096]{0:T(1024)}, u32[]{:S(2)}) copy-start(s32[4096]{0:T(1024)} %param.20) | copy-start | bytes 49156
  65.6 6.5 %copy-start.11 = (s32[4096]{0:T(1024)S(1)}, s32[4096]{0:T(1024)}, u32[]{:S(2)}) copy-start(s32[4096]{0:T(1024)} %param.19) | copy-start | bytes 49156
  65.6 57.6 %all-to-all-start.1 = ((bf16[64,64,256]{2,1,0:T(8,128)(2,1)}), bf16[64,64,256]{2,1,0:T(8,128)(2,1)S(1)}, u32[]{:S(2)}, u32[]{:S(2)}) async-start(bf16[64,64,256]{2,1,0:T(8,128)(2,1)} %bitcast.7), calls=%async_computation.1 | async-start | bytes 4194304 | tf_op jit(solution)/shard_map/all_to_all | solution.py:567
  72.1 1.1 copy-start.5
  88.2 1.0 copy-start.3
  123.2 34.4 %all-to-all-start.3 = ((bf16[64,64,128]{2,1,0:T(8,128)(2,1)}), bf16[64,64,128]{2,1,0:T(8,128)(2,1)S(1)}, u32[]{:S(2)}, u32[]{:S(2)}) async-start(bf16[64,64,128]{2,1,0:T(8,128)(2,1)} %bitcast.25), calls=%async_computation.3 | async-start | bytes 2097152 | tf_op jit(solution)/shard_map/all_to_all | solution.py:570
  129.1 1.1 copy-start.6
  156.1 1.3 copy-start.2
  157.6 61.4 %all-to-all-start.2 = ((bf16[64,64,256]{2,1,0:T(8,128)(2,1)}), bf16[64,64,256]{2,1,0:T(8,128)(2,1)S(1)}, u32[]{:S(2)}, u32[]{:S(2)}) async-start(bf16[64,64,256]{2,1,0:T(8,128)(2,1)} %bitcast.22), calls=%async_computation.2 | async-start | bytes 4194304 | tf_op jit(solution)/shard_map/all_to_all | solution.py:571
  167.8 61.2 %copy-start.4 = (bf16[128,384]{1,0:T(8,128)(2,1)S(1)}, bf16[128,384]{1,0:T(8,128)(2,1)}, u32[]{:S(2)}) copy-start(bf16[128,384]{1,0:T(8,128)(2,1)} %get-tuple-element.45.refs_4_) | copy-start | bytes 294916
  167.8 56.4 %collective-permute-start.9 = (bf16[128,384]{1,0:T(8,128)(2,1)}, bf16[128,384]{1,0:T(8,128)(2,1)}, u32[]{:S(2)}, u32[]{:S(2)}) collective-permute-start(bf16[128,384]{1,0:T(8,128)(2,1)} %get-tuple-element.46), channel_id=1, source_target_pairs={{0,1},{1,2},{2,3},{3,0},{4,5},{5,6},{6,7},{7,4},{8,9},{9,10},{10,1... | collective-permute-start | bytes 294920 | tf_op jit(solution)/shard_map/ppermute | solution.py:501
  168.8 56.7 %collective-permute-start.10 = (bf16[128,384]{1,0:T(8,128)(2,1)}, bf16[128,384]{1,0:T(8,128)(2,1)}, u32[]{:S(2)}, u32[]{:S(2)}) collective-permute-start(bf16[128,384]{1,0:T(8,128)(2,1)} %get-tuple-element.47), channel_id=1, source_target_pairs={{0,2},{1,3},{2,0},{3,1},{4,6},{5,7},{6,4},{7,5},{8,10},{9,11},{10,... | collective-permute-start | bytes 294920 | tf_op jit(solution)/shard_map/ppermute | solution.py:501
  170.9 54.6 %collective-permute-start.11 = (bf16[128,384]{1,0:T(8,128)(2,1)}, bf16[128,384]{1,0:T(8,128)(2,1)}, u32[]{:S(2)}, u32[]{:S(2)}) collective-permute-start(bf16[128,384]{1,0:T(8,128)(2,1)} %get-tuple-element.48), channel_id=1, source_target_pairs={{0,3},{1,0},{2,1},{3,2},{4,7},{5,4},{6,5},{7,6},{8,11},{9,8},{10,9... | collective-permute-start | bytes 294920 | tf_op jit(solution)/shard_map/ppermute | solution.py:501
  221.0 5.3 %collective-permute-start.6 = (bf16[128,384]{1,0:T(8,128)(2,1)S(1)}, bf16[128,384]{1,0:T(8,128)(2,1)S(1)}, u32[]{:S(2)}, u32[]{:S(2)}) collective-permute-start(bf16[128,384]{1,0:T(8,128)(2,1)S(1)} %get-tuple-element.42), channel_id=1, source_target_pairs={{0,1},{1,2},{2,3},{3,0},{4,5},{5,6},{6,7},{7,4},{8,9},{9,10},{10,1... | collective-permute-start | bytes 294920 | tf_op jit(solution)/shard_map/ppermute | solution.py:501
  222.1 6.7 %collective-permute-start.7 = (bf16[128,384]{1,0:T(8,128)(2,1)S(1)}, bf16[128,384]{1,0:T(8,128)(2,1)S(1)}, u32[]{:S(2)}, u32[]{:S(2)}) collective-permute-start(bf16[128,384]{1,0:T(8,128)(2,1)S(1)} %get-tuple-element.43), channel_id=1, source_target_pairs={{0,2},{1,3},{2,0},{3,1},{4,6},{5,7},{6,4},{7,5},{8,10},{9,11},{10,... | collective-permute-start | bytes 294920 | tf_op jit(solution)/shard_map/ppermute | solution.py:501
  224.2 4.8 %collective-permute-start.8 = (bf16[128,384]{1,0:T(8,128)(2,1)S(1)}, bf16[128,384]{1,0:T(8,128)(2,1)S(1)}, u32[]{:S(2)}, u32[]{:S(2)}) collective-permute-start(bf16[128,384]{1,0:T(8,128)(2,1)S(1)} %get-tuple-element.44), channel_id=1, source_target_pairs={{0,3},{1,0},{2,1},{3,2},{4,7},{5,4},{6,5},{7,6},{8,11},{9,8},{10,9... | collective-permute-start | bytes 294920 | tf_op jit(solution)/shard_map/ppermute | solution.py:501
  229.0 21.4 %copy-start.12 = (s32[512]{0:T(512)S(1)}, s32[512]{0:T(512)}, u32[]{:S(2)}) copy-start(s32[512]{0:T(512)} %param.21) | copy-start | bytes 6148
  241.7 4.8 %collective-permute-start.12 = (bf16[128,384]{1,0:T(8,128)(2,1)S(1)}, bf16[128,384]{1,0:T(8,128)(2,1)S(1)}, u32[]{:S(2)}, u32[]{:S(2)}) collective-permute-start(bf16[128,384]{1,0:T(8,128)(2,1)S(1)} %get-tuple-element.51), channel_id=1, source_target_pairs={{0,1},{1,2},{2,3},{3,0},{4,5},{5,6},{6,7},{7,4},{8,9},{9,10},{10,1... | collective-permute-start | bytes 294920 | tf_op jit(solution)/shard_map/ppermute | solution.py:501
  243.8 5.6 %collective-permute-start.13 = (bf16[128,384]{1,0:T(8,128)(2,1)S(1)}, bf16[128,384]{1,0:T(8,128)(2,1)S(1)}, u32[]{:S(2)}, u32[]{:S(2)}) collective-permute-start(bf16[128,384]{1,0:T(8,128)(2,1)S(1)} %get-tuple-element.52), channel_id=1, source_target_pairs={{0,2},{1,3},{2,0},{3,1},{4,6},{5,7},{6,4},{7,5},{8,10},{9,11},{10,... | collective-permute-start | bytes 294920 | tf_op jit(solution)/shard_map/ppermute | solution.py:501
  245.6 4.8 %collective-permute-start.14 = (bf16[128,384]{1,0:T(8,128)(2,1)S(1)}, bf16[128,384]{1,0:T(8,128)(2,1)S(1)}, u32[]{:S(2)}, u32[]{:S(2)}) collective-permute-start(bf16[128,384]{1,0:T(8,128)(2,1)S(1)} %get-tuple-element.53), channel_id=1, source_target_pairs={{0,3},{1,0},{2,1},{3,2},{4,7},{5,4},{6,5},{7,6},{8,11},{9,8},{10,9... | collective-permute-start | bytes 294920 | tf_op jit(solution)/shard_map/ppermute | solution.py:501
  252.8 3.6 %collective-permute-start.15 = (bf16[1024,384]{1,0:T(8,128)(2,1)S(1)}, bf16[1024,384]{1,0:T(8,128)(2,1)S(1)}, u32[]{:S(2)}, u32[]{:S(2)}) collective-permute-start(bf16[1024,384]{1,0:T(8,128)(2,1)S(1)} %get-tuple-element.55), channel_id=1, source_target_pairs={{0,4},{4,0},{1,5},{5,1},{2,6},{6,2},{3,7},{7,3},{8,12},{12,8},{9,1... | collective-permute-start | bytes 2359304 | tf_op jit(solution)/shard_map/ppermute | solution.py:501
  256.6 6.2 %collective-permute-start.18 = (bf16[256,384]{1,0:T(8,128)(2,1)S(1)}, bf16[256,384]{1,0:T(8,128)(2,1)S(1)}, u32[]{:S(2)}, u32[]{:S(2)}) collective-permute-start(bf16[256,384]{1,0:T(8,128)(2,1)S(1)} %get-tuple-element.59), channel_id=1, source_target_pairs={{0,192},{64,0},{128,64},{192,128},{1,193},{65,1},{129,65},{193,129... | collective-permute-start | bytes 589832 | tf_op jit(solution)/shard_map/ppermute | solution.py:501
  258.2 7.3 %collective-permute-start.17 = (bf16[256,384]{1,0:T(8,128)(2,1)S(1)}, bf16[256,384]{1,0:T(8,128)(2,1)S(1)}, u32[]{:S(2)}, u32[]{:S(2)}) collective-permute-start(bf16[256,384]{1,0:T(8,128)(2,1)S(1)} %get-tuple-element.58), channel_id=1, source_target_pairs={{0,128},{64,192},{128,0},{192,64},{1,129},{65,193},{129,1},{193,65... | collective-permute-start | bytes 589832 | tf_op jit(solution)/shard_map/ppermute | solution.py:501
  259.4 11.4 %collective-permute-start.16 = (bf16[256,384]{1,0:T(8,128)(2,1)S(1)}, bf16[256,384]{1,0:T(8,128)(2,1)S(1)}, u32[]{:S(2)}, u32[]{:S(2)}) collective-permute-start(bf16[256,384]{1,0:T(8,128)(2,1)S(1)} %get-tuple-element.57), channel_id=1, source_target_pairs={{0,64},{64,128},{128,192},{192,0},{1,65},{65,129},{129,193},{193,1... | collective-permute-start | bytes 589832 | tf_op jit(solution)/shard_map/ppermute | solution.py:501
  270.7 43.3 %copy-start.1 = (bf16[384,384]{1,0:T(8,128)(2,1)S(1)}, bf16[384,384]{1,0:T(8,128)(2,1)}, u32[]{:S(2)}) copy-start(bf16[384,384]{1,0:T(8,128)(2,1)} %param.15) | copy-start | bytes 884740
  282.6 31.5 %copy-start.13 = (bf16[32,384]{1,0:T(8,128)(2,1)}, bf16[32,384]{1,0:T(8,128)(2,1)S(1)}, u32[]{:S(2)}) copy-start(bf16[32,384]{1,0:T(8,128)(2,1)S(1)} %multiply_convert_fusion) | copy-start | bytes 73732
  305.6 6.0 %collective-permute-start.19 = (bf16[1024,384]{1,0:T(8,128)(2,1)S(1)}, bf16[1024,384]{1,0:T(8,128)(2,1)S(1)}, u32[]{:S(2)}, u32[]{:S(2)}) collective-permute-start(bf16[1024,384]{1,0:T(8,128)(2,1)S(1)} %bitcast.26), channel_id=1, source_target_pairs={{0,4},{4,0},{1,5},{5,1},{2,6},{6,2},{3,7},{7,3},{8,12},{12,8},{9,1... | collective-permute-start | bytes 2359304 | tf_op jit(solution)/shard_map/ppermute | solution.py:501
Sparse Core Ops, SparseCore 0:
  65.8 142.2 all-gather.2

commit v7 on v6

--- a/solution.py
+++ b/solution.py
@@ -29,7 +29,7 @@
 ATOMS = ATOM_DEV * N_GRAPH
 HALF_ATOMS = ATOMS // N_CORE
 BLOCK = 512
-ATOM_BLOCK = 256
+ATOM_BLOCK = 512
 PARTS = ((0, 128), (128, 384))
 
 F32 = jnp.float32
@@ -58,8 +58,11 @@
 
 def picks_of(column, count):
     lane = lax.broadcasted_iota(I32, column.shape, 1)
+    low = ones_where((column & 127) == lane)
+    high = (column >> 7).astype(F32).astype(BF16)
+    none = jnp.zeros_like(low)
     return jnp.concatenate(
-        [ones_where(column == lane + k) for k in range(0, count, 128)], axis=1
+        [jnp.where(high == k, low, none) for k in range(count // 128)], axis=1
     )
 
 
@@ -68,9 +71,12 @@
 
 
 def members(row, count, first):
-    place = lax.broadcasted_iota(I32, (count, 128), 0) + first
+    shape = (128, row.shape[1])
+    local = jnp.broadcast_to(row - first, shape)
+    low = ones_where((local & 127) == lax.broadcasted_iota(I32, shape, 0))
+    high = local >> 7
     return jnp.concatenate(
-        [ones_where(place == row[:, k : k + 128]) for k in range(0, row.shape[1], 128)], axis=1
+        [low * ones_where(high == k) for k in range(count // 128)], axis=0
     )
 
 
@@ -303,6 +309,7 @@
 
 WIDE = 2 * COLS
 AHEAD = 6
+AHEAD = 6
 
 
 def layers_kernel(mp_ref, *refs):
@@ -419,7 +426,7 @@
             out_ref[pl.ds(first, ATOM_BLOCK), :] = part.astype(BF16)
             return carry
 
-        lax.fori_loop(0, HALF_ATOMS // ATOM_BLOCK, one, 0)
+        lax.fori_loop(0, HALF_ATOMS // ATOM_BLOCK, one, 0, unroll=True)
 
 
 def atoms(mp, core, edge_atom, hiddens):
@@ -462,22 +469,17 @@
 def final_kernel(mp_ref, core_ref, atom_ref, h0, h1, h2, h3, mine_ref, other_ref, out_ref):
     me, core = mp_ref[0], core_ref[0]
     for k, hidden_ref in enumerate((h0, h1, h2, h3)):
-        place = lax.rem(me + N_MP - k, N_MP) * ROWS
-        out_ref[pl.ds(pl.multiple_of(place, ROWS), ROWS), :] = hidden_ref[...]
-
-    def one(i, carry):
-        rows = pl.ds(pl.multiple_of(i * ROWS, ROWS), ROWS)
-        row = atom_ref[:, rows]
+        row = at_block(atom_ref, me, k)
         group = row // ATOM_DEV
         spot = (group // N_CORE) * ATOM_DEV + row % ATOM_DEV
         near = jnp.where(group % N_CORE == core, spot, -1)
         far = jnp.where(group % N_CORE == core, -1, spot)
         taken = product(picks(near, HALF_ATOMS), mine_ref[...])
         taken = taken + product(picks(far, HALF_ATOMS), other_ref[...])
-        out_ref[rows, :] = (out_ref[rows, :].astype(F32) + taken).astype(BF16)
-        return carry
-
-    lax.fori_loop(0, N_MP, one, 0, unroll=2)
+        place = lax.rem(me + N_MP - k, N_MP) * ROWS
+        out_ref[pl.ds(pl.multiple_of(place, ROWS), ROWS), :] = (
+            hidden_ref[...].astype(F32) + taken
+        ).astype(BF16)
 
 
 def final(mp, core, edge_atom, hiddens, mine, other):

time: 322 us -> 320 us (level)
  no operation moved by 1% of the time
where the time goes in v7:
time: 320 us; the launch traced here: 319 us
  waiting for transfers between devices  123 us (38%)
  Pallas kernels  69 us (22%)
  starting transfers between devices  67 us (21%)
  blocking collectives  34.5 us (11%)
  between operations  14.3 us (4%)
  local copies, waits for them, and re-layouts  8.85 us (3%)
    all_to_all x1, waiting for transfers between devices, local(): second = exchange(sums(second, PARTS[1]))  44.9 us
    pallas_call x2, Pallas kernels, triplets(): pl.pallas_call(functools.partial(triplet_kernel, groups), grid=(TRIP_STEP...  40.3 us
    ppermute x20, waiting for transfers between devices, turn(): lax.ppermute(array, axis, [(i, (i + shift) % count) for i in range(count)])  34.9 us
    all_to_all x1, waiting for transfers between devices, local(): second = exchange(second)  34.1 us
    ppermute x20, starting transfers between devices, turn(): lax.ppermute(array, axis, [(i, (i + shift) % count) for i in range(count)])  32.2 us
    all_to_all x1, starting transfers between devices, local(): first = exchange(first)  13 us
    pallas_call x1, Pallas kernels, layers(): pl.pallas_call(layers_kernel, in_specs=[SCALAR] + [vmem] * (2 * N_MP) + [...  12.7 us
    all_to_all x1, blocking collectives, local(): atom_sum = summed(lax.all_to_all(part, 'graph_1', 0, 0, tiled=True))  11.7 us
  transfers between devices with their start and end apart: 25, of which 18 were waited for; matrix products, arithmetic and copies ran while one was open for 2% of the time, Pallas kernels for 14%

profile of v7, /device:TPU:1, one launch (start us, length us, event | category | flops | bytes accessed | tf_op | source)
XLA Modules:
  0.0 318.8 jit_solution(1409419124156817908)
XLA Ops:
  7.2 2.3 project.1
  9.5 2.1 collective-permute-start
  11.6 2.6 collective-permute-start.1
  14.2 1.1 collective-permute-start.2
  15.3 0.8 reshape.63.list_ref
  16.2 4.0 %collective-permute-done.1.c_ref = bf16[512,128]{1,0:T(8,128)(2,1)S(1)} collective-permute-done((bf16[512,128]{1,0:T(8,128)(2,1)}, bf16[512,128]{1,0:T(8,128)(2,1)S(1)}, u32[]{:S(2)}, u32[]{:S(2)}) %collective-permute-start.1) | collective-permute-done | bytes 131104 | tf_op jit(solution)/shard_map/ppermute | solution.py:503
  20.2 0.9 copy-done.8
  21.1 3.0 send.2
  24.0 13.0 %all-to-all-start = ((bf16[64,64,128]{2,1,0:T(8,128)(2,1)}), bf16[64,64,128]{2,1,0:T(8,128)(2,1)S(1)}, u32[]{:S(2)}, u32[]{:S(2)}) async-start(bf16[64,64,128]{2,1,0:T(8,128)(2,1)} %bitcast.6), calls=%async_computation | async-start | bytes 2097152 | tf_op jit(solution)/shard_map/all_to_all | solution.py:566
  37.2 2.4 constant_dynamic-slice_fusion.1
  39.6 1.0 collective-permute-start.3
  40.6 2.1 collective-permute-start.4
  42.7 1.3 collective-permute-start.5
  44.0 2.2 pad_maximum_fusion
  46.2 2.1 collective-permute-done.3.b_ref
  48.3 6.0 %collective-permute-done.4.c_ref = bf16[512,256]{1,0:T(8,128)(2,1)S(1)} collective-permute-done((bf16[512,256]{1,0:T(8,128)(2,1)S(1)}, bf16[512,256]{1,0:T(8,128)(2,1)S(1)}, u32[]{:S(2)}, u32[]{:S(2)}) %collective-permute-start.4) | collective-permute-done | bytes 262176 | tf_op jit(solution)/shard_map/ppermute | solution.py:503
  54.3 3.2 %send.3 = bf16[4096,256]{1,0:T(8,128)(2,1)} custom-call(s32[1,4096]{1,0:T(1,128)S(1)} %reshape.63.list_ref, bf16[512,256]{1,0:T(8,128)(2,1)S(1)} %copy-done.7, bf16[512,256]{1,0:T(8,128)(2,1)S(1)} %collective-permute-done.3.b_ref, bf16[512,256]{1,0:T(8,128)(2,1)S(1)} %collective-permute-done.4.c_ref, bf16[512,256]{1,0:T(8,128)(2,1)S(1)} %collective-permute-done.5.d_ref), custom_call_target="tpu_custom_call" | custom-call | flops 1073741824 | bytes 3072000 | tf_op jit(solution)/shard_map/send/pallas_call | solution.py:140
  57.5 8.1 %all-to-all-done = bf16[64,64,128]{2,1,0:T(8,128)(2,1)S(1)} async-done(((bf16[64,64,128]{2,1,0:T(8,128)(2,1)}), bf16[64,64,128]{2,1,0:T(8,128)(2,1)S(1)}, u32[]{:S(2)}, u32[]{:S(2)}) %all-to-all-start) | async-done | bytes 1048608 | tf_op jit(solution)/shard_map/all_to_all | solution.py:566
  65.7 6.3 %all-to-all-start.1 = ((bf16[64,64,256]{2,1,0:T(8,128)(2,1)}), bf16[64,64,256]{2,1,0:T(8,128)(2,1)S(1)}, u32[]{:S(2)}, u32[]{:S(2)}) async-start(bf16[64,64,256]{2,1,0:T(8,128)(2,1)} %bitcast.7), calls=%async_computation.1 | async-start | bytes 4194304 | tf_op jit(solution)/shard_map/all_to_all | solution.py:569
  72.1 1.1 copy-done.5
  73.3 14.9 %triplets.3 = bf16[4,1024,128]{2,1,0:T(8,128)(2,1)S(1)} custom-call(s32[1,4096]{1,0:T(1,128)S(1)} %bitcast.28, s32[1,4096]{1,0:T(1,128)S(1)} %bitcast.30, s32[1,4096]{1,0:T(1,128)S(1)} %bitcast.32, f32[42,4096]{1,0:T(8,128)S(1)} %copy-done.5, bf16[144,128]{1,0:T(8,128)(2,1)S(1)} %slice.9.weight_ref, bf16[4096,128]{1,0:T(8,128)(2,1)S(1)} %bitcast.23), custom_call_target="tpu_custom_call" | custom-call | flops 8589934592 | bytes 2304000 | tf_op jit(solution)/shard_map/triplets/pallas_call | solution.py:231
  88.2 1.0 copy-done.3
  89.1 34.1 %all-to-all-done.1 = bf16[64,64,256]{2,1,0:T(8,128)(2,1)S(1)} async-done(((bf16[64,64,256]{2,1,0:T(8,128)(2,1)}), bf16[64,64,256]{2,1,0:T(8,128)(2,1)S(1)}, u32[]{:S(2)}, u32[]{:S(2)}) %all-to-all-start.1) | async-done | bytes 2097184 | tf_op jit(solution)/shard_map/all_to_all | solution.py:569
  123.3 5.8 %all-to-all-start.3 = ((bf16[64,64,128]{2,1,0:T(8,128)(2,1)}), bf16[64,64,128]{2,1,0:T(8,128)(2,1)S(1)}, u32[]{:S(2)}, u32[]{:S(2)}) async-start(bf16[64,64,128]{2,1,0:T(8,128)(2,1)} %bitcast.25), calls=%async_computation.3 | async-start | bytes 2097152 | tf_op jit(solution)/shard_map/all_to_all | solution.py:572
  129.1 1.1 copy-done.6
  130.2 25.4 %triplets.2 = bf16[2,2048,256]{2,1,0:T(8,128)(2,1)S(1)} custom-call(s32[1,4096]{1,0:T(1,128)S(1)} %bitcast.29, s32[1,4096]{1,0:T(1,128)S(1)} %bitcast.31, s32[1,4096]{1,0:T(1,128)S(1)} %bitcast.33, f32[42,4096]{1,0:T(8,128)S(1)} %copy-done.6, bf16[144,256]{1,0:T(8,128)(2,1)S(1)} %slice.8.weight_ref, bf16[4096,256]{1,0:T(8,128)(2,1)S(1)} %bitcast.21), custom_call_target="tpu_custom_call" | custom-call | flops 17179869184 | bytes 4608000 | tf_op jit(solution)/shard_map/triplets/pallas_call | solution.py:231
  155.6 1.3 copy-done.2
  156.9 0.7 all-to-all-done.3
  157.6 9.6 %all-to-all-start.2 = ((bf16[64,64,256]{2,1,0:T(8,128)(2,1)}), bf16[64,64,256]{2,1,0:T(8,128)(2,1)S(1)}, u32[]{:S(2)}, u32[]{:S(2)}) async-start(bf16[64,64,256]{2,1,0:T(8,128)(2,1)} %bitcast.22), calls=%async_computation.2 | async-start | bytes 4194304 | tf_op jit(solution)/shard_map/all_to_all | solution.py:573
  167.3 1.0 collective-permute-start.9
  168.3 2.1 collective-permute-start.10
  170.4 1.3 collective-permute-start.11
  171.7 1.9 edges.2
  173.6 44.9 %all-to-all-done.2 = bf16[64,64,256]{2,1,0:T(8,128)(2,1)S(1)} async-done(((bf16[64,64,256]{2,1,0:T(8,128)(2,1)}), bf16[64,64,256]{2,1,0:T(8,128)(2,1)S(1)}, u32[]{:S(2)}, u32[]{:S(2)}) %all-to-all-start.2) | async-done | bytes 2097184 | tf_op jit(solution)/shard_map/all_to_all | solution.py:573
  218.5 2.0 edges.3
  220.5 1.0 collective-permute-start.6
  221.6 2.1 collective-permute-start.7
  223.7 1.3 collective-permute-start.8
  225.0 0.8 collective-permute-done.6.refs_1_
  225.8 2.5 collective-permute-done.7.refs_2_
  228.3 0.2 collective-permute-done.8.refs_3_
  228.5 12.7 %layers.1 = (bf16[128,384]{1,0:T(8,128)(2,1)S(1)}, bf16[128,384]{1,0:T(8,128)(2,1)S(1)}, bf16[128,384]{1,0:T(8,128)(2,1)S(1)}, bf16[128,384]{1,0:T(8,128)(2,1)S(1)}) custom-call(s32[1]{0:T(128)} %bitcast.mp_ref, bf16[128,384]{1,0:T(8,128)(2,1)S(1)} %get-tuple-element.41.refs_0_, bf16[128,384]{1,0:T(8,128)(2,1)S(1)} %collective-permute-done.6.refs_1_, ...), custom_call_target="tpu_custom_call" | custom-call | flops 3623878656 | bytes 28311552 | tf_op jit(solution)/shard_map/layers/pallas_call | solution.py:385
  241.2 2.0 collective-permute-start.12
  243.3 1.8 collective-permute-start.13
  245.1 0.7 collective-permute-start.14
  245.8 0.2 collective-permute-done.12.h1
  246.0 2.9 collective-permute-done.13.h2
  248.9 1.0 collective-permute-done.14.h3
  249.9 1.3 atoms.1
  251.1 1.7 collective-permute-start.15
  252.8 1.9 collective-permute-done.15.got_ref
  254.7 0.2 meet.1
  254.9 1.6 collective-permute-start.18
  256.5 1.1 collective-permute-start.17
  257.7 3.4 %collective-permute-done.18 = bf16[256,384]{1,0:T(8,128)(2,1)S(1)} collective-permute-done((bf16[256,384]{1,0:T(8,128)(2,1)S(1)}, bf16[256,384]{1,0:T(8,128)(2,1)S(1)}, u32[]{:S(2)}, u32[]{:S(2)}) %collective-permute-start.18) | collective-permute-done | bytes 196640 | tf_op jit(solution)/shard_map/ppermute | solution.py:503
  261.1 2.8 collective-permute-done.17
  263.9 5.2 %collective-permute-done.16 = bf16[256,384]{1,0:T(8,128)(2,1)S(1)} collective-permute-done((bf16[256,384]{1,0:T(8,128)(2,1)S(1)}, bf16[256,384]{1,0:T(8,128)(2,1)S(1)}, u32[]{:S(2)}, u32[]{:S(2)}) %collective-permute-start.16) | collective-permute-done | bytes 196640 | tf_op jit(solution)/shard_map/ppermute | solution.py:503
  269.1 0.1 add_convert_fusion
  269.2 11.7 %all_to_all.35 = bf16[8,32,384]{2,1,0:T(8,128)(2,1)S(1)} all-to-all(bf16[8,32,384]{2,1,0:T(8,128)(2,1)S(1)} %bitcast.38), channel_id=1, replica_groups=mesh['graph_0'=4,'graph_1'=8,'graph_2'=2,'mp'=4] {'graph_1'}, dimensions={0} | all-to-all | bytes 393216 | tf_op jit(solution)/shard_map/all_to_all | solution.py:585
  281.0 11.3 %all_to_all.36 = bf16[8,32,384]{2,1,0:T(8,128)(2,1)S(1)} all-to-all(bf16[8,32,384]{2,1,0:T(8,128)(2,1)S(1)} %broadcast_in_dim.25), channel_id=1, replica_groups=mesh['graph_0'=4,'graph_1'=8,'graph_2'=2,'mp'=4] {'graph_1'}, dimensions={0} | all-to-all | bytes 393216 | tf_op jit(solution)/shard_map/all_to_all | solution.py:587
  292.3 11.6 %all_to_all.37 = bf16[4,256,384]{2,1,0:T(8,128)(2,1)S(1)} all-to-all(bf16[4,256,384]{2,1,0:T(8,128)(2,1)S(1)} %broadcast_in_dim.27), channel_id=1, replica_groups=mesh['graph_0'=4,'graph_1'=8,'graph_2'=2,'mp'=4] {'graph_0'}, dimensions={0} | all-to-all | bytes 1572864 | tf_op jit(solution)/shard_map/all_to_all | solution.py:590
  303.9 4.1 %collective-permute-start.19 = (bf16[1024,384]{1,0:T(8,128)(2,1)S(1)}, bf16[1024,384]{1,0:T(8,128)(2,1)S(1)}, u32[]{:S(2)}, u32[]{:S(2)}) collective-permute-start(bf16[1024,384]{1,0:T(8,128)(2,1)S(1)} %bitcast.26), channel_id=1, source_target_pairs={{0,4},{4,0},{1,5},{5,1},{2,6},{6,2},{3,7},{7,3},{8,12},{12,8},{9,1... | collective-permute-start | bytes 2359304 | tf_op jit(solution)/shard_map/ppermute | solution.py:503
  308.0 1.9 collective-permute-done.19.other_ref
  309.9 2.1 final.1
  (45 shorter events, 0.4 us)
Async XLA Ops:
  7.2 30.0 %copy-start = (bf16[384,384]{1,0:T(8,128)(2,1)S(1)}, bf16[384,384]{1,0:T(8,128)(2,1)}, u32[]{:S(2)}) copy-start(bf16[384,384]{1,0:T(8,128)(2,1)} %param.15) | copy-start | bytes 884740
  9.5 6.7 %collective-permute-start = (bf16[512,128]{1,0:T(8,128)(2,1)}, bf16[512,128]{1,0:T(8,128)(2,1)S(1)}, u32[]{:S(2)}, u32[]{:S(2)}) collective-permute-start(bf16[512,128]{1,0:T(8,128)(2,1)} %get-tuple-element.31.a_ref), channel_id=1, source_target_pairs={{0,1},{1,2},{2,3},{3,0},{4,5},{5,6},{6,7},{7,4},{8,9},{9,10},{10,1... | collective-permute-start | bytes 393224 | tf_op jit(solution)/shard_map/ppermute | solution.py:503
  11.6 8.5 %collective-permute-start.1 = (bf16[512,128]{1,0:T(8,128)(2,1)}, bf16[512,128]{1,0:T(8,128)(2,1)S(1)}, u32[]{:S(2)}, u32[]{:S(2)}) collective-permute-start(bf16[512,128]{1,0:T(8,128)(2,1)} %get-tuple-element.31.a_ref), channel_id=1, source_target_pairs={{0,2},{1,3},{2,0},{3,1},{4,6},{5,7},{6,4},{7,5},{8,10},{9,11},{10,... | collective-permute-start | bytes 393224 | tf_op jit(solution)/shard_map/ppermute | solution.py:503
  14.2 5.9 %collective-permute-start.2 = (bf16[512,128]{1,0:T(8,128)(2,1)}, bf16[512,128]{1,0:T(8,128)(2,1)S(1)}, u32[]{:S(2)}, u32[]{:S(2)}) collective-permute-start(bf16[512,128]{1,0:T(8,128)(2,1)} %get-tuple-element.31.a_ref), channel_id=1, source_target_pairs={{0,3},{1,0},{2,1},{3,2},{4,7},{5,4},{6,5},{7,6},{8,11},{9,8},{10,9... | collective-permute-start | bytes 393224 | tf_op jit(solution)/shard_map/ppermute | solution.py:503
  20.2 0.9 copy-start.8
  24.0 41.6 %all-to-all-start = ((bf16[64,64,128]{2,1,0:T(8,128)(2,1)}), bf16[64,64,128]{2,1,0:T(8,128)(2,1)S(1)}, u32[]{:S(2)}, u32[]{:S(2)}) async-start(bf16[64,64,128]{2,1,0:T(8,128)(2,1)} %bitcast.6), calls=%async_computation | async-start | bytes 2097152 | tf_op jit(solution)/shard_map/all_to_all | solution.py:566
  37.1 191.4 %all-gather.3.cloned.1.call-start = ((), (), s32[]{:S(2)}) async-start(), calls=%async_computation.7 | async-start | bytes 33177600 | tf_op jit(solution)/shard_map/all_gather | solution.py:570
  37.1 2.4 copy-start.7
  39.6 8.7 %collective-permute-start.3 = (bf16[512,256]{1,0:T(8,128)(2,1)S(1)}, bf16[512,256]{1,0:T(8,128)(2,1)S(1)}, u32[]{:S(2)}, u32[]{:S(2)}) collective-permute-start(bf16[512,256]{1,0:T(8,128)(2,1)S(1)} %copy-done.7), channel_id=1, source_target_pairs={{0,1},{1,2},{2,3},{3,0},{4,5},{5,6},{6,7},{7,4},{8,9},{9,10},{10,1... | collective-permute-start | bytes 786440 | tf_op jit(solution)/shard_map/ppermute | solution.py:503
  40.6 13.7 %collective-permute-start.4 = (bf16[512,256]{1,0:T(8,128)(2,1)S(1)}, bf16[512,256]{1,0:T(8,128)(2,1)S(1)}, u32[]{:S(2)}, u32[]{:S(2)}) collective-permute-start(bf16[512,256]{1,0:T(8,128)(2,1)S(1)} %copy-done.7), channel_id=1, source_target_pairs={{0,2},{1,3},{2,0},{3,1},{4,6},{5,7},{6,4},{7,5},{8,10},{9,11},{10,... | collective-permute-start | bytes 786440 | tf_op jit(solution)/shard_map/ppermute | solution.py:503
  42.7 11.6 %collective-permute-start.5 = (bf16[512,256]{1,0:T(8,128)(2,1)S(1)}, bf16[512,256]{1,0:T(8,128)(2,1)S(1)}, u32[]{:S(2)}, u32[]{:S(2)}) collective-permute-start(bf16[512,256]{1,0:T(8,128)(2,1)S(1)} %copy-done.7), channel_id=1, source_target_pairs={{0,3},{1,0},{2,1},{3,2},{4,7},{5,4},{6,5},{7,6},{8,11},{9,8},{10,9... | collective-permute-start | bytes 786440 | tf_op jit(solution)/shard_map/ppermute | solution.py:503
  65.6 6.4 %copy-start.14 = (f32[42,384]{1,0:T(8,128)S(1)}, f32[42,384]{1,0:T(8,128)}, u32[]{:S(2)}) copy-start(f32[42,384]{1,0:T(8,128)} %param.14) | copy-start | bytes 193540
  65.6 6.5 %copy-start.9 = (s32[4096]{0:T(1024)S(1)}, s32[4096]{0:T(1024)}, u32[]{:S(2)}) copy-start(s32[4096]{0:T(1024)} %param.18) | copy-start | bytes 49156
  65.6 6.5 %copy-start.10 = (s32[4096]{0:T(1024)S(1)}, s32[4096]{0:T(1024)}, u32[]{:S(2)}) copy-start(s32[4096]{0:T(1024)} %param.20) | copy-start | bytes 49156
  65.6 6.5 %copy-start.11 = (s32[4096]{0:T(1024)S(1)}, s32[4096]{0:T(1024)}, u32[]{:S(2)}) copy-start(s32[4096]{0:T(1024)} %param.19) | copy-start | bytes 49156
  65.7 57.6 %all-to-all-start.1 = ((bf16[64,64,256]{2,1,0:T(8,128)(2,1)}), bf16[64,64,256]{2,1,0:T(8,128)(2,1)S(1)}, u32[]{:S(2)}, u32[]{:S(2)}) async-start(bf16[64,64,256]{2,1,0:T(8,128)(2,1)} %bitcast.7), calls=%async_computation.1 | async-start | bytes 4194304 | tf_op jit(solution)/shard_map/all_to_all | solution.py:569
  72.1 1.1 copy-start.5
  88.1 1.0 copy-start.3
  123.3 34.4 %all-to-all-start.3 = ((bf16[64,64,128]{2,1,0:T(8,128)(2,1)}), bf16[64,64,128]{2,1,0:T(8,128)(2,1)S(1)}, u32[]{:S(2)}, u32[]{:S(2)}) async-start(bf16[64,64,128]{2,1,0:T(8,128)(2,1)} %bitcast.25), calls=%async_computation.3 | async-start | bytes 2097152 | tf_op jit(solution)/shard_map/all_to_all | solution.py:572
  129.1 1.1 copy-start.6
  155.6 1.3 copy-start.2
  157.6 60.9 %all-to-all-start.2 = ((bf16[64,64,256]{2,1,0:T(8,128)(2,1)}), bf16[64,64,256]{2,1,0:T(8,128)(2,1)S(1)}, u32[]{:S(2)}, u32[]{:S(2)}) async-start(bf16[64,64,256]{2,1,0:T(8,128)(2,1)} %bitcast.22), calls=%async_computation.2 | async-start | bytes 4194304 | tf_op jit(solution)/shard_map/all_to_all | solution.py:573
  167.3 61.2 %copy-start.4 = (bf16[128,384]{1,0:T(8,128)(2,1)S(1)}, bf16[128,384]{1,0:T(8,128)(2,1)}, u32[]{:S(2)}) copy-start(bf16[128,384]{1,0:T(8,128)(2,1)} %get-tuple-element.45.refs_4_) | copy-start | bytes 294916
  167.3 56.4 %collective-permute-start.9 = (bf16[128,384]{1,0:T(8,128)(2,1)}, bf16[128,384]{1,0:T(8,128)(2,1)}, u32[]{:S(2)}, u32[]{:S(2)}) collective-permute-start(bf16[128,384]{1,0:T(8,128)(2,1)} %get-tuple-element.46), channel_id=1, source_target_pairs={{0,1},{1,2},{2,3},{3,0},{4,5},{5,6},{6,7},{7,4},{8,9},{9,10},{10,1... | collective-permute-start | bytes 294920 | tf_op jit(solution)/shard_map/ppermute | solution.py:503
  168.3 56.7 %collective-permute-start.10 = (bf16[128,384]{1,0:T(8,128)(2,1)}, bf16[128,384]{1,0:T(8,128)(2,1)}, u32[]{:S(2)}, u32[]{:S(2)}) collective-permute-start(bf16[128,384]{1,0:T(8,128)(2,1)} %get-tuple-element.47), channel_id=1, source_target_pairs={{0,2},{1,3},{2,0},{3,1},{4,6},{5,7},{6,4},{7,5},{8,10},{9,11},{10,... | collective-permute-start | bytes 294920 | tf_op jit(solution)/shard_map/ppermute | solution.py:503
  170.4 54.6 %collective-permute-start.11 = (bf16[128,384]{1,0:T(8,128)(2,1)}, bf16[128,384]{1,0:T(8,128)(2,1)}, u32[]{:S(2)}, u32[]{:S(2)}) collective-permute-start(bf16[128,384]{1,0:T(8,128)(2,1)} %get-tuple-element.48), channel_id=1, source_target_pairs={{0,3},{1,0},{2,1},{3,2},{4,7},{5,4},{6,5},{7,6},{8,11},{9,8},{10,9... | collective-permute-start | bytes 294920 | tf_op jit(solution)/shard_map/ppermute | solution.py:503
  220.5 5.3 %collective-permute-start.6 = (bf16[128,384]{1,0:T(8,128)(2,1)S(1)}, bf16[128,384]{1,0:T(8,128)(2,1)S(1)}, u32[]{:S(2)}, u32[]{:S(2)}) collective-permute-start(bf16[128,384]{1,0:T(8,128)(2,1)S(1)} %get-tuple-element.42), channel_id=1, source_target_pairs={{0,1},{1,2},{2,3},{3,0},{4,5},{5,6},{6,7},{7,4},{8,9},{9,10},{10,1... | collective-permute-start | bytes 294920 | tf_op jit(solution)/shard_map/ppermute | solution.py:503
  221.6 6.7 %collective-permute-start.7 = (bf16[128,384]{1,0:T(8,128)(2,1)S(1)}, bf16[128,384]{1,0:T(8,128)(2,1)S(1)}, u32[]{:S(2)}, u32[]{:S(2)}) collective-permute-start(bf16[128,384]{1,0:T(8,128)(2,1)S(1)} %get-tuple-element.43), channel_id=1, source_target_pairs={{0,2},{1,3},{2,0},{3,1},{4,6},{5,7},{6,4},{7,5},{8,10},{9,11},{10,... | collective-permute-start | bytes 294920 | tf_op jit(solution)/shard_map/ppermute | solution.py:503
  223.7 4.8 %collective-permute-start.8 = (bf16[128,384]{1,0:T(8,128)(2,1)S(1)}, bf16[128,384]{1,0:T(8,128)(2,1)S(1)}, u32[]{:S(2)}, u32[]{:S(2)}) collective-permute-start(bf16[128,384]{1,0:T(8,128)(2,1)S(1)} %get-tuple-element.44), channel_id=1, source_target_pairs={{0,3},{1,0},{2,1},{3,2},{4,7},{5,4},{6,5},{7,6},{8,11},{9,8},{10,9... | collective-permute-start | bytes 294920 | tf_op jit(solution)/shard_map/ppermute | solution.py:503
  228.5 21.4 %copy-start.12 = (s32[512]{0:T(512)S(1)}, s32[512]{0:T(512)}, u32[]{:S(2)}) copy-start(s32[512]{0:T(512)} %param.21) | copy-start | bytes 6148
  241.2 4.8 %collective-permute-start.12 = (bf16[128,384]{1,0:T(8,128)(2,1)S(1)}, bf16[128,384]{1,0:T(8,128)(2,1)S(1)}, u32[]{:S(2)}, u32[]{:S(2)}) collective-permute-start(bf16[128,384]{1,0:T(8,128)(2,1)S(1)} %get-tuple-element.51), channel_id=1, source_target_pairs={{0,1},{1,2},{2,3},{3,0},{4,5},{5,6},{6,7},{7,4},{8,9},{9,10},{10,1... | collective-permute-start | bytes 294920 | tf_op jit(solution)/shard_map/ppermute | solution.py:503
  243.3 5.6 %collective-permute-start.13 = (bf16[128,384]{1,0:T(8,128)(2,1)S(1)}, bf16[128,384]{1,0:T(8,128)(2,1)S(1)}, u32[]{:S(2)}, u32[]{:S(2)}) collective-permute-start(bf16[128,384]{1,0:T(8,128)(2,1)S(1)} %get-tuple-element.52), channel_id=1, source_target_pairs={{0,2},{1,3},{2,0},{3,1},{4,6},{5,7},{6,4},{7,5},{8,10},{9,11},{10,... | collective-permute-start | bytes 294920 | tf_op jit(solution)/shard_map/ppermute | solution.py:503
  245.1 4.8 %collective-permute-start.14 = (bf16[128,384]{1,0:T(8,128)(2,1)S(1)}, bf16[128,384]{1,0:T(8,128)(2,1)S(1)}, u32[]{:S(2)}, u32[]{:S(2)}) collective-permute-start(bf16[128,384]{1,0:T(8,128)(2,1)S(1)} %get-tuple-element.53), channel_id=1, source_target_pairs={{0,3},{1,0},{2,1},{3,2},{4,7},{5,4},{6,5},{7,6},{8,11},{9,8},{10,9... | collective-permute-start | bytes 294920 | tf_op jit(solution)/shard_map/ppermute | solution.py:503
  251.1 3.6 %collective-permute-start.15 = (bf16[1024,384]{1,0:T(8,128)(2,1)S(1)}, bf16[1024,384]{1,0:T(8,128)(2,1)S(1)}, u32[]{:S(2)}, u32[]{:S(2)}) collective-permute-start(bf16[1024,384]{1,0:T(8,128)(2,1)S(1)} %get-tuple-element.55), channel_id=1, source_target_pairs={{0,4},{4,0},{1,5},{5,1},{2,6},{6,2},{3,7},{7,3},{8,12},{12,8},{9,1... | collective-permute-start | bytes 2359304 | tf_op jit(solution)/shard_map/ppermute | solution.py:503
  254.9 6.2 %collective-permute-start.18 = (bf16[256,384]{1,0:T(8,128)(2,1)S(1)}, bf16[256,384]{1,0:T(8,128)(2,1)S(1)}, u32[]{:S(2)}, u32[]{:S(2)}) collective-permute-start(bf16[256,384]{1,0:T(8,128)(2,1)S(1)} %get-tuple-element.59), channel_id=1, source_target_pairs={{0,192},{64,0},{128,64},{192,128},{1,193},{65,1},{129,65},{193,129... | collective-permute-start | bytes 589832 | tf_op jit(solution)/shard_map/ppermute | solution.py:503
  256.5 7.3 %collective-permute-start.17 = (bf16[256,384]{1,0:T(8,128)(2,1)S(1)}, bf16[256,384]{1,0:T(8,128)(2,1)S(1)}, u32[]{:S(2)}, u32[]{:S(2)}) collective-permute-start(bf16[256,384]{1,0:T(8,128)(2,1)S(1)} %get-tuple-element.58), channel_id=1, source_target_pairs={{0,128},{64,192},{128,0},{192,64},{1,129},{65,193},{129,1},{193,65... | collective-permute-start | bytes 589832 | tf_op jit(solution)/shard_map/ppermute | solution.py:503
  257.7 11.4 %collective-permute-start.16 = (bf16[256,384]{1,0:T(8,128)(2,1)S(1)}, bf16[256,384]{1,0:T(8,128)(2,1)S(1)}, u32[]{:S(2)}, u32[]{:S(2)}) collective-permute-start(bf16[256,384]{1,0:T(8,128)(2,1)S(1)} %get-tuple-element.57), channel_id=1, source_target_pairs={{0,64},{64,128},{128,192},{192,0},{1,65},{65,129},{129,193},{193,1... | collective-permute-start | bytes 589832 | tf_op jit(solution)/shard_map/ppermute | solution.py:503
  269.1 42.9 %copy-start.1 = (bf16[384,384]{1,0:T(8,128)(2,1)S(1)}, bf16[384,384]{1,0:T(8,128)(2,1)}, u32[]{:S(2)}) copy-start(bf16[384,384]{1,0:T(8,128)(2,1)} %param.15) | copy-start | bytes 884740
  280.9 31.1 %copy-start.13 = (bf16[32,384]{1,0:T(8,128)(2,1)}, bf16[32,384]{1,0:T(8,128)(2,1)S(1)}, u32[]{:S(2)}) copy-start(bf16[32,384]{1,0:T(8,128)(2,1)S(1)} %multiply_convert_fusion) | copy-start | bytes 73732
  303.9 6.0 %collective-permute-start.19 = (bf16[1024,384]{1,0:T(8,128)(2,1)S(1)}, bf16[1024,384]{1,0:T(8,128)(2,1)S(1)}, u32[]{:S(2)}, u32[]{:S(2)}) collective-permute-start(bf16[1024,384]{1,0:T(8,128)(2,1)S(1)} %bitcast.26), channel_id=1, source_target_pairs={{0,4},{4,0},{1,5},{5,1},{2,6},{6,2},{3,7},{7,3},{8,12},{12,8},{9,1... | collective-permute-start | bytes 2359304 | tf_op jit(solution)/shard_map/ppermute | solution.py:503
Sparse Core Ops, SparseCore 0:
  65.8 142.2 all-gather.2

commit v8 on v7

--- a/solution.py
+++ b/solution.py
@@ -152,16 +152,15 @@
     )(lists, *partials)
 
 
-TRIP_BLOCK = 512
-TRIP_STEPS = TRIPS // TRIP_BLOCK
-SLOT_BLOCK = 512
-SUM_CHUNK = 1024
+TRIP_BLOCKS = {128: (512, 512, 1024, 48), 256: (1024, 512, TRIPS, 62)}
 
 
 def triplet_kernel(
-    groups, in_ref, live_ref, to_ref, basis_ref, weight_ref, table_ref, out_ref, table, values, padded
+    groups, blocks, in_ref, live_ref, to_ref, basis_ref, weight_ref, table_ref, out_ref, table, values, padded
 ):
     step = pl.program_id(0)
+    trip_block, slot_block, sum_chunk = blocks
+    trip_steps = TRIPS // trip_block
     width = table_ref.shape[1]
     deep = SLOTS // groups
 
@@ -171,7 +170,7 @@
         for h in range(groups):
             table[:, h * width : (h + 1) * width] = table_ref[h * deep : (h + 1) * deep, :]
 
-    @pl.when(step < TRIP_STEPS)
+    @pl.when(step < trip_steps)
     def _():
         padded[0:NSBF, :] = basis_ref[...] * live_ref[...].astype(F32)
         basis = padded[...]
@@ -181,20 +180,12 @@
         coef = lax.dot_general(
             stacked, weight_ref[...], (((0,), (0,)), ((), ())), preferred_element_type=F32
         )
-        place = pl.multiple_of(step * TRIP_BLOCK, TRIP_BLOCK)
+        place = pl.multiple_of(step * trip_block, trip_block)
         source = column_of(in_ref[...])
-        target = column_of(to_ref[:, pl.ds(place, TRIP_BLOCK)])
+        target = column_of(to_ref[:, pl.ds(place, trip_block)])
         spot = source & (deep - 1)
 
-        def more(i, total):
-            first = pl.multiple_of(i * SUM_CHUNK, SUM_CHUNK)
-            return total + product(
-                picks_of(spot - first, SUM_CHUNK), table[pl.ds(first, SUM_CHUNK), :]
-            )
-
-        candidates = product(picks_of(spot, SUM_CHUNK), table[:SUM_CHUNK, :])
-        if deep > SUM_CHUNK:
-            candidates = lax.fori_loop(1, deep // SUM_CHUNK, more, candidates)
+        candidates = product(picks_of(spot, deep), table[...])
         for k in range(0, width, 128):
             value = candidates[:, k : k + 128]
             for h in range(1, groups):
@@ -204,21 +195,27 @@
             for h in range(groups):
                 at = h * width + k
                 here = (target >= h * deep) & (target < (h + 1) * deep)
-                values[pl.ds(place, TRIP_BLOCK), at : at + 128] = jnp.where(here, value, 0.0).astype(
+                values[pl.ds(place, trip_block), at : at + 128] = jnp.where(here, value, 0.0).astype(
                     BF16
                 )
 
-    @pl.when(step >= TRIP_STEPS)
+    @pl.when(step >= trip_steps)
     def _():
-        first = (step - TRIP_STEPS) * SLOT_BLOCK
+        first = (step - trip_steps) * slot_block
+
+        def part(rows):
+            chosen = members(to_ref[:, rows] & (deep - 1), slot_block, first)
+            return product(chosen, values[rows, :])
 
         def more(i, total):
-            rows = pl.ds(pl.multiple_of(i * SUM_CHUNK, SUM_CHUNK), SUM_CHUNK)
-            chosen = members(to_ref[:, rows] & (deep - 1), SLOT_BLOCK, first)
-            return total + product(chosen, values[rows, :])
-
-        empty = jnp.zeros((SLOT_BLOCK, groups * width), F32)
-        total = lax.fori_loop(0, TRIPS // SUM_CHUNK, more, empty).astype(BF16)
+            return total + part(pl.ds(pl.multiple_of(i * sum_chunk, sum_chunk), sum_chunk))
+
+        if sum_chunk == TRIPS:
+            total = part(slice(0, TRIPS))
+        else:
+            empty = jnp.zeros((slot_block, groups * width), F32)
+            total = lax.fori_loop(0, TRIPS // sum_chunk, more, empty)
+        total = total.astype(BF16)
         for h in range(groups):
             out_ref[h] = total[:, h * width : (h + 1) * width]
 
@@ -227,28 +224,30 @@
     width = table.shape[1]
     groups = 512 // width
     deep = SLOTS // groups
-    gather_step = lambda i: (0, jnp.minimum(i, TRIP_STEPS - 1))
-    return pl.pallas_call(
-        functools.partial(triplet_kernel, groups),
-        grid=(TRIP_STEPS + deep // SLOT_BLOCK,),
+    trip_block, slot_block, sum_chunk, mib = TRIP_BLOCKS[width]
+    trip_steps = TRIPS // trip_block
+    gather_step = lambda i: (0, jnp.minimum(i, trip_steps - 1))
+    return pl.pallas_call(
+        functools.partial(triplet_kernel, groups, (trip_block, slot_block, sum_chunk)),
+        grid=(trip_steps + deep // slot_block,),
         in_specs=[
-            pl.BlockSpec((1, TRIP_BLOCK), gather_step),
-            pl.BlockSpec((1, TRIP_BLOCK), gather_step),
+            pl.BlockSpec((1, trip_block), gather_step),
+            pl.BlockSpec((1, trip_block), gather_step),
             whole((1, TRIPS)),
-            pl.BlockSpec((NSBF, TRIP_BLOCK), gather_step),
+            pl.BlockSpec((NSBF, trip_block), gather_step),
             whole((3 * BASIS_PAD, width)),
             whole((SLOTS, width)),
         ],
         out_specs=pl.BlockSpec(
-            (groups, SLOT_BLOCK, width), lambda i: (0, jnp.maximum(i - TRIP_STEPS, 0), 0)
+            (groups, slot_block, width), lambda i: (0, jnp.maximum(i - trip_steps, 0), 0)
         ),
         out_shape=shape_of(groups, deep, width),
         scratch_shapes=[
             pltpu.VMEM((deep, groups * width), BF16),
             pltpu.VMEM((TRIPS, groups * width), BF16),
-            pltpu.VMEM((BASIS_PAD, TRIP_BLOCK), F32),
+            pltpu.VMEM((BASIS_PAD, trip_block), F32),
         ],
-        compiler_params=params(48),
+        compiler_params=params(mib),
         name="triplets",
         cost_estimate=pl.CostEstimate(
             flops=4 * TRIPS * SLOTS * width, bytes_accessed=18000 * width, transcendentals=0
@@ -259,8 +258,8 @@
 EDGE_CHUNK = 1024
 
 
-def edges_kernel(mp_ref, list_ref, table_ref, *refs):
-    earlier, outs, total = refs[: -N_MP - 1], refs[-N_MP - 1 : -1], refs[-1]
+def edges_kernel(has_earlier, mp_ref, list_ref, table_ref, *refs):
+    earlier, outs, total = refs[:has_earlier], refs[has_earlier:-1], refs[-1]
     step = pl.program_id(0)
     part = product(members(list_ref[...], EDGE_DEV, 0), table_ref[...])
 
@@ -274,30 +273,34 @@
 
     @pl.when(step == SLOTS // EDGE_CHUNK - 1)
     def _():
-        for k, out_ref in enumerate(outs):
+        for k in range(N_MP):
             place = lax.rem(mp_ref[0] + k, N_MP) * ROWS
-            low = 0
+            block = total[pl.ds(pl.multiple_of(place, ROWS), ROWS), :].astype(BF16)
             if earlier:
-                low = earlier[k].shape[1]
-                out_ref[:, :low] = earlier[k][...]
-            out_ref[:, low:] = total[pl.ds(pl.multiple_of(place, ROWS), ROWS), :].astype(BF16)
+                low = earlier[0].shape[2]
+                outs[k][:, :low] = earlier[0][k]
+                outs[k][:, low:] = block
+            else:
+                outs[0][k] = block
 
 
 def edges(mp, lists, returned, earlier):
     width = returned.shape[1]
-    before = [block.shape[1] for block in earlier]
-    full = width + (before[0] if before else 0)
-    return pl.pallas_call(
-        edges_kernel,
+    if earlier:
+        shapes = [(ROWS, width + earlier[0].shape[2])] * N_MP
+    else:
+        shapes = [(N_MP, ROWS, width)]
+    return pl.pallas_call(
+        functools.partial(edges_kernel, len(earlier)),
         grid=(SLOTS // EDGE_CHUNK,),
         in_specs=[
             SCALAR,
             pl.BlockSpec((1, EDGE_CHUNK), lambda i: (0, i)),
             pl.BlockSpec((EDGE_CHUNK, width), lambda i: (i, 0)),
         ]
-        + [whole((ROWS, w)) for w in before],
-        out_specs=[whole((ROWS, full))] * N_MP,
-        out_shape=[shape_of(ROWS, full)] * N_MP,
+        + [whole(block.shape) for block in earlier],
+        out_specs=[whole(shape) for shape in shapes],
+        out_shape=[shape_of(*shape) for shape in shapes],
         scratch_shapes=[pltpu.VMEM((EDGE_DEV, width), F32)],
         compiler_params=params(24),
         name="edges",

time: 320 us -> 316 us (0.988)
  waiting for transfers between devices: 123 us -> 127 us
    all_to_all x1, waiting for transfers between devices: 0.71 us -> 5.06 us  [local(): first = exchange(sums(first, PARTS[0]))]
    all_to_all x1, starting transfers between devices: 9.62 us -> 6.19 us  [local(): second = exchange(sums(second, PARTS[1]))]
  transfers between devices with their start and end apart: 25 -> 25, of which waited for: 18 -> 17; matrix products, arithmetic and copies ran while one was open for 2% -> 2% of each run, Pallas kernels for 14% -> 13%
where the time goes in v8:
time: 316 us; the launch traced here: 315 us
  waiting for transfers between devices  127 us (40%)
  Pallas kernels  66.3 us (21%)
  starting transfers between devices  64 us (20%)
  blocking collectives  34.5 us (11%)
  between operations  14.3 us (5%)
  local copies, waits for them, and re-layouts  6.52 us (2%)
    all_to_all x1, waiting for transfers between devices, local(): second = exchange(sums(second, PARTS[1]))  44.2 us
    pallas_call x2, Pallas kernels, triplets(): pl.pallas_call(functools.partial(triplet_kernel, groups, (trip_block, slo...  38.6 us
    all_to_all x1, waiting for transfers between devices, local(): second = exchange(second)  35.3 us
    ppermute x20, waiting for transfers between devices, turn(): lax.ppermute(array, axis, [(i, (i + shift) % count) for i in range(count)])  34.7 us
    ppermute x20, starting transfers between devices, turn(): lax.ppermute(array, axis, [(i, (i + shift) % count) for i in range(count)])  32.4 us
    all_to_all x1, starting transfers between devices, local(): first = exchange(first)  13 us
    pallas_call x1, Pallas kernels, layers(): pl.pallas_call(layers_kernel, in_specs=[SCALAR] + [vmem] * (2 * N_MP) + [...  11.8 us
    all_to_all x1, blocking collectives, local(): atom_sum = summed(lax.all_to_all(part, 'graph_1', 0, 0, tiled=True))  11.7 us
  transfers between devices with their start and end apart: 25, of which 17 were waited for; matrix products, arithmetic and copies ran while one was open for 2% of the time, Pallas kernels for 13%

profile of v8, /device:TPU:1, one launch (start us, length us, event | category | flops | bytes accessed | tf_op | source)
XLA Modules:
  0.0 315.5 jit_solution(12607081930397589372)
XLA Ops:
  7.2 2.3 project.1
  9.5 2.1 collective-permute-start
  11.6 2.6 collective-permute-start.1
  14.3 1.1 collective-permute-start.2
  15.3 0.8 reshape.63.list_ref
  16.2 4.0 %collective-permute-done.1.c_ref = bf16[512,128]{1,0:T(8,128)(2,1)S(1)} collective-permute-done((bf16[512,128]{1,0:T(8,128)(2,1)}, bf16[512,128]{1,0:T(8,128)(2,1)S(1)}, u32[]{:S(2)}, u32[]{:S(2)}) %collective-permute-start.1) | collective-permute-done | bytes 131104 | tf_op jit(solution)/shard_map/ppermute | solution.py:506
  20.2 0.9 copy-done.5
  21.1 3.0 send.2
  24.1 13.0 %all-to-all-start = ((bf16[64,64,128]{2,1,0:T(8,128)(2,1)}), bf16[64,64,128]{2,1,0:T(8,128)(2,1)S(1)}, u32[]{:S(2)}, u32[]{:S(2)}) async-start(bf16[64,64,128]{2,1,0:T(8,128)(2,1)} %bitcast.6), calls=%async_computation | async-start | bytes 2097152 | tf_op jit(solution)/shard_map/all_to_all | solution.py:569
  37.1 0.0 all-gather.3.cloned.1.call-start
  37.2 2.4 constant_dynamic-slice_fusion.1
  39.6 1.0 collective-permute-start.3
  40.6 2.1 collective-permute-start.4
  42.7 1.3 collective-permute-start.5
  44.1 2.2 pad_maximum_fusion
  46.2 2.1 collective-permute-done.3.b_ref
  48.3 6.0 %collective-permute-done.4.c_ref = bf16[512,256]{1,0:T(8,128)(2,1)S(1)} collective-permute-done((bf16[512,256]{1,0:T(8,128)(2,1)S(1)}, bf16[512,256]{1,0:T(8,128)(2,1)S(1)}, u32[]{:S(2)}, u32[]{:S(2)}) %collective-permute-start.4) | collective-permute-done | bytes 262176 | tf_op jit(solution)/shard_map/ppermute | solution.py:506
  54.3 3.2 %send.3 = bf16[4096,256]{1,0:T(8,128)(2,1)} custom-call(s32[1,4096]{1,0:T(1,128)S(1)} %reshape.63.list_ref, bf16[512,256]{1,0:T(8,128)(2,1)S(1)} %copy-done.4, bf16[512,256]{1,0:T(8,128)(2,1)S(1)} %collective-permute-done.3.b_ref, bf16[512,256]{1,0:T(8,128)(2,1)S(1)} %collective-permute-done.4.c_ref, bf16[512,256]{1,0:T(8,128)(2,1)S(1)} %collective-permute-done.5.d_ref), custom_call_target="tpu_custom_call" | custom-call | flops 1073741824 | bytes 3072000 | tf_op jit(solution)/shard_map/send/pallas_call | solution.py:140
  57.6 8.1 %all-to-all-done = bf16[64,64,128]{2,1,0:T(8,128)(2,1)S(1)} async-done(((bf16[64,64,128]{2,1,0:T(8,128)(2,1)}), bf16[64,64,128]{2,1,0:T(8,128)(2,1)S(1)}, u32[]{:S(2)}, u32[]{:S(2)}) %all-to-all-start) | async-done | bytes 1048608 | tf_op jit(solution)/shard_map/all_to_all | solution.py:569
  65.7 6.5 %all-to-all-start.1 = ((bf16[64,64,256]{2,1,0:T(8,128)(2,1)}), bf16[64,64,256]{2,1,0:T(8,128)(2,1)}, u32[]{:S(2)}, u32[]{:S(2)}) async-start(bf16[64,64,256]{2,1,0:T(8,128)(2,1)} %bitcast.7), calls=%async_computation.1 | async-start | bytes 4194304 | tf_op jit(solution)/shard_map/all_to_all | solution.py:572
  72.4 15.7 %triplets.3 = bf16[4,1024,128]{2,1,0:T(8,128)(2,1)} custom-call(s32[1,4096]{1,0:T(1,128)S(1)} %bitcast.26, s32[1,4096]{1,0:T(1,128)S(1)} %bitcast.28, s32[1,4096]{1,0:T(1,128)S(1)} %bitcast.30, f32[42,4096]{1,0:T(8,128)S(1)} %copy-done.3, bf16[144,128]{1,0:T(8,128)(2,1)S(1)} %slice.9.weight_ref, bf16[4096,128]{1,0:T(8,128)(2,1)S(1)} %bitcast.21), custom_call_target="tpu_custom_call" | custom-call | flops 8589934592 | bytes 2304000 | tf_op jit(solution)/shard_map/triplets/pallas_call | solution.py:230
  88.1 35.3 %all-to-all-done.1 = bf16[64,64,256]{2,1,0:T(8,128)(2,1)} async-done(((bf16[64,64,256]{2,1,0:T(8,128)(2,1)}), bf16[64,64,256]{2,1,0:T(8,128)(2,1)}, u32[]{:S(2)}, u32[]{:S(2)}) %all-to-all-start.1) | async-done | bytes 2097184 | tf_op jit(solution)/shard_map/all_to_all | solution.py:572
  123.4 5.8 %all-to-all-start.3 = ((bf16[64,64,128]{2,1,0:T(8,128)(2,1)}), bf16[64,64,128]{2,1,0:T(8,128)(2,1)S(1)}, u32[]{:S(2)}, u32[]{:S(2)}) async-start(bf16[64,64,128]{2,1,0:T(8,128)(2,1)} %bitcast.13), calls=%async_computation.3 | async-start | bytes 2097152 | tf_op jit(solution)/shard_map/all_to_all | solution.py:575
  129.2 0.6 slice.8.weight_ref
  129.9 22.8 %triplets.2 = bf16[2,2048,256]{2,1,0:T(8,128)(2,1)} custom-call(s32[1,4096]{1,0:T(1,128)} %bitcast.25, s32[1,4096]{1,0:T(1,128)} %bitcast.27, s32[1,4096]{1,0:T(1,128)} %bitcast.29, f32[42,4096]{1,0:T(8,128)} %basis_ref.3, bf16[144,256]{1,0:T(8,128)(2,1)} %slice.8.weight_ref, bf16[4096,256]{1,0:T(8,128)(2,1)} %bitcast.9.table_ref), custom_call_target="tpu_custom_call" | custom-call | flops 17179869184 | bytes 4608000 | tf_op jit(solution)/shard_map/triplets/pallas_call | solution.py:230
  152.7 5.1 %all-to-all-done.3 = bf16[64,64,128]{2,1,0:T(8,128)(2,1)S(1)} async-done(((bf16[64,64,128]{2,1,0:T(8,128)(2,1)}), bf16[64,64,128]{2,1,0:T(8,128)(2,1)S(1)}, u32[]{:S(2)}, u32[]{:S(2)}) %all-to-all-start.3) | async-done | bytes 1048608 | tf_op jit(solution)/shard_map/all_to_all | solution.py:575
  157.8 6.2 %all-to-all-start.2 = ((bf16[64,64,256]{2,1,0:T(8,128)(2,1)}), bf16[64,64,256]{2,1,0:T(8,128)(2,1)S(1)}, u32[]{:S(2)}, u32[]{:S(2)}) async-start(bf16[64,64,256]{2,1,0:T(8,128)(2,1)} %bitcast.34), calls=%async_computation.2 | async-start | bytes 4194304 | tf_op jit(solution)/shard_map/all_to_all | solution.py:576
  164.0 1.0 collective-permute-start.9
  165.0 2.1 collective-permute-start.10
  167.1 1.3 collective-permute-start.11
  168.4 1.9 edges.2.refs_0_
  170.3 0.6 copy-done.10
  171.0 44.2 %all-to-all-done.2 = bf16[64,64,256]{2,1,0:T(8,128)(2,1)S(1)} async-done(((bf16[64,64,256]{2,1,0:T(8,128)(2,1)}), bf16[64,64,256]{2,1,0:T(8,128)(2,1)S(1)}, u32[]{:S(2)}, u32[]{:S(2)}) %all-to-all-start.2) | async-done | bytes 2097184 | tf_op jit(solution)/shard_map/all_to_all | solution.py:576
  215.2 0.9 copy-done.11
  216.1 2.0 edges.3
  218.2 1.0 collective-permute-start.6
  219.2 2.1 collective-permute-start.7
  221.3 1.3 collective-permute-start.8
  222.6 0.8 collective-permute-done.6.refs_1_
  223.4 2.5 collective-permute-done.7.refs_2_
  225.9 0.2 collective-permute-done.8.refs_3_
  226.1 11.8 %layers.1 = (bf16[128,384]{1,0:T(8,128)(2,1)S(1)}, bf16[128,384]{1,0:T(8,128)(2,1)S(1)}, bf16[128,384]{1,0:T(8,128)(2,1)S(1)}, bf16[128,384]{1,0:T(8,128)(2,1)S(1)}) custom-call(s32[1]{0:T(128)} %bitcast.mp_ref, bf16[128,384]{1,0:T(8,128)(2,1)S(1)} %get-tuple-element.33.refs_0_, bf16[128,384]{1,0:T(8,128)(2,1)S(1)} %collective-permute-done.6.refs_1_, ...), custom_call_target="tpu_custom_call" | custom-call | flops 3623878656 | bytes 28311552 | tf_op jit(solution)/shard_map/layers/pallas_call | solution.py:388
  237.9 2.1 collective-permute-start.12
  239.9 1.8 collective-permute-start.13
  241.7 0.9 collective-permute-start.14
  242.6 2.9 collective-permute-done.13.h2
  245.6 0.9 collective-permute-done.14.h3
  246.5 1.3 atoms.1
  247.8 1.7 collective-permute-start.15
  249.4 1.9 collective-permute-done.15.got_ref
  251.3 0.2 meet.1
  251.5 1.6 collective-permute-start.18
  253.2 1.2 collective-permute-start.17
  254.3 3.4 %collective-permute-done.18 = bf16[256,384]{1,0:T(8,128)(2,1)S(1)} collective-permute-done((bf16[256,384]{1,0:T(8,128)(2,1)S(1)}, bf16[256,384]{1,0:T(8,128)(2,1)S(1)}, u32[]{:S(2)}, u32[]{:S(2)}) %collective-permute-start.18) | collective-permute-done | bytes 196640 | tf_op jit(solution)/shard_map/ppermute | solution.py:506
  257.7 2.8 collective-permute-done.17
  260.5 5.2 %collective-permute-done.16 = bf16[256,384]{1,0:T(8,128)(2,1)S(1)} collective-permute-done((bf16[256,384]{1,0:T(8,128)(2,1)S(1)}, bf16[256,384]{1,0:T(8,128)(2,1)S(1)}, u32[]{:S(2)}, u32[]{:S(2)}) %collective-permute-start.16) | collective-permute-done | bytes 196640 | tf_op jit(solution)/shard_map/ppermute | solution.py:506
  265.7 0.1 add_convert_fusion
  265.8 11.7 %all_to_all.35 = bf16[8,32,384]{2,1,0:T(8,128)(2,1)S(1)} all-to-all(bf16[8,32,384]{2,1,0:T(8,128)(2,1)S(1)} %bitcast.36), channel_id=1, replica_groups=mesh['graph_0'=4,'graph_1'=8,'graph_2'=2,'mp'=4] {'graph_1'}, dimensions={0} | all-to-all | bytes 393216 | tf_op jit(solution)/shard_map/all_to_all | solution.py:588
  277.6 11.3 %all_to_all.36 = bf16[8,32,384]{2,1,0:T(8,128)(2,1)S(1)} all-to-all(bf16[8,32,384]{2,1,0:T(8,128)(2,1)S(1)} %broadcast_in_dim.25), channel_id=1, replica_groups=mesh['graph_0'=4,'graph_1'=8,'graph_2'=2,'mp'=4] {'graph_1'}, dimensions={0} | all-to-all | bytes 393216 | tf_op jit(solution)/shard_map/all_to_all | solution.py:590
  288.9 0.1 broadcast_in_dim.27
  288.9 11.6 %all_to_all.37 = bf16[4,256,384]{2,1,0:T(8,128)(2,1)S(1)} all-to-all(bf16[4,256,384]{2,1,0:T(8,128)(2,1)S(1)} %broadcast_in_dim.27), channel_id=1, replica_groups=mesh['graph_0'=4,'graph_1'=8,'graph_2'=2,'mp'=4] {'graph_0'}, dimensions={0} | all-to-all | bytes 1572864 | tf_op jit(solution)/shard_map/all_to_all | solution.py:593
  300.5 4.1 %collective-permute-start.19 = (bf16[1024,384]{1,0:T(8,128)(2,1)S(1)}, bf16[1024,384]{1,0:T(8,128)(2,1)S(1)}, u32[]{:S(2)}, u32[]{:S(2)}) collective-permute-start(bf16[1024,384]{1,0:T(8,128)(2,1)S(1)} %bitcast.23), channel_id=1, source_target_pairs={{0,4},{4,0},{1,5},{5,1},{2,6},{6,2},{3,7},{7,3},{8,12},{12,8},{9,1... | collective-permute-start | bytes 2359304 | tf_op jit(solution)/shard_map/ppermute | solution.py:506
  304.6 1.9 collective-permute-done.19.other_ref
  306.5 2.1 final.1
  (43 shorter events, 0.2 us)
Async XLA Ops:
  7.2 30.0 %copy-start = (bf16[384,384]{1,0:T(8,128)(2,1)S(1)}, bf16[384,384]{1,0:T(8,128)(2,1)}, u32[]{:S(2)}) copy-start(bf16[384,384]{1,0:T(8,128)(2,1)} %param.15) | copy-start | bytes 884740
  9.5 6.7 %collective-permute-start = (bf16[512,128]{1,0:T(8,128)(2,1)}, bf16[512,128]{1,0:T(8,128)(2,1)S(1)}, u32[]{:S(2)}, u32[]{:S(2)}) collective-permute-start(bf16[512,128]{1,0:T(8,128)(2,1)} %get-tuple-element.27.a_ref), channel_id=1, source_target_pairs={{0,1},{1,2},{2,3},{3,0},{4,5},{5,6},{6,7},{7,4},{8,9},{9,10},{10,1... | collective-permute-start | bytes 393224 | tf_op jit(solution)/shard_map/ppermute | solution.py:506
  11.6 8.5 %collective-permute-start.1 = (bf16[512,128]{1,0:T(8,128)(2,1)}, bf16[512,128]{1,0:T(8,128)(2,1)S(1)}, u32[]{:S(2)}, u32[]{:S(2)}) collective-permute-start(bf16[512,128]{1,0:T(8,128)(2,1)} %get-tuple-element.27.a_ref), channel_id=1, source_target_pairs={{0,2},{1,3},{2,0},{3,1},{4,6},{5,7},{6,4},{7,5},{8,10},{9,11},{10,... | collective-permute-start | bytes 393224 | tf_op jit(solution)/shard_map/ppermute | solution.py:506
  14.3 5.9 %collective-permute-start.2 = (bf16[512,128]{1,0:T(8,128)(2,1)}, bf16[512,128]{1,0:T(8,128)(2,1)S(1)}, u32[]{:S(2)}, u32[]{:S(2)}) collective-permute-start(bf16[512,128]{1,0:T(8,128)(2,1)} %get-tuple-element.27.a_ref), channel_id=1, source_target_pairs={{0,3},{1,0},{2,1},{3,2},{4,7},{5,4},{6,5},{7,6},{8,11},{9,8},{10,9... | collective-permute-start | bytes 393224 | tf_op jit(solution)/shard_map/ppermute | solution.py:506
  20.2 0.9 copy-start.5
  24.1 41.6 %all-to-all-start = ((bf16[64,64,128]{2,1,0:T(8,128)(2,1)}), bf16[64,64,128]{2,1,0:T(8,128)(2,1)S(1)}, u32[]{:S(2)}, u32[]{:S(2)}) async-start(bf16[64,64,128]{2,1,0:T(8,128)(2,1)} %bitcast.6), calls=%async_computation | async-start | bytes 2097152 | tf_op jit(solution)/shard_map/all_to_all | solution.py:569
  37.1 189.0 %all-gather.3.cloned.1.call-start = ((), (), s32[]{:S(2)}) async-start(), calls=%async_computation.7 | async-start | bytes 33177600 | tf_op jit(solution)/shard_map/all_gather | solution.py:573
  37.2 2.4 copy-start.4
  39.6 8.7 %collective-permute-start.3 = (bf16[512,256]{1,0:T(8,128)(2,1)S(1)}, bf16[512,256]{1,0:T(8,128)(2,1)S(1)}, u32[]{:S(2)}, u32[]{:S(2)}) collective-permute-start(bf16[512,256]{1,0:T(8,128)(2,1)S(1)} %copy-done.4), channel_id=1, source_target_pairs={{0,1},{1,2},{2,3},{3,0},{4,5},{5,6},{6,7},{7,4},{8,9},{9,10},{10,1... | collective-permute-start | bytes 786440 | tf_op jit(solution)/shard_map/ppermute | solution.py:506
  40.6 13.7 %collective-permute-start.4 = (bf16[512,256]{1,0:T(8,128)(2,1)S(1)}, bf16[512,256]{1,0:T(8,128)(2,1)S(1)}, u32[]{:S(2)}, u32[]{:S(2)}) collective-permute-start(bf16[512,256]{1,0:T(8,128)(2,1)S(1)} %copy-done.4), channel_id=1, source_target_pairs={{0,2},{1,3},{2,0},{3,1},{4,6},{5,7},{6,4},{7,5},{8,10},{9,11},{10,... | collective-permute-start | bytes 786440 | tf_op jit(solution)/shard_map/ppermute | solution.py:506
  42.7 11.6 %collective-permute-start.5 = (bf16[512,256]{1,0:T(8,128)(2,1)S(1)}, bf16[512,256]{1,0:T(8,128)(2,1)S(1)}, u32[]{:S(2)}, u32[]{:S(2)}) collective-permute-start(bf16[512,256]{1,0:T(8,128)(2,1)S(1)} %copy-done.4), channel_id=1, source_target_pairs={{0,3},{1,0},{2,1},{3,2},{4,7},{5,4},{6,5},{7,6},{8,11},{9,8},{10,9... | collective-permute-start | bytes 786440 | tf_op jit(solution)/shard_map/ppermute | solution.py:506
  65.7 6.6 %copy-start.13 = (f32[42,384]{1,0:T(8,128)S(1)}, f32[42,384]{1,0:T(8,128)}, u32[]{:S(2)}) copy-start(f32[42,384]{1,0:T(8,128)} %param.14) | copy-start | bytes 193540
  65.7 6.7 %copy-start.3 = (f32[42,4096]{1,0:T(8,128)S(1)}, f32[42,4096]{1,0:T(8,128)}, u32[]{:S(2)}) copy-start(f32[42,4096]{1,0:T(8,128)} %basis_ref.3) | copy-start | bytes 2064388
  65.7 6.7 %copy-start.6 = (s32[4096]{0:T(1024)S(1)}, s32[4096]{0:T(1024)}, u32[]{:S(2)}) copy-start(s32[4096]{0:T(1024)} %param.18) | copy-start | bytes 49156
  65.7 6.7 %copy-start.7 = (s32[4096]{0:T(1024)S(1)}, s32[4096]{0:T(1024)}, u32[]{:S(2)}) copy-start(s32[4096]{0:T(1024)} %param.20) | copy-start | bytes 49156
  65.7 6.7 %copy-start.8 = (s32[4096]{0:T(1024)S(1)}, s32[4096]{0:T(1024)}, u32[]{:S(2)}) copy-start(s32[4096]{0:T(1024)} %param.19) | copy-start | bytes 49156
  65.7 57.7 %all-to-all-start.1 = ((bf16[64,64,256]{2,1,0:T(8,128)(2,1)}), bf16[64,64,256]{2,1,0:T(8,128)(2,1)}, u32[]{:S(2)}, u32[]{:S(2)}) async-start(bf16[64,64,256]{2,1,0:T(8,128)(2,1)} %bitcast.7), calls=%async_computation.1 | async-start | bytes 4194304 | tf_op jit(solution)/shard_map/all_to_all | solution.py:572
  123.4 34.4 %all-to-all-start.3 = ((bf16[64,64,128]{2,1,0:T(8,128)(2,1)}), bf16[64,64,128]{2,1,0:T(8,128)(2,1)S(1)}, u32[]{:S(2)}, u32[]{:S(2)}) async-start(bf16[64,64,128]{2,1,0:T(8,128)(2,1)} %bitcast.13), calls=%async_computation.3 | async-start | bytes 2097152 | tf_op jit(solution)/shard_map/all_to_all | solution.py:575
  157.8 57.4 %all-to-all-start.2 = ((bf16[64,64,256]{2,1,0:T(8,128)(2,1)}), bf16[64,64,256]{2,1,0:T(8,128)(2,1)S(1)}, u32[]{:S(2)}, u32[]{:S(2)}) async-start(bf16[64,64,256]{2,1,0:T(8,128)(2,1)} %bitcast.34), calls=%async_computation.2 | async-start | bytes 4194304 | tf_op jit(solution)/shard_map/all_to_all | solution.py:576
  164.0 62.1 %copy-start.2 = (bf16[128,384]{1,0:T(8,128)(2,1)S(1)}, bf16[128,384]{1,0:T(8,128)(2,1)}, u32[]{:S(2)}) copy-start(bf16[128,384]{1,0:T(8,128)(2,1)} %get-tuple-element.37.refs_4_) | copy-start | bytes 294916
  164.0 57.3 %collective-permute-start.9 = (bf16[128,384]{1,0:T(8,128)(2,1)}, bf16[128,384]{1,0:T(8,128)(2,1)S(1)}, u32[]{:S(2)}, u32[]{:S(2)}) collective-permute-start(bf16[128,384]{1,0:T(8,128)(2,1)} %get-tuple-element.38), channel_id=1, source_target_pairs={{0,1},{1,2},{2,3},{3,0},{4,5},{5,6},{6,7},{7,4},{8,9},{9,10},{10,1... | collective-permute-start | bytes 294920 | tf_op jit(solution)/shard_map/ppermute | solution.py:506
  165.0 57.6 %collective-permute-start.10 = (bf16[128,384]{1,0:T(8,128)(2,1)}, bf16[128,384]{1,0:T(8,128)(2,1)S(1)}, u32[]{:S(2)}, u32[]{:S(2)}) collective-permute-start(bf16[128,384]{1,0:T(8,128)(2,1)} %get-tuple-element.39), channel_id=1, source_target_pairs={{0,2},{1,3},{2,0},{3,1},{4,6},{5,7},{6,4},{7,5},{8,10},{9,11},{10,... | collective-permute-start | bytes 294920 | tf_op jit(solution)/shard_map/ppermute | solution.py:506
  167.1 55.5 %collective-permute-start.11 = (bf16[128,384]{1,0:T(8,128)(2,1)}, bf16[128,384]{1,0:T(8,128)(2,1)S(1)}, u32[]{:S(2)}, u32[]{:S(2)}) collective-permute-start(bf16[128,384]{1,0:T(8,128)(2,1)} %get-tuple-element.40), channel_id=1, source_target_pairs={{0,3},{1,0},{2,1},{3,2},{4,7},{5,4},{6,5},{7,6},{8,11},{9,8},{10,9... | collective-permute-start | bytes 294920 | tf_op jit(solution)/shard_map/ppermute | solution.py:506
  170.3 0.7 copy-start.10
  215.2 0.9 copy-start.11
  218.2 5.3 %collective-permute-start.6 = (bf16[128,384]{1,0:T(8,128)(2,1)S(1)}, bf16[128,384]{1,0:T(8,128)(2,1)S(1)}, u32[]{:S(2)}, u32[]{:S(2)}) collective-permute-start(bf16[128,384]{1,0:T(8,128)(2,1)S(1)} %get-tuple-element.34), channel_id=1, source_target_pairs={{0,1},{1,2},{2,3},{3,0},{4,5},{5,6},{6,7},{7,4},{8,9},{9,10},{10,1... | collective-permute-start | bytes 294920 | tf_op jit(solution)/shard_map/ppermute | solution.py:506
  219.2 6.7 %collective-permute-start.7 = (bf16[128,384]{1,0:T(8,128)(2,1)S(1)}, bf16[128,384]{1,0:T(8,128)(2,1)S(1)}, u32[]{:S(2)}, u32[]{:S(2)}) collective-permute-start(bf16[128,384]{1,0:T(8,128)(2,1)S(1)} %get-tuple-element.35), channel_id=1, source_target_pairs={{0,2},{1,3},{2,0},{3,1},{4,6},{5,7},{6,4},{7,5},{8,10},{9,11},{10,... | collective-permute-start | bytes 294920 | tf_op jit(solution)/shard_map/ppermute | solution.py:506
  221.3 4.8 %collective-permute-start.8 = (bf16[128,384]{1,0:T(8,128)(2,1)S(1)}, bf16[128,384]{1,0:T(8,128)(2,1)S(1)}, u32[]{:S(2)}, u32[]{:S(2)}) collective-permute-start(bf16[128,384]{1,0:T(8,128)(2,1)S(1)} %get-tuple-element.36), channel_id=1, source_target_pairs={{0,3},{1,0},{2,1},{3,2},{4,7},{5,4},{6,5},{7,6},{8,11},{9,8},{10,9... | collective-permute-start | bytes 294920 | tf_op jit(solution)/shard_map/ppermute | solution.py:506
  226.1 20.4 %copy-start.9 = (s32[512]{0:T(512)S(1)}, s32[512]{0:T(512)}, u32[]{:S(2)}) copy-start(s32[512]{0:T(512)} %param.21) | copy-start | bytes 6148
  237.9 4.8 %collective-permute-start.12 = (bf16[128,384]{1,0:T(8,128)(2,1)S(1)}, bf16[128,384]{1,0:T(8,128)(2,1)S(1)}, u32[]{:S(2)}, u32[]{:S(2)}) collective-permute-start(bf16[128,384]{1,0:T(8,128)(2,1)S(1)} %get-tuple-element.43), channel_id=1, source_target_pairs={{0,1},{1,2},{2,3},{3,0},{4,5},{5,6},{6,7},{7,4},{8,9},{9,10},{10,1... | collective-permute-start | bytes 294920 | tf_op jit(solution)/shard_map/ppermute | solution.py:506
  239.9 5.6 %collective-permute-start.13 = (bf16[128,384]{1,0:T(8,128)(2,1)S(1)}, bf16[128,384]{1,0:T(8,128)(2,1)S(1)}, u32[]{:S(2)}, u32[]{:S(2)}) collective-permute-start(bf16[128,384]{1,0:T(8,128)(2,1)S(1)} %get-tuple-element.44), channel_id=1, source_target_pairs={{0,2},{1,3},{2,0},{3,1},{4,6},{5,7},{6,4},{7,5},{8,10},{9,11},{10,... | collective-permute-start | bytes 294920 | tf_op jit(solution)/shard_map/ppermute | solution.py:506
  241.7 4.8 %collective-permute-start.14 = (bf16[128,384]{1,0:T(8,128)(2,1)S(1)}, bf16[128,384]{1,0:T(8,128)(2,1)S(1)}, u32[]{:S(2)}, u32[]{:S(2)}) collective-permute-start(bf16[128,384]{1,0:T(8,128)(2,1)S(1)} %get-tuple-element.45), channel_id=1, source_target_pairs={{0,3},{1,0},{2,1},{3,2},{4,7},{5,4},{6,5},{7,6},{8,11},{9,8},{10,9... | collective-permute-start | bytes 294920 | tf_op jit(solution)/shard_map/ppermute | solution.py:506
  247.8 3.6 %collective-permute-start.15 = (bf16[1024,384]{1,0:T(8,128)(2,1)S(1)}, bf16[1024,384]{1,0:T(8,128)(2,1)S(1)}, u32[]{:S(2)}, u32[]{:S(2)}) collective-permute-start(bf16[1024,384]{1,0:T(8,128)(2,1)S(1)} %get-tuple-element.47), channel_id=1, source_target_pairs={{0,4},{4,0},{1,5},{5,1},{2,6},{6,2},{3,7},{7,3},{8,12},{12,8},{9,1... | collective-permute-start | bytes 2359304 | tf_op jit(solution)/shard_map/ppermute | solution.py:506
  251.5 6.2 %collective-permute-start.18 = (bf16[256,384]{1,0:T(8,128)(2,1)S(1)}, bf16[256,384]{1,0:T(8,128)(2,1)S(1)}, u32[]{:S(2)}, u32[]{:S(2)}) collective-permute-start(bf16[256,384]{1,0:T(8,128)(2,1)S(1)} %get-tuple-element.51), channel_id=1, source_target_pairs={{0,192},{64,0},{128,64},{192,128},{1,193},{65,1},{129,65},{193,129... | collective-permute-start | bytes 589832 | tf_op jit(solution)/shard_map/ppermute | solution.py:506
  253.2 7.3 %collective-permute-start.17 = (bf16[256,384]{1,0:T(8,128)(2,1)S(1)}, bf16[256,384]{1,0:T(8,128)(2,1)S(1)}, u32[]{:S(2)}, u32[]{:S(2)}) collective-permute-start(bf16[256,384]{1,0:T(8,128)(2,1)S(1)} %get-tuple-element.50), channel_id=1, source_target_pairs={{0,128},{64,192},{128,0},{192,64},{1,129},{65,193},{129,1},{193,65... | collective-permute-start | bytes 589832 | tf_op jit(solution)/shard_map/ppermute | solution.py:506
  254.3 11.4 %collective-permute-start.16 = (bf16[256,384]{1,0:T(8,128)(2,1)S(1)}, bf16[256,384]{1,0:T(8,128)(2,1)S(1)}, u32[]{:S(2)}, u32[]{:S(2)}) collective-permute-start(bf16[256,384]{1,0:T(8,128)(2,1)S(1)} %get-tuple-element.49), channel_id=1, source_target_pairs={{0,64},{64,128},{128,192},{192,0},{1,65},{65,129},{129,193},{193,1... | collective-permute-start | bytes 589832 | tf_op jit(solution)/shard_map/ppermute | solution.py:506
  265.7 42.9 %copy-start.1 = (bf16[384,384]{1,0:T(8,128)(2,1)S(1)}, bf16[384,384]{1,0:T(8,128)(2,1)}, u32[]{:S(2)}) copy-start(bf16[384,384]{1,0:T(8,128)(2,1)} %param.15) | copy-start | bytes 884740
  277.6 31.1 %copy-start.12 = (bf16[32,384]{1,0:T(8,128)(2,1)}, bf16[32,384]{1,0:T(8,128)(2,1)S(1)}, u32[]{:S(2)}) copy-start(bf16[32,384]{1,0:T(8,128)(2,1)S(1)} %multiply_convert_fusion) | copy-start | bytes 73732
  300.5 6.0 %collective-permute-start.19 = (bf16[1024,384]{1,0:T(8,128)(2,1)S(1)}, bf16[1024,384]{1,0:T(8,128)(2,1)S(1)}, u32[]{:S(2)}, u32[]{:S(2)}) collective-permute-start(bf16[1024,384]{1,0:T(8,128)(2,1)S(1)} %bitcast.23), channel_id=1, source_target_pairs={{0,4},{4,0},{1,5},{5,1},{2,6},{6,2},{3,7},{7,3},{8,12},{12,8},{9,1... | collective-permute-start | bytes 2359304 | tf_op jit(solution)/shard_map/ppermute | solution.py:506
Sparse Core Ops, SparseCore 0:
  65.8 142.2 all-gather.2

commit v9 on v8

--- a/solution.py
+++ b/solution.py
@@ -312,12 +312,44 @@
 
 WIDE = 2 * COLS
 AHEAD = 6
+HELD = 2
+
+
+def hold_kernel(from_ref, to_ref, sems):
+    def fetch(i):
+        which, block = i // N_MP, i % N_MP
+        return pltpu.make_async_copy(
+            from_ref.at[block, pl.ds(which * D, D), :],
+            to_ref.at[which, :, pl.ds(block * COLS, COLS)],
+            sems.at[i],
+        )
+
+    for i in range(HELD * N_MP):
+        fetch(i).start()
+    for i in range(HELD * N_MP):
+        fetch(i).wait()
+
+
+def hold(gathered):
+    return pl.pallas_call(
+        hold_kernel,
+        in_specs=[pl.BlockSpec(memory_space=pl.ANY)],
+        out_specs=pl.BlockSpec(memory_space=pl.ANY),
+        out_shape=shape_of(HELD, D, D),
+        scratch_shapes=[pltpu.SemaphoreType.DMA((HELD * N_MP,))],
+        compiler_params=pltpu.CompilerParams(vmem_limit_bytes=44 * 1024 * 1024),
+        name="hold",
+        cost_estimate=pl.CostEstimate(
+            flops=0, bytes_accessed=4 * HELD * D * D, transcendentals=0
+        ),
+    )(gathered)
+
 AHEAD = 6
 
 
 def layers_kernel(mp_ref, *refs):
     updates, states, weight_ref = refs[:N_MP], refs[N_MP : 2 * N_MP], refs[2 * N_MP]
-    refs = refs[2 * N_MP + 1 :]
+    held, refs = refs[2 * N_MP + 1], refs[2 * N_MP + 2 :]
     outs, (hidden, given, inner, up, weights, up_sem, sems) = refs[:N_MP], refs[N_MP:]
     me = mp_ref[0]
 
@@ -326,15 +358,15 @@
         rows = pl.multiple_of(lax.rem(which, HALF_MAPS) * D, D)
         return pltpu.make_async_copy(
             weight_ref.at[lax.div(which, HALF_MAPS) * N_MP + block, pl.ds(rows, D), :],
-            weights.at[which, :, pl.ds(pl.multiple_of(block * COLS, 128), COLS)],
-            sems.at[i],
+            weights.at[which - HELD, :, pl.ds(pl.multiple_of(block * COLS, 128), COLS)],
+            sems.at[i - HELD * N_MP],
         )
 
     up_fetch = pltpu.make_async_copy(
         weight_ref.at[:, pl.ds(HALF_MAPS * D, UP_HALF), :], up, up_sem
     )
     up_fetch.start()
-    for i in range(AHEAD):
+    for i in range(HELD * N_MP, HELD * N_MP + AHEAD):
         fetch(i).start()
 
     a, b, c, d = (ref[...].astype(F32) for ref in updates)
@@ -360,9 +392,12 @@
             def _():
                 fetch(i + AHEAD).start()
 
-        return weights[which, :, pl.ds(pl.multiple_of(side * WIDE, 128), WIDE)]
-
-    def layer(index, carry):
+        return weights[which - HELD, :, pl.ds(pl.multiple_of(side * WIDE, 128), WIDE)]
+
+    def ready(which, side):
+        return held[which, :, pl.ds(pl.multiple_of(side * WIDE, 128), WIDE)]
+
+    def layer(index, carry, arrived=arrived):
         def one(side, carry):
             at = pl.ds(pl.multiple_of(side * WIDE, 128), WIDE)
             inner[:, at] = silu(product(given[...], arrived(2 * index, side))).astype(BF16)
@@ -377,17 +412,18 @@
             given[:, at] = fresh.astype(BF16)
         return carry
 
-    lax.fori_loop(0, MAPS // 2, layer, 0)
+    layer(0, 0, ready)
+    lax.fori_loop(HELD // 2, MAPS // 2, layer, 0)
     for k, out_ref in enumerate(outs):
         place = pl.multiple_of(lax.rem(me + k, N_MP) * COLS, 128)
         out_ref[...] = given[:, pl.ds(place, COLS)]
 
 
-def layers(mp, updates, states, gathered):
+def layers(mp, updates, states, gathered, held):
     vmem = pl.BlockSpec(memory_space=pltpu.VMEM)
     return pl.pallas_call(
         layers_kernel,
-        in_specs=[SCALAR] + [vmem] * (2 * N_MP) + [pl.BlockSpec(memory_space=pl.ANY)],
+        in_specs=[SCALAR] + [vmem] * (2 * N_MP) + [pl.BlockSpec(memory_space=pl.ANY), vmem],
         out_specs=[vmem] * N_MP,
         out_shape=[shape_of(ROWS, COLS)] * N_MP,
         scratch_shapes=[
@@ -395,18 +431,18 @@
             pltpu.VMEM((ROWS, D), BF16),
             pltpu.VMEM((ROWS, D), BF16),
             pltpu.VMEM((N_CORE * N_MP, UP_HALF, COLS), BF16),
-            pltpu.VMEM((MAPS, D, D), BF16),
+            pltpu.VMEM((MAPS - HELD, D, D), BF16),
             pltpu.SemaphoreType.DMA,
-            pltpu.SemaphoreType.DMA((MAPS * N_MP,)),
+            pltpu.SemaphoreType.DMA(((MAPS - HELD) * N_MP,)),
         ],
-        compiler_params=pltpu.CompilerParams(vmem_limit_bytes=48 * 1024 * 1024),
+        compiler_params=pltpu.CompilerParams(vmem_limit_bytes=30 * 1024 * 1024),
         name="layers",
         cost_estimate=pl.CostEstimate(
             flops=2 * ROWS * D * D * MAPS,
             bytes_accessed=2 * D * D * MAPS,
             transcendentals=ROWS * D * MAPS,
         ),
-    )(mp, *updates, *states, gathered)
+    )(mp, *updates, *states, gathered, held)
 
 
 def at_block(ref, me, k):
@@ -576,8 +612,9 @@
     second = exchange(sums(second, PARTS[1]))
     blocks = edges(mp, lists, first.reshape(SLOTS, -1), [])
     blocks = edges(mp, lists, second.reshape(SLOTS, -1), blocks)
+    gathered, *blocks = lax.optimization_barrier((gathered, *blocks))
     updates = turned(blocks, "mp")
-    hiddens = turned(layers(mp, updates, states, gathered), "mp")
+    hiddens = turned(layers(mp, updates, states, gathered, hold(gathered)), "mp")
     keep, give = atoms(mp, core, atom_row, hiddens)
     x = jnp.full((1,), lax.axis_index("graph_0"), I32)
     parts = turned(meet(x, keep, turn(give, "graph_2", N_CORE, 1)), "graph_0")

time: 316 us -> 317 us (level)
  starting transfers between devices: 64 us -> 55.9 us
  waiting for transfers between devices: 127 us -> 131 us
  Pallas kernels: 66.3 us -> 69.5 us
    ppermute x20, starting transfers between devices: 32.4 us -> 25.3 us  [turn(): lax.ppermute(array, axis, [(i, (i + shift) % count) for i in range(count)])]
    pallas_call x0 -> x1, Pallas kernels: none -> 3.78 us  [hold(): pl.pallas_call(hold_kernel, in_specs=[pl.BlockSpec(memory_space=pl.ANY)],...]
    ppermute x20, waiting for transfers between devices: 34.7 us -> 38.2 us  [turn(): lax.ppermute(array, axis, [(i, (i + shift) % count) for i in range(count)])]
  transfers between devices with their start and end apart: 25 -> 25, of which waited for: 17 -> 20; matrix products, arithmetic and copies ran while one was open for 2% -> 2% of each run, Pallas kernels for 13% -> 15%
where the time goes in v9:
time: 317 us
  waiting for transfers between devices  131 us (41%)
  Pallas kernels  69.5 us (22%)
  starting transfers between devices  55.9 us (18%)
  blocking collectives  36.6 us (12%)
  between operations  14.4 us (5%)
  local copies, waits for them, and re-layouts  6.52 us (2%)
    all_to_all x1, waiting for transfers between devices, local(): second = exchange(sums(second, PARTS[1]))  45.9 us
    pallas_call x2, Pallas kernels, triplets(): pl.pallas_call(functools.partial(triplet_kernel, groups, (trip_block, slo...  38.8 us
    ppermute x20, waiting for transfers between devices, turn(): lax.ppermute(array, axis, [(i, (i + shift) % count) for i in range(count)])  38.2 us
    all_to_all x1, waiting for transfers between devices, local(): second = exchange(second)  35.3 us
    ppermute x20, starting transfers between devices, turn(): lax.ppermute(array, axis, [(i, (i + shift) % count) for i in range(count)])  25.3 us
    all_to_all x1, blocking collectives, local(): lax.all_to_all(jnp.broadcast_to(table[None], (N_X, N_Z * ATOM_DEV, COLS))...  13.5 us
    all_to_all x1, starting transfers between devices, local(): first = exchange(first)  12.1 us
    all_to_all x1, blocking collectives, local(): atom_sum = summed(lax.all_to_all(part, 'graph_1', 0, 0, tiled=True))  12 us
  transfers between devices with their start and end apart: 25, of which 20 were waited for; matrix products, arithmetic and copies ran while one was open for 2% of the time, Pallas kernels for 15%

profile of v9, /device:TPU:1, one launch (start us, length us, event | category | flops | bytes accessed | tf_op | source)
XLA Modules:
  0.0 316.6 jit_solution(940538812509836961)
XLA Ops:
  7.2 2.3 project.1
  9.5 3.6 %collective-permute-start.2 = (bf16[512,128]{1,0:T(8,128)(2,1)}, bf16[512,128]{1,0:T(8,128)(2,1)S(1)}, u32[]{:S(2)}, u32[]{:S(2)}) collective-permute-start(bf16[512,128]{1,0:T(8,128)(2,1)} %get-tuple-element.32.a_ref), channel_id=1, source_target_pairs={{0,3},{1,0},{2,1},{3,2},{4,7},{5,4},{6,5},{7,6},{8,11},{9,8},{10,9... | collective-permute-start | bytes 393224 | tf_op jit(solution)/shard_map/ppermute | solution.py:542
  13.1 0.3 collective-permute-start.1
  13.4 0.7 collective-permute-start
  14.1 0.8 reshape.63.list_ref
  15.0 2.0 collective-permute-done.2.d_ref
  17.0 1.7 collective-permute-done.1.c_ref
  18.7 4.2 %collective-permute-done.b_ref = bf16[512,128]{1,0:T(8,128)(2,1)S(1)} collective-permute-done((bf16[512,128]{1,0:T(8,128)(2,1)}, bf16[512,128]{1,0:T(8,128)(2,1)S(1)}, u32[]{:S(2)}, u32[]{:S(2)}) %collective-permute-start) | collective-permute-done | bytes 131104 | tf_op jit(solution)/shard_map/ppermute | solution.py:542
  22.9 0.9 copy-done.5
  23.8 3.0 send.2
  26.8 12.1 %all-to-all-start = ((bf16[64,64,128]{2,1,0:T(8,128)(2,1)}), bf16[64,64,128]{2,1,0:T(8,128)(2,1)S(1)}, u32[]{:S(2)}, u32[]{:S(2)}) async-start(bf16[64,64,128]{2,1,0:T(8,128)(2,1)} %bitcast.3), calls=%async_computation | async-start | bytes 2097152 | tf_op jit(solution)/shard_map/all_to_all | solution.py:605
  39.0 2.4 constant_dynamic-slice_fusion.1
  41.4 0.4 collective-permute-start.5
  41.8 0.3 collective-permute-start.4
  42.1 0.8 collective-permute-start.3
  43.0 2.2 pad_maximum_fusion
  45.1 3.8 %collective-permute-done.5.d_ref = bf16[512,256]{1,0:T(8,128)(2,1)S(1)} collective-permute-done((bf16[512,256]{1,0:T(8,128)(2,1)S(1)}, bf16[512,256]{1,0:T(8,128)(2,1)S(1)}, u32[]{:S(2)}, u32[]{:S(2)}) %collective-permute-start.5) | collective-permute-done | bytes 262176 | tf_op jit(solution)/shard_map/ppermute | solution.py:542
  48.9 1.5 collective-permute-done.4.c_ref
  50.4 6.7 %collective-permute-done.3.b_ref = bf16[512,256]{1,0:T(8,128)(2,1)S(1)} collective-permute-done((bf16[512,256]{1,0:T(8,128)(2,1)S(1)}, bf16[512,256]{1,0:T(8,128)(2,1)S(1)}, u32[]{:S(2)}, u32[]{:S(2)}) %collective-permute-start.3) | collective-permute-done | bytes 262176 | tf_op jit(solution)/shard_map/ppermute | solution.py:542
  57.1 3.2 %send.3 = bf16[4096,256]{1,0:T(8,128)(2,1)} custom-call(s32[1,4096]{1,0:T(1,128)S(1)} %reshape.63.list_ref, bf16[512,256]{1,0:T(8,128)(2,1)S(1)} %copy-done.4, bf16[512,256]{1,0:T(8,128)(2,1)S(1)} %collective-permute-done.3.b_ref, bf16[512,256]{1,0:T(8,128)(2,1)S(1)} %collective-permute-done.4.c_ref, bf16[512,256]{1,0:T(8,128)(2,1)S(1)} %collective-permute-done.5.d_ref), custom_call_target="tpu_custom_call" | custom-call | flops 1073741824 | bytes 3072000 | tf_op jit(solution)/shard_map/send/pallas_call | solution.py:140
  60.4 7.1 %all-to-all-done = bf16[64,64,128]{2,1,0:T(8,128)(2,1)S(1)} async-done(((bf16[64,64,128]{2,1,0:T(8,128)(2,1)}), bf16[64,64,128]{2,1,0:T(8,128)(2,1)S(1)}, u32[]{:S(2)}, u32[]{:S(2)}) %all-to-all-start) | async-done | bytes 1048608 | tf_op jit(solution)/shard_map/all_to_all | solution.py:605
  67.5 6.5 %all-to-all-start.1 = ((bf16[64,64,256]{2,1,0:T(8,128)(2,1)}), bf16[64,64,256]{2,1,0:T(8,128)(2,1)}, u32[]{:S(2)}, u32[]{:S(2)}) async-start(bf16[64,64,256]{2,1,0:T(8,128)(2,1)} %bitcast.4), calls=%async_computation.1 | async-start | bytes 4194304 | tf_op jit(solution)/shard_map/all_to_all | solution.py:608
  74.1 15.7 %triplets.3 = bf16[4,1024,128]{2,1,0:T(8,128)(2,1)} custom-call(s32[1,4096]{1,0:T(1,128)S(1)} %bitcast.26, s32[1,4096]{1,0:T(1,128)S(1)} %bitcast.28, s32[1,4096]{1,0:T(1,128)S(1)} %bitcast.30, f32[42,4096]{1,0:T(8,128)S(1)} %copy-done.3, bf16[144,128]{1,0:T(8,128)(2,1)S(1)} %slice.9.weight_ref, bf16[4096,128]{1,0:T(8,128)(2,1)S(1)} %bitcast.21), custom_call_target="tpu_custom_call" | custom-call | flops 8589934592 | bytes 2304000 | tf_op jit(solution)/shard_map/triplets/pallas_call | solution.py:230
  89.9 35.3 %all-to-all-done.1 = bf16[64,64,256]{2,1,0:T(8,128)(2,1)} async-done(((bf16[64,64,256]{2,1,0:T(8,128)(2,1)}), bf16[64,64,256]{2,1,0:T(8,128)(2,1)}, u32[]{:S(2)}, u32[]{:S(2)}) %all-to-all-start.1) | async-done | bytes 2097184 | tf_op jit(solution)/shard_map/all_to_all | solution.py:608
  125.2 5.8 %all-to-all-start.3 = ((bf16[64,64,128]{2,1,0:T(8,128)(2,1)}), bf16[64,64,128]{2,1,0:T(8,128)(2,1)S(1)}, u32[]{:S(2)}, u32[]{:S(2)}) async-start(bf16[64,64,128]{2,1,0:T(8,128)(2,1)} %bitcast.14), calls=%async_computation.3 | async-start | bytes 2097152 | tf_op jit(solution)/shard_map/all_to_all | solution.py:611
  131.0 0.6 slice.8.weight_ref
  131.7 23.0 %triplets.2 = bf16[2,2048,256]{2,1,0:T(8,128)(2,1)} custom-call(s32[1,4096]{1,0:T(1,128)} %bitcast.25, s32[1,4096]{1,0:T(1,128)} %bitcast.27, s32[1,4096]{1,0:T(1,128)} %bitcast.29, f32[42,4096]{1,0:T(8,128)} %basis_ref.3, bf16[144,256]{1,0:T(8,128)(2,1)} %slice.8.weight_ref, bf16[4096,256]{1,0:T(8,128)(2,1)} %bitcast.10.table_ref), custom_call_target="tpu_custom_call" | custom-call | flops 17179869184 | bytes 4608000 | tf_op jit(solution)/shard_map/triplets/pallas_call | solution.py:230
  154.7 4.9 %all-to-all-done.3 = bf16[64,64,128]{2,1,0:T(8,128)(2,1)S(1)} async-done(((bf16[64,64,128]{2,1,0:T(8,128)(2,1)}), bf16[64,64,128]{2,1,0:T(8,128)(2,1)S(1)}, u32[]{:S(2)}, u32[]{:S(2)}) %all-to-all-start.3) | async-done | bytes 1048608 | tf_op jit(solution)/shard_map/all_to_all | solution.py:611
  159.6 6.2 %all-to-all-start.2 = ((bf16[64,64,256]{2,1,0:T(8,128)(2,1)}), bf16[64,64,256]{2,1,0:T(8,128)(2,1)S(1)}, u32[]{:S(2)}, u32[]{:S(2)}) async-start(bf16[64,64,256]{2,1,0:T(8,128)(2,1)} %bitcast.35), calls=%async_computation.2 | async-start | bytes 4194304 | tf_op jit(solution)/shard_map/all_to_all | solution.py:612
  165.9 1.5 collective-permute-start.10
  167.3 1.2 collective-permute-start.11
  168.5 1.9 edges.2.refs_0_
  170.4 0.6 copy-done.10
  171.1 45.9 %all-to-all-done.2 = bf16[64,64,256]{2,1,0:T(8,128)(2,1)S(1)} async-done(((bf16[64,64,256]{2,1,0:T(8,128)(2,1)}), bf16[64,64,256]{2,1,0:T(8,128)(2,1)S(1)}, u32[]{:S(2)}, u32[]{:S(2)}) %all-to-all-start.2) | async-done | bytes 2097184 | tf_op jit(solution)/shard_map/all_to_all | solution.py:612
  217.0 0.9 copy-done.11
  217.9 2.0 edges.3
  220.1 1.5 collective-permute-start.7
  221.5 1.2 collective-permute-start.8
  222.7 3.8 %hold.1.refs_9_ = bf16[2,1536,1536]{2,1,0:T(8,128)(2,1)S(1)} custom-call(bf16[8,4800,384]{2,1,0:T(8,128)(2,1)} %bitcast.33), custom_call_target="tpu_custom_call" | custom-call | bytes 18874368 | tf_op jit(solution)/shard_map/hold/pallas_call | solution.py:334
  226.5 1.0 collective-permute-done.6.refs_1_
  227.6 0.1 collective-permute-done.8.refs_3_
  227.7 10.9 %layers.1 = (bf16[128,384]{1,0:T(8,128)(2,1)S(1)}, bf16[128,384]{1,0:T(8,128)(2,1)S(1)}, bf16[128,384]{1,0:T(8,128)(2,1)S(1)}, bf16[128,384]{1,0:T(8,128)(2,1)S(1)}) custom-call(s32[1]{0:T(128)} %bitcast.mp_ref, bf16[128,384]{1,0:T(8,128)(2,1)S(1)} %get-tuple-element.43.refs_0_, bf16[128,384]{1,0:T(8,128)(2,1)S(1)} %collective-permute-done.6.refs_1_, ...), custom_call_target="tpu_custom_call" | custom-call | flops 3623878656 | bytes 28311552 | tf_op jit(solution)/shard_map/layers/pallas_call | solution.py:424
  238.6 0.5 collective-permute-start.12
  239.1 3.5 %collective-permute-start.13 = (bf16[128,384]{1,0:T(8,128)(2,1)S(1)}, bf16[128,384]{1,0:T(8,128)(2,1)S(1)}, u32[]{:S(2)}, u32[]{:S(2)}) collective-permute-start(bf16[128,384]{1,0:T(8,128)(2,1)S(1)} %get-tuple-element.54), channel_id=1, source_target_pairs={{0,2},{1,3},{2,0},{3,1},{4,6},{5,7},{6,4},{7,5},{8,10},{9,11},{10,... | collective-permute-start | bytes 294920 | tf_op jit(solution)/shard_map/ppermute | solution.py:542
  242.7 0.8 collective-permute-done.12.h1
  243.5 3.0 collective-permute-done.13.h2
  246.5 0.9 collective-permute-done.14.h3
  247.4 1.3 atoms.1
  248.6 1.6 collective-permute-start.15
  250.3 1.9 collective-permute-done.15.got_ref
  252.2 0.2 meet.1
  252.4 0.7 collective-permute-start.16
  253.1 1.9 collective-permute-start.17
  255.0 0.8 collective-permute-start.18
  255.7 4.2 %collective-permute-done.16 = bf16[256,384]{1,0:T(8,128)(2,1)S(1)} collective-permute-done((bf16[256,384]{1,0:T(8,128)(2,1)S(1)}, bf16[256,384]{1,0:T(8,128)(2,1)S(1)}, u32[]{:S(2)}, u32[]{:S(2)}) %collective-permute-start.16) | collective-permute-done | bytes 196640 | tf_op jit(solution)/shard_map/ppermute | solution.py:542
  259.9 4.0 %collective-permute-done.17 = bf16[256,384]{1,0:T(8,128)(2,1)S(1)} collective-permute-done((bf16[256,384]{1,0:T(8,128)(2,1)S(1)}, bf16[256,384]{1,0:T(8,128)(2,1)S(1)}, u32[]{:S(2)}, u32[]{:S(2)}) %collective-permute-start.17) | collective-permute-done | bytes 196640 | tf_op jit(solution)/shard_map/ppermute | solution.py:542
  263.9 0.4 collective-permute-done.18
  264.3 0.1 add_convert_fusion
  264.4 12.0 %all_to_all.35 = bf16[8,32,384]{2,1,0:T(8,128)(2,1)S(1)} all-to-all(bf16[8,32,384]{2,1,0:T(8,128)(2,1)S(1)} %bitcast.37), channel_id=1, replica_groups=mesh['graph_0'=4,'graph_1'=8,'graph_2'=2,'mp'=4] {'graph_1'}, dimensions={0} | all-to-all | bytes 393216 | tf_op jit(solution)/shard_map/all_to_all | solution.py:625
  276.5 11.0 %all_to_all.36 = bf16[8,32,384]{2,1,0:T(8,128)(2,1)S(1)} all-to-all(bf16[8,32,384]{2,1,0:T(8,128)(2,1)S(1)} %broadcast_in_dim.25), channel_id=1, replica_groups=mesh['graph_0'=4,'graph_1'=8,'graph_2'=2,'mp'=4] {'graph_1'}, dimensions={0} | all-to-all | bytes 393216 | tf_op jit(solution)/shard_map/all_to_all | solution.py:627
  287.6 13.5 %all_to_all.37 = bf16[4,256,384]{2,1,0:T(8,128)(2,1)S(1)} all-to-all(bf16[4,256,384]{2,1,0:T(8,128)(2,1)S(1)} %broadcast_in_dim.27), channel_id=1, replica_groups=mesh['graph_0'=4,'graph_1'=8,'graph_2'=2,'mp'=4] {'graph_0'}, dimensions={0} | all-to-all | bytes 1572864 | tf_op jit(solution)/shard_map/all_to_all | solution.py:630
  301.1 4.6 %collective-permute-start.19 = (bf16[1024,384]{1,0:T(8,128)(2,1)S(1)}, bf16[1024,384]{1,0:T(8,128)(2,1)S(1)}, u32[]{:S(2)}, u32[]{:S(2)}) collective-permute-start(bf16[1024,384]{1,0:T(8,128)(2,1)S(1)} %bitcast.23), channel_id=1, source_target_pairs={{0,4},{4,0},{1,5},{5,1},{2,6},{6,2},{3,7},{7,3},{8,12},{12,8},{9,1... | collective-permute-start | bytes 2359304 | tf_op jit(solution)/shard_map/ppermute | solution.py:542
  305.7 1.9 collective-permute-done.19.other_ref
  307.7 2.1 final.1
  (46 shorter events, 0.5 us)
Async XLA Ops:
  7.2 31.8 %copy-start = (bf16[384,384]{1,0:T(8,128)(2,1)S(1)}, bf16[384,384]{1,0:T(8,128)(2,1)}, u32[]{:S(2)}) copy-start(bf16[384,384]{1,0:T(8,128)(2,1)} %param.15) | copy-start | bytes 884740
  9.5 7.5 %collective-permute-start.2 = (bf16[512,128]{1,0:T(8,128)(2,1)}, bf16[512,128]{1,0:T(8,128)(2,1)S(1)}, u32[]{:S(2)}, u32[]{:S(2)}) collective-permute-start(bf16[512,128]{1,0:T(8,128)(2,1)} %get-tuple-element.32.a_ref), channel_id=1, source_target_pairs={{0,3},{1,0},{2,1},{3,2},{4,7},{5,4},{6,5},{7,6},{8,11},{9,8},{10,9... | collective-permute-start | bytes 393224 | tf_op jit(solution)/shard_map/ppermute | solution.py:542
  13.1 5.6 %collective-permute-start.1 = (bf16[512,128]{1,0:T(8,128)(2,1)}, bf16[512,128]{1,0:T(8,128)(2,1)S(1)}, u32[]{:S(2)}, u32[]{:S(2)}) collective-permute-start(bf16[512,128]{1,0:T(8,128)(2,1)} %get-tuple-element.32.a_ref), channel_id=1, source_target_pairs={{0,2},{1,3},{2,0},{3,1},{4,6},{5,7},{6,4},{7,5},{8,10},{9,11},{10,... | collective-permute-start | bytes 393224 | tf_op jit(solution)/shard_map/ppermute | solution.py:542
  13.4 9.5 %collective-permute-start = (bf16[512,128]{1,0:T(8,128)(2,1)}, bf16[512,128]{1,0:T(8,128)(2,1)S(1)}, u32[]{:S(2)}, u32[]{:S(2)}) collective-permute-start(bf16[512,128]{1,0:T(8,128)(2,1)} %get-tuple-element.32.a_ref), channel_id=1, source_target_pairs={{0,1},{1,2},{2,3},{3,0},{4,5},{5,6},{6,7},{7,4},{8,9},{9,10},{10,1... | collective-permute-start | bytes 393224 | tf_op jit(solution)/shard_map/ppermute | solution.py:542
  22.9 0.9 copy-start.5
  26.8 40.6 %all-to-all-start = ((bf16[64,64,128]{2,1,0:T(8,128)(2,1)}), bf16[64,64,128]{2,1,0:T(8,128)(2,1)S(1)}, u32[]{:S(2)}, u32[]{:S(2)}) async-start(bf16[64,64,128]{2,1,0:T(8,128)(2,1)} %bitcast.3), calls=%async_computation | async-start | bytes 2097152 | tf_op jit(solution)/shard_map/all_to_all | solution.py:605
  38.9 181.1 %all-gather.3.cloned.1.call-start = ((), (), s32[]{:S(2)}) async-start(), calls=%async_computation.7 | async-start | bytes 33177600 | tf_op jit(solution)/shard_map/all_gather | solution.py:609
  38.9 2.4 copy-start.4
  41.4 7.5 %collective-permute-start.5 = (bf16[512,256]{1,0:T(8,128)(2,1)S(1)}, bf16[512,256]{1,0:T(8,128)(2,1)S(1)}, u32[]{:S(2)}, u32[]{:S(2)}) collective-permute-start(bf16[512,256]{1,0:T(8,128)(2,1)S(1)} %copy-done.4), channel_id=1, source_target_pairs={{0,3},{1,0},{2,1},{3,2},{4,7},{5,4},{6,5},{7,6},{8,11},{9,8},{10,9... | collective-permute-start | bytes 786440 | tf_op jit(solution)/shard_map/ppermute | solution.py:542
  41.8 8.7 %collective-permute-start.4 = (bf16[512,256]{1,0:T(8,128)(2,1)S(1)}, bf16[512,256]{1,0:T(8,128)(2,1)S(1)}, u32[]{:S(2)}, u32[]{:S(2)}) collective-permute-start(bf16[512,256]{1,0:T(8,128)(2,1)S(1)} %copy-done.4), channel_id=1, source_target_pairs={{0,2},{1,3},{2,0},{3,1},{4,6},{5,7},{6,4},{7,5},{8,10},{9,11},{10,... | collective-permute-start | bytes 786440 | tf_op jit(solution)/shard_map/ppermute | solution.py:542
  42.1 15.0 %collective-permute-start.3 = (bf16[512,256]{1,0:T(8,128)(2,1)S(1)}, bf16[512,256]{1,0:T(8,128)(2,1)S(1)}, u32[]{:S(2)}, u32[]{:S(2)}) collective-permute-start(bf16[512,256]{1,0:T(8,128)(2,1)S(1)} %copy-done.4), channel_id=1, source_target_pairs={{0,1},{1,2},{2,3},{3,0},{4,5},{5,6},{6,7},{7,4},{8,9},{9,10},{10,1... | collective-permute-start | bytes 786440 | tf_op jit(solution)/shard_map/ppermute | solution.py:542
  67.4 6.6 %copy-start.13 = (f32[42,384]{1,0:T(8,128)S(1)}, f32[42,384]{1,0:T(8,128)}, u32[]{:S(2)}) copy-start(f32[42,384]{1,0:T(8,128)} %param.14) | copy-start | bytes 193540
  67.4 6.7 %copy-start.3 = (f32[42,4096]{1,0:T(8,128)S(1)}, f32[42,4096]{1,0:T(8,128)}, u32[]{:S(2)}) copy-start(f32[42,4096]{1,0:T(8,128)} %basis_ref.3) | copy-start | bytes 2064388
  67.4 6.7 %copy-start.6 = (s32[4096]{0:T(1024)S(1)}, s32[4096]{0:T(1024)}, u32[]{:S(2)}) copy-start(s32[4096]{0:T(1024)} %param.18) | copy-start | bytes 49156
  67.4 6.7 %copy-start.7 = (s32[4096]{0:T(1024)S(1)}, s32[4096]{0:T(1024)}, u32[]{:S(2)}) copy-start(s32[4096]{0:T(1024)} %param.20) | copy-start | bytes 49156
  67.5 6.7 %copy-start.8 = (s32[4096]{0:T(1024)S(1)}, s32[4096]{0:T(1024)}, u32[]{:S(2)}) copy-start(s32[4096]{0:T(1024)} %param.19) | copy-start | bytes 49156
  67.5 57.7 %all-to-all-start.1 = ((bf16[64,64,256]{2,1,0:T(8,128)(2,1)}), bf16[64,64,256]{2,1,0:T(8,128)(2,1)}, u32[]{:S(2)}, u32[]{:S(2)}) async-start(bf16[64,64,256]{2,1,0:T(8,128)(2,1)} %bitcast.4), calls=%async_computation.1 | async-start | bytes 4194304 | tf_op jit(solution)/shard_map/all_to_all | solution.py:608
  125.2 34.4 %all-to-all-start.3 = ((bf16[64,64,128]{2,1,0:T(8,128)(2,1)}), bf16[64,64,128]{2,1,0:T(8,128)(2,1)S(1)}, u32[]{:S(2)}, u32[]{:S(2)}) async-start(bf16[64,64,128]{2,1,0:T(8,128)(2,1)} %bitcast.14), calls=%async_computation.3 | async-start | bytes 2097152 | tf_op jit(solution)/shard_map/all_to_all | solution.py:611
  154.7 12.6 %copy-start.14 = (bf16[128,384]{1,0:T(8,128)(2,1)S(1)}, bf16[128,384]{1,0:T(8,128)(2,1)}, u32[]{:S(2)}) copy-start(bf16[128,384]{1,0:T(8,128)(2,1)} %get-tuple-element.50) | copy-start | bytes 294916
  159.6 57.4 %all-to-all-start.2 = ((bf16[64,64,256]{2,1,0:T(8,128)(2,1)}), bf16[64,64,256]{2,1,0:T(8,128)(2,1)S(1)}, u32[]{:S(2)}, u32[]{:S(2)}) async-start(bf16[64,64,256]{2,1,0:T(8,128)(2,1)} %bitcast.35), calls=%async_computation.2 | async-start | bytes 4194304 | tf_op jit(solution)/shard_map/all_to_all | solution.py:612
  165.8 55.8 %collective-permute-start.9 = (bf16[128,384]{1,0:T(8,128)(2,1)}, bf16[128,384]{1,0:T(8,128)(2,1)S(1)}, u32[]{:S(2)}, u32[]{:S(2)}) collective-permute-start(bf16[128,384]{1,0:T(8,128)(2,1)} %get-tuple-element.48), channel_id=1, source_target_pairs={{0,1},{1,2},{2,3},{3,0},{4,5},{5,6},{6,7},{7,4},{8,9},{9,10},{10,1... | collective-permute-start | bytes 294920 | tf_op jit(solution)/shard_map/ppermute | solution.py:542
  165.9 60.7 %collective-permute-start.10 = (bf16[128,384]{1,0:T(8,128)(2,1)}, bf16[128,384]{1,0:T(8,128)(2,1)S(1)}, u32[]{:S(2)}, u32[]{:S(2)}) collective-permute-start(bf16[128,384]{1,0:T(8,128)(2,1)} %get-tuple-element.49), channel_id=1, source_target_pairs={{0,2},{1,3},{2,0},{3,1},{4,6},{5,7},{6,4},{7,5},{8,10},{9,11},{10,... | collective-permute-start | bytes 294920 | tf_op jit(solution)/shard_map/ppermute | solution.py:542
  167.3 59.2 %collective-permute-start.11 = (bf16[128,384]{1,0:T(8,128)(2,1)S(1)}, bf16[128,384]{1,0:T(8,128)(2,1)S(1)}, u32[]{:S(2)}, u32[]{:S(2)}) collective-permute-start(bf16[128,384]{1,0:T(8,128)(2,1)S(1)} %copy-done.14), channel_id=1, source_target_pairs={{0,3},{1,0},{2,1},{3,2},{4,7},{5,4},{6,5},{7,6},{8,11},{9,8},{10,9... | collective-permute-start | bytes 294920 | tf_op jit(solution)/shard_map/ppermute | solution.py:542
  170.4 0.7 copy-start.10
  217.0 0.9 copy-start.11
  220.0 7.7 %copy-start.2 = (bf16[128,384]{1,0:T(8,128)(2,1)S(1)}, bf16[128,384]{1,0:T(8,128)(2,1)}, u32[]{:S(2)}) copy-start(bf16[128,384]{1,0:T(8,128)(2,1)} %get-tuple-element.47.refs_4_) | copy-start | bytes 294916
  220.0 7.6 %collective-permute-start.6 = (bf16[128,384]{1,0:T(8,128)(2,1)S(1)}, bf16[128,384]{1,0:T(8,128)(2,1)S(1)}, u32[]{:S(2)}, u32[]{:S(2)}) collective-permute-start(bf16[128,384]{1,0:T(8,128)(2,1)S(1)} %get-tuple-element.44), channel_id=1, source_target_pairs={{0,1},{1,2},{2,3},{3,0},{4,5},{5,6},{6,7},{7,4},{8,9},{9,10},{10,1... | collective-permute-start | bytes 294920 | tf_op jit(solution)/shard_map/ppermute | solution.py:542
  220.1 7.5 %collective-permute-start.7 = (bf16[128,384]{1,0:T(8,128)(2,1)S(1)}, bf16[128,384]{1,0:T(8,128)(2,1)S(1)}, u32[]{:S(2)}, u32[]{:S(2)}) collective-permute-start(bf16[128,384]{1,0:T(8,128)(2,1)S(1)} %get-tuple-element.45), channel_id=1, source_target_pairs={{0,2},{1,3},{2,0},{3,1},{4,6},{5,7},{6,4},{7,5},{8,10},{9,11},{10,... | collective-permute-start | bytes 294920 | tf_op jit(solution)/shard_map/ppermute | solution.py:542
  221.5 6.2 %collective-permute-start.8 = (bf16[128,384]{1,0:T(8,128)(2,1)S(1)}, bf16[128,384]{1,0:T(8,128)(2,1)S(1)}, u32[]{:S(2)}, u32[]{:S(2)}) collective-permute-start(bf16[128,384]{1,0:T(8,128)(2,1)S(1)} %get-tuple-element.46), channel_id=1, source_target_pairs={{0,3},{1,0},{2,1},{3,2},{4,7},{5,4},{6,5},{7,6},{8,11},{9,8},{10,9... | collective-permute-start | bytes 294920 | tf_op jit(solution)/shard_map/ppermute | solution.py:542
  227.7 19.7 %copy-start.9 = (s32[512]{0:T(512)S(1)}, s32[512]{0:T(512)}, u32[]{:S(2)}) copy-start(s32[512]{0:T(512)} %param.21) | copy-start | bytes 6148
  238.6 4.8 %collective-permute-start.12 = (bf16[128,384]{1,0:T(8,128)(2,1)S(1)}, bf16[128,384]{1,0:T(8,128)(2,1)S(1)}, u32[]{:S(2)}, u32[]{:S(2)}) collective-permute-start(bf16[128,384]{1,0:T(8,128)(2,1)S(1)} %get-tuple-element.53), channel_id=1, source_target_pairs={{0,1},{1,2},{2,3},{3,0},{4,5},{5,6},{6,7},{7,4},{8,9},{9,10},{10,1... | collective-permute-start | bytes 294920 | tf_op jit(solution)/shard_map/ppermute | solution.py:542
  239.1 7.4 %collective-permute-start.13 = (bf16[128,384]{1,0:T(8,128)(2,1)S(1)}, bf16[128,384]{1,0:T(8,128)(2,1)S(1)}, u32[]{:S(2)}, u32[]{:S(2)}) collective-permute-start(bf16[128,384]{1,0:T(8,128)(2,1)S(1)} %get-tuple-element.54), channel_id=1, source_target_pairs={{0,2},{1,3},{2,0},{3,1},{4,6},{5,7},{6,4},{7,5},{8,10},{9,11},{10,... | collective-permute-start | bytes 294920 | tf_op jit(solution)/shard_map/ppermute | solution.py:542
  242.6 4.7 %collective-permute-start.14 = (bf16[128,384]{1,0:T(8,128)(2,1)S(1)}, bf16[128,384]{1,0:T(8,128)(2,1)S(1)}, u32[]{:S(2)}, u32[]{:S(2)}) collective-permute-start(bf16[128,384]{1,0:T(8,128)(2,1)S(1)} %get-tuple-element.55), channel_id=1, source_target_pairs={{0,3},{1,0},{2,1},{3,2},{4,7},{5,4},{6,5},{7,6},{8,11},{9,8},{10,9... | collective-permute-start | bytes 294920 | tf_op jit(solution)/shard_map/ppermute | solution.py:542
  248.6 3.6 %collective-permute-start.15 = (bf16[1024,384]{1,0:T(8,128)(2,1)S(1)}, bf16[1024,384]{1,0:T(8,128)(2,1)S(1)}, u32[]{:S(2)}, u32[]{:S(2)}) collective-permute-start(bf16[1024,384]{1,0:T(8,128)(2,1)S(1)} %get-tuple-element.57), channel_id=1, source_target_pairs={{0,4},{4,0},{1,5},{5,1},{2,6},{6,2},{3,7},{7,3},{8,12},{12,8},{9,1... | collective-permute-start | bytes 2359304 | tf_op jit(solution)/shard_map/ppermute | solution.py:542
  252.4 7.6 %collective-permute-start.16 = (bf16[256,384]{1,0:T(8,128)(2,1)S(1)}, bf16[256,384]{1,0:T(8,128)(2,1)S(1)}, u32[]{:S(2)}, u32[]{:S(2)}) collective-permute-start(bf16[256,384]{1,0:T(8,128)(2,1)S(1)} %get-tuple-element.59), channel_id=1, source_target_pairs={{0,64},{64,128},{128,192},{192,0},{1,65},{65,129},{129,193},{193,1... | collective-permute-start | bytes 589832 | tf_op jit(solution)/shard_map/ppermute | solution.py:542
  253.1 10.8 %collective-permute-start.17 = (bf16[256,384]{1,0:T(8,128)(2,1)S(1)}, bf16[256,384]{1,0:T(8,128)(2,1)S(1)}, u32[]{:S(2)}, u32[]{:S(2)}) collective-permute-start(bf16[256,384]{1,0:T(8,128)(2,1)S(1)} %get-tuple-element.60), channel_id=1, source_target_pairs={{0,128},{64,192},{128,0},{192,64},{1,129},{65,193},{129,1},{193,65... | collective-permute-start | bytes 589832 | tf_op jit(solution)/shard_map/ppermute | solution.py:542
  255.0 9.3 %collective-permute-start.18 = (bf16[256,384]{1,0:T(8,128)(2,1)S(1)}, bf16[256,384]{1,0:T(8,128)(2,1)S(1)}, u32[]{:S(2)}, u32[]{:S(2)}) collective-permute-start(bf16[256,384]{1,0:T(8,128)(2,1)S(1)} %get-tuple-element.61), channel_id=1, source_target_pairs={{0,192},{64,0},{128,64},{192,128},{1,193},{65,1},{129,65},{193,129... | collective-permute-start | bytes 589832 | tf_op jit(solution)/shard_map/ppermute | solution.py:542
  264.3 45.5 %copy-start.1 = (bf16[384,384]{1,0:T(8,128)(2,1)S(1)}, bf16[384,384]{1,0:T(8,128)(2,1)}, u32[]{:S(2)}) copy-start(bf16[384,384]{1,0:T(8,128)(2,1)} %param.15) | copy-start | bytes 884740
  276.5 33.3 %copy-start.12 = (bf16[32,384]{1,0:T(8,128)(2,1)}, bf16[32,384]{1,0:T(8,128)(2,1)S(1)}, u32[]{:S(2)}) copy-start(bf16[32,384]{1,0:T(8,128)(2,1)S(1)} %multiply_convert_fusion) | copy-start | bytes 73732
  301.1 6.5 %collective-permute-start.19 = (bf16[1024,384]{1,0:T(8,128)(2,1)S(1)}, bf16[1024,384]{1,0:T(8,128)(2,1)S(1)}, u32[]{:S(2)}, u32[]{:S(2)}) collective-permute-start(bf16[1024,384]{1,0:T(8,128)(2,1)S(1)} %bitcast.23), channel_id=1, source_target_pairs={{0,4},{4,0},{1,5},{5,1},{2,6},{6,2},{3,7},{7,3},{8,12},{12,8},{9,1... | collective-permute-start | bytes 2359304 | tf_op jit(solution)/shard_map/ppermute | solution.py:542
Sparse Core Ops, SparseCore 0:
  67.6 140.2 all-gather.2
